TPU v7x, 128 devices: a whole 4x4x4 slice. The times are simulated.
128 devices in a mesh: dp: 16 (over x, y), ctx: 8 (over z, core).
Axes of the slice: x: 4, y: 4, z: 4, core: 2. Of those that a mesh axis runs over, the one named last changes fastest.
Arguments:
- hidden_acts: bfloat16 [131072, 1536], P(('dp', 'ctx')), may hold values from -6 to 6
- out_grad: bfloat16 [131072, 5120], P(('dp', 'ctx')), may hold values from -96 to 96
- old_logp: float32 [16, 8192], P('dp', 'ctx'), may hold values from -4 to -0.3
- new_logp: float32 [16, 8192], P('dp', 'ctx'), may hold values from -4.3 to 0
- roll_len: int32 [16], P('dp'), may hold values from 2048 to 8192, as said below
- resp_mask: int32 [16, 8192], P('dp', 'ctx'), may hold values 0 or 1
- advantage: float32 [16, 1], P('dp'), may hold values from -4 to 4
Outputs:
- bucket_grad: float32 [1536, 5120], P('dp', 'ctx')
Inputs may be any that keep to these rules, and one draw needn't show every extreme that they name: `roll_len`: some rollout fills all 8192 positions.
All inputs are finite; a program needn't handle non-finite values. No bound on the sum of `resp_mask` on one device may be relied on, other than what follows from the above.
Results may differ from a plain program's by a relative error of at most 0.0028.
Values sent between devices are 32-bit elements; how exact they have to be, the bound alone decides.
A program may use at most 192 MiB of HBM per device.

v0:
```python
import jax
import jax.numpy as jnp
from jax import lax
from jax.sharding import PartitionSpec as P

CLIP_LOW = 0.0003
CLIP_HIGH = 0.0004


def shards(hidden_acts, out_grad, old_logp, new_logp, roll_len, resp_mask, advantage):
    width = old_logp.shape[1]
    places = lax.axis_index("ctx") * width + jnp.arange(width, dtype=jnp.int32)
    masked = jnp.where(places < roll_len[0], resp_mask[0], 0).astype(jnp.float32)
    gap_sum, count = lax.psum(
        (jnp.sum((new_logp[0] - old_logp[0]) * masked), jnp.sum(masked)), "ctx"
    )
    adv = advantage[0, 0]
    length = jnp.maximum(count, 1.0)
    seq_ratio = jnp.exp(gap_sum / length)
    active = jnp.where(adv >= 0.0, seq_ratio < 1.0 + CLIP_HIGH, seq_ratio > 1.0 - CLIP_LOW).astype(
        jnp.float32
    )
    seq_weight = -adv * seq_ratio * active / length
    token_coef = masked * seq_weight
    scaled = (token_coef[:, None] * out_grad).astype(jnp.bfloat16)
    unit_share = lax.psum_scatter(
        lax.dot_general(
            hidden_acts, scaled, (((0,), (0,)), ((), ())), preferred_element_type=jnp.float32
        ),
        "dp",
        scatter_dimension=0,
        tiled=True,
    )
    return lax.psum_scatter(unit_share, "ctx", scatter_dimension=1, tiled=True)


def solution(mesh):
    placed = (
        P(("dp", "ctx"), None),
        P(("dp", "ctx"), None),
        P("dp", "ctx"),
        P("dp", "ctx"),
        P("dp"),
        P("dp", "ctx"),
        P("dp", None),
    )
    return jax.shard_map(
        shards, mesh=mesh, in_specs=placed, out_specs=P("dp", "ctx"), check_vma=False
    )
```

profile of v0, /device:TPU:0, one launch (start us, length us, event | category | flops | bytes accessed | tf_op | source)
XLA Modules:
  0.0 315.6 jit_solution(13741832230433318615)
XLA Ops:
  6.5 0.0 copy-start
  6.5 0.0 reduce-scatter.7.cloned.1.call-start
  8.1 0.7 sub.6
  8.9 1.4 convert_reduce_fusion
  10.2 16.6 %all-reduce = (f32[]{:T(128)}, f32[]{:T(128)}) all-reduce(f32[]{:T(128)} %get-tuple-element.6, f32[]{:T(128)} %get-tuple-element.5), channel_id=1, replica_groups=mesh['dp'=16,'ctx'=8] {'ctx'}, use_global_device_ids=true, to_apply=%region_1.2 | all-reduce | flops 2 | bytes 16 | tf_op jit(solution)/shard_map/psum | solution.py:14
  28.2 0.7 convert_multiply_fusion
  28.9 0.0 copy-done
  28.9 24.9 %convolution_bitcast_fusion = f32[1536,5120]{0,1:T(8,128)} fusion(bf16[1024,1536]{1,0:T(8,128)(2,1)S(1)} %copy-done, bf16[1024,5120]{1,0:T(8,128)(2,1)} %param.8, f32[1024]{0:T(1024)S(1)} %convert_multiply_fusion), kind=kOutput, calls=%fused_computation | convolution fusion | flops 16121856000 | bytes 45092864 | tf_op jit(solution)/shard_map/dot_general | solution.py:27
  53.8 30.8 %copy.10 = f32[1536,5120]{1,0:T(8,128)} copy(f32[1536,5120]{0,1:T(8,128)} %convolution_bitcast_fusion) | data formatting | bytes 62914560
  84.6 0.0 reduce-scatter.7.cloned.1.call-update
  84.6 0.0 copy-start.1
  84.6 0.0 reduce-scatter.5.cloned.1.call-start
  84.7 184.3 %reduce-scatter.7.cloned.1.call-done = f32[96,5120]{1,0:T(8,128)} async-done(((f32[1536,5120]{1,0:T(8,128)}), f32[96,5120]{1,0:T(8,128)}) %reduce-scatter.7.cloned.1.call-update) | async-done | bytes 1966096
  269.0 3.1 copy.11
  272.1 0.0 reduce-scatter.5.cloned.1.call-update
  272.1 34.8 %reduce-scatter.5.cloned.1.call-done = f32[96,640]{0,1:T(8,128)} async-done(((f32[96,5120]{0,1:T(8,128)}), f32[96,640]{0,1:T(8,128)}) %reduce-scatter.5.cloned.1.call-update) | async-done | bytes 245776 | tf_op jit(solution)/shard_map/reduce_scatter | solution.py:34
  306.9 1.8 copy.9
  308.7 0.0 copy-done.1
Async XLA Ops:
  6.5 22.3 %copy-start = (bf16[1024,1536]{1,0:T(8,128)(2,1)S(1)}, bf16[1024,1536]{1,0:T(8,128)(2,1)}, u32[]{:S(2)}) copy-start(bf16[1024,1536]{1,0:T(8,128)(2,1)} %param.7) | copy-start | bytes 9437188
  6.5 262.4 %reduce-scatter.7.cloned.1.call-start = ((), (), s32[]{:S(2)}) async-start(), calls=%async_computation.3 | async-start | bytes 33423360
  84.6 224.1 %copy-start.1 = (bf16[1024,1536]{1,0:T(8,128)(2,1)S(1)}, bf16[1024,1536]{1,0:T(8,128)(2,1)}, u32[]{:S(2)}) copy-start(bf16[1024,1536]{1,0:T(8,128)(2,1)} %param.7) | copy-start | bytes 9437188
  84.6 222.3 %reduce-scatter.5.cloned.1.call-start = ((), (), s32[]{:S(2)}) async-start(), calls=%async_computation.2 | async-start | bytes 2949120 | tf_op jit(solution)/shard_map/reduce_scatter | solution.py:34
Sparse Core Ops, SparseCore 0:
  84.7 184.1 reduce-scatter.6
  272.2 34.6 reduce-scatter.4
where the time goes:
time: 316 us
  waiting for transfers between devices  219 us (69%)
  local copies, waits for them, and re-layouts  35.7 us (11%)
  matrix products  24.9 us (8%)
  blocking collectives  16.6 us (5%)
  between operations  16.4 us (5%)
    unnamed x3, waiting for transfers between devices  184 us
    reduce_scatter x1, waiting for transfers between devices, shards(): return lax.psum_scatter(unit_share, 'ctx', scatter_dimension=1, tiled=True)  34.8 us
    unnamed x6, local copies, waits for them, and re-layouts  33.9 us
    dot_general x1, matrix products, shards(): lax.dot_general(hidden_acts, scaled, (((0,), (0,)), ((), ())), preferred_...  24.9 us
    psum x1, blocking collectives, shards(): lax.psum((jnp.sum((new_logp[0] - old_logp[0]) * masked), jnp.sum(masked))...  16.6 us
  transfers between devices with their start and end apart: 2, of which 2 were waited for; matrix products, arithmetic and copies ran while one was open for 0% of the time, Pallas kernels for 0%

commit v1 on v0

v1 whole, which is shorter than its diff:
```python
import jax
import jax.numpy as jnp
from jax import lax
from jax.sharding import PartitionSpec as P

CLIP_LOW = 0.0003
CLIP_HIGH = 0.0004


def shards(hidden_acts, out_grad, old_logp, new_logp, roll_len, resp_mask, advantage, n_dp, n_ctx):
    width = old_logp.shape[1]
    places = lax.axis_index("ctx") * width + jnp.arange(width, dtype=jnp.int32)
    masked = jnp.where(places < roll_len[0], resp_mask[0], 0).astype(jnp.float32)
    gap_sum, count = lax.psum(
        (jnp.sum((new_logp[0] - old_logp[0]) * masked), jnp.sum(masked)), "ctx"
    )
    adv = advantage[0, 0]
    length = jnp.maximum(count, 1.0)
    seq_ratio = jnp.exp(gap_sum / length)
    active = jnp.where(adv >= 0.0, seq_ratio < 1.0 + CLIP_HIGH, seq_ratio > 1.0 - CLIP_LOW).astype(
        jnp.float32
    )
    seq_weight = -adv * seq_ratio * active / length
    token_coef = masked * seq_weight
    scaled = (token_coef[:, None] * out_grad).astype(jnp.bfloat16)
    t, hb = hidden_acts.shape
    d = out_grad.shape[1]
    h3 = hidden_acts.reshape(t, n_dp, hb // n_dp)
    s3 = scaled.reshape(t, n_ctx, d // n_ctx)
    part = jnp.einsum("tar,tbc->barc", h3, s3, preferred_element_type=jnp.float32)
    part = part.reshape(n_dp * n_ctx, hb // n_dp, d // n_ctx)
    out = lax.psum_scatter(part, ("ctx", "dp"), scatter_dimension=0, tiled=True)
    return out[0]


def solution(mesh):
    placed = (
        P(("dp", "ctx"), None),
        P(("dp", "ctx"), None),
        P("dp", "ctx"),
        P("dp", "ctx"),
        P("dp"),
        P("dp", "ctx"),
        P("dp", None),
    )
    n_dp, n_ctx = mesh.shape["dp"], mesh.shape["ctx"]

    def f(*a):
        return shards(*a, n_dp, n_ctx)

    return jax.shard_map(
        f, mesh=mesh, in_specs=placed, out_specs=P("dp", "ctx"), check_vma=False
    )
```

time: 316 us -> 347 us (1.098)
  waiting for transfers between devices: 219 us -> 263 us
  local copies, waits for them, and re-layouts: 35.7 us -> 13.6 us
  other arithmetic: 2.77 us -> 13.4 us
    reduce_scatter x1, waiting for transfers between devices: 34.8 us -> 263 us  [shards(): out = lax.psum_scatter(part, ('ctx', 'dp'), scatter_dimension=0, tiled=True)]
    unnamed x3 -> x1, waiting for transfers between devices: 184 us -> 0.02 us
    unnamed x6 -> x2, local copies, waits for them, and re-layouts: 33.9 us -> 13.6 us
    convert_element_type x0 -> x1, other arithmetic: none -> 10.7 us  [shards(): scaled = (token_coef[:, None] * out_grad).astype(jnp.bfloat16)]
  transfers between devices with their start and end apart: 2 -> 1, of which waited for: 2 -> 1; matrix products, arithmetic and copies ran while one was open for 0% -> 0% of each run, Pallas kernels for 0% -> 0%
where the time goes in v1:
time: 347 us
  waiting for transfers between devices  263 us (76%)
  matrix products  24.1 us (7%)
  blocking collectives  16.6 us (5%)
  between operations  16 us (5%)
  local copies, waits for them, and re-layouts  13.6 us (4%)
  other arithmetic  13.4 us (4%)
    reduce_scatter x1, waiting for transfers between devices, shards(): out = lax.psum_scatter(part, ('ctx', 'dp'), scatter_dimension=0, tiled=True)  263 us
    dot_general x1, matrix products, shards(): jnp.einsum('tar,tbc->barc', h3, s3, preferred_element_type=jnp.float32)  24.1 us
    psum x1, blocking collectives, shards(): lax.psum((jnp.sum((new_logp[0] - old_logp[0]) * masked), jnp.sum(masked))...  16.6 us
    unnamed x2, local copies, waits for them, and re-layouts  13.6 us
    convert_element_type x1, other arithmetic, shards(): scaled = (token_coef[:, None] * out_grad).astype(jnp.bfloat16)  10.7 us
  transfers between devices with their start and end apart: 1, of which 1 were waited for; matrix products, arithmetic and copies ran while one was open for 0% of the time, Pallas kernels for 0%

profile of v1, /device:TPU:0, one launch (start us, length us, event | category | flops | bytes accessed | tf_op | source)
XLA Modules:
  0.0 346.6 jit_solution(16012254615246104974)
XLA Ops:
  6.5 0.0 reduce-scatter.2.cloned.1.call-start
  7.8 0.7 sub.6
  8.5 1.4 convert_reduce_fusion
  9.9 16.6 %all-reduce = (f32[]{:T(128)}, f32[]{:T(128)}) all-reduce(f32[]{:T(128)} %get-tuple-element.6, f32[]{:T(128)} %get-tuple-element.5), channel_id=1, replica_groups=mesh['dp'=16,'ctx'=8] {'ctx'}, use_global_device_ids=true, to_apply=%region_1.2 | all-reduce | flops 2 | bytes 16 | tf_op jit(solution)/shard_map/psum | solution.py:14
  27.9 3.2 copy.10
  31.0 0.7 convert_multiply_fusion
  31.7 10.7 %multiply_convert_fusion = bf16[1024,5120]{1,0:T(8,128)(2,1)} fusion(bf16[1024,5120]{1,0:T(8,128)(2,1)} %param.8, f32[1024]{0:T(1024)S(1)} %convert_multiply_fusion), kind=kLoop, calls=%fused_computation | loop fusion | flops 15728640 | bytes 20975616 | tf_op jit(solution)/shard_map/convert_element_type | solution.py:25
  42.4 10.4 %copy.15 = bf16[128,8,8,640]{3,2,1,0:T(8,128)(2,1)} copy(bf16[128,8,8,640]{3,1,2,0:T(8,128)(2,1)} %bitcast.19) | data formatting | bytes 20971520
  52.8 24.1 %fusion = f32[8,640,16,96]{1,3,2,0:T(8,128)} fusion(bf16[1024,16,96,1]{0,2,1,3:T(8,128)(2,1)S(1)} %bitcast.22, bf16[1024,8,640,1]{2,1,0,3:T(8,128)(2,1)} %bitcast.21), kind=kOutput, calls=%fused_computation.1 | convolution fusion | flops 16106127360 | bytes 45088768 | tf_op jit(solution)/shard_map/tar,tbc->barc/dot_general | solution.py:30
  77.0 0.0 reduce-scatter.2.cloned.1.call-update
  77.0 262.8 %reduce-scatter.2.cloned.1.call-done = f32[1,96,640]{2,1,0:T(8,128)} async-done(((f32[128,96,640]{2,1,0:T(8,128)}), f32[1,96,640]{2,1,0:T(8,128)}) %reduce-scatter.2.cloned.1.call-update) | async-done | bytes 245776 | tf_op jit(solution)/shard_map/reduce_scatter | solution.py:32
Async XLA Ops:
  6.5 333.2 %reduce-scatter.2.cloned.1.call-start = ((), (), s32[]{:S(2)}) async-start(), calls=%async_computation.1 | async-start | bytes 31703040 | tf_op jit(solution)/shard_map/reduce_scatter | solution.py:32
Sparse Core Ops, SparseCore 0:
  77.1 262.6 reduce-scatter.1

commit v2 on v0

v2 whole, which is shorter than its diff:
```python
import jax
import jax.numpy as jnp
import numpy as np
from jax import lax
from jax.experimental import pallas as pl
from jax.experimental.pallas import tpu as pltpu
from jax.sharding import Mesh
from jax.sharding import PartitionSpec as P

CLIP_LOW = 0.0003
CLIP_HIGH = 0.0004
ROW_TILE = 384


def half_matmul(sel, coef, grad, hid_t, n_dp, n_z, width):
    hb, t = hid_t.shape
    rows = hb // n_dp
    per_tile = ROW_TILE // rows
    n_tiles = hb // ROW_TILE

    def kernel(sel_ref, coef_ref, grad_ref, hid_ref, out_ref, scaled_ref):
        @pl.when(pl.program_id(1) == 0)
        def _():
            scaled_ref[...] = (coef_ref[...] * grad_ref[...].astype(jnp.float32)).astype(jnp.bfloat16)

        acc = jnp.dot(hid_ref[...], scaled_ref[...], preferred_element_type=jnp.float32)
        for k in range(per_tile):
            out_ref[k, 0] = acc[k * rows:(k + 1) * rows, :]

    grid_spec = pltpu.PrefetchScalarGridSpec(
        num_scalar_prefetch=1,
        grid=(n_z, n_tiles),
        in_specs=[
            pl.BlockSpec((t, 1), lambda z, i, s: (0, 0)),
            pl.BlockSpec((t, width), lambda z, i, s: (0, z * 2 + s[0])),
            pl.BlockSpec((ROW_TILE, t), lambda z, i, s: (i, 0)),
        ],
        out_specs=pl.BlockSpec((per_tile, 1, rows, width), lambda z, i, s: (i, z, 0, 0)),
        scratch_shapes=[pltpu.VMEM((t, width), jnp.bfloat16)],
    )
    flops = 2 * hb * t * width * n_z
    return pl.pallas_call(
        kernel,
        grid_spec=grid_spec,
        out_shape=jax.ShapeDtypeStruct((n_dp, n_z, rows, width), jnp.float32),
        compiler_params=pltpu.CompilerParams(vmem_limit_bytes=48 * 1024 * 1024),
        cost_estimate=pl.CostEstimate(
            flops=flops, transcendentals=0,
            bytes_accessed=hb * t * 2 + t * width * n_z * 2 + hb * width * n_z * 4,
        ),
    )(sel, coef, grad, hid_t)


def shards(hidden_acts, out_grad, old_logp, new_logp, roll_len, resp_mask, advantage):
    n_dp = lax.axis_size("dp")
    n_z = lax.axis_size("z")
    n_core = lax.axis_size("core")
    width = old_logp.shape[1]
    ctx = lax.axis_index("z") * n_core + lax.axis_index("core")
    places = ctx * width + jnp.arange(width, dtype=jnp.int32)
    masked = jnp.where(places < roll_len[0], resp_mask[0], 0).astype(jnp.float32)
    gap_sum, count = lax.psum(
        (jnp.sum((new_logp[0] - old_logp[0]) * masked), jnp.sum(masked)), ("z", "core")
    )
    adv = advantage[0, 0]
    length = jnp.maximum(count, 1.0)
    seq_ratio = jnp.exp(gap_sum / length)
    active = jnp.where(adv >= 0.0, seq_ratio < 1.0 + CLIP_HIGH, seq_ratio > 1.0 - CLIP_LOW).astype(
        jnp.float32
    )
    seq_weight = -adv * seq_ratio * active / length
    token_coef = (masked * seq_weight)[:, None]
    d = out_grad.shape[1]
    col = d // (n_z * n_core)
    hid_t = hidden_acts.T
    core = lax.axis_index("core")
    other = jnp.reshape(1 - core, (1,)).astype(jnp.int32)
    mine = jnp.reshape(core, (1,)).astype(jnp.int32)
    theirs = half_matmul(other, token_coef, out_grad, hid_t, n_dp, n_z, col)
    got = lax.ppermute(theirs, "core", perm=[(0, 1), (1, 0)])
    own = half_matmul(mine, token_coef, out_grad, hid_t, n_dp, n_z, col)
    chip = own + got
    rows = lax.psum_scatter(chip, "dp", scatter_dimension=0, tiled=True)[0]
    return lax.psum_scatter(rows, "z", scatter_dimension=0, tiled=True)[0]


def solution(mesh):
    n_dp, n_ctx = mesh.shape["dp"], mesh.shape["ctx"]
    fine = Mesh(np.asarray(mesh.devices).reshape(n_dp, n_ctx // 2, 2), ("dp", "z", "core"))
    tok = ("dp", "z", "core")
    placed = (
        P(tok, None),
        P(tok, None),
        P("dp", ("z", "core")),
        P("dp", ("z", "core")),
        P("dp"),
        P("dp", ("z", "core")),
        P("dp", None),
    )
    return jax.shard_map(
        shards, mesh=fine, in_specs=placed, out_specs=P("dp", ("z", "core")), check_vma=False
    )
```

time: 316 us -> 232 us (0.73)
  waiting for transfers between devices: 219 us -> 134 us
  Pallas kernels: 0 us -> 38.8 us
  local copies, waits for them, and re-layouts: 35.7 us -> 4.88 us
  matrix products: 24.9 us -> 0 us
  other arithmetic: 2.77 us -> 20.1 us
    unnamed x3, waiting for transfers between devices: 184 us -> 105 us
    pallas_call x0 -> x2, Pallas kernels: none -> 38.8 us  [half_matmul(): pl.pallas_call(kernel, grid_spec=grid_spec, out_shape=jax.ShapeDtypeStruc...]
    unnamed x6 -> x1, local copies, waits for them, and re-layouts: 33.9 us -> 3.18 us
    dot_general x1 -> x0, matrix products: 24.9 us -> none  [shards(): lax.dot_general(hidden_acts, scaled, (((0,), (0,)), ((), ())), preferred_...]
    add x0 -> x1, other arithmetic: none -> 16.9 us  [shards(): chip = own + got]
    reduce_scatter x1, waiting for transfers between devices: 34.8 us -> 25.3 us  [shards(): return lax.psum_scatter(rows, 'z', scatter_dimension=0, tiled=True)[0]]
    ppermute x0 -> x1, waiting for transfers between devices: none -> 4.65 us  [shards(): got = lax.ppermute(theirs, 'core', perm=[(0, 1), (1, 0)])]
  transfers between devices with their start and end apart: 2 -> 3, of which waited for: 2 -> 3; matrix products, arithmetic and copies ran while one was open for 0% -> 0% of each run, Pallas kernels for 0% -> 8%
where the time goes in v2:
time: 232 us; the launch traced here: 231 us
  waiting for transfers between devices  134 us (58%)
  Pallas kernels  38.8 us (17%)
  other arithmetic  20.1 us (9%)
  blocking collectives  16.7 us (7%)
  between operations  16.1 us (7%)
  local copies, waits for them, and re-layouts  4.88 us (2%)
    unnamed x3, waiting for transfers between devices  105 us
    pallas_call x2, Pallas kernels, half_matmul(): pl.pallas_call(kernel, grid_spec=grid_spec, out_shape=jax.ShapeDtypeStruc...  38.8 us
    reduce_scatter x1, waiting for transfers between devices, shards(): return lax.psum_scatter(rows, 'z', scatter_dimension=0, tiled=True)[0]  25.3 us
    add x1, other arithmetic, shards(): chip = own + got  16.9 us
    psum x1, blocking collectives, shards(): lax.psum((jnp.sum((new_logp[0] - old_logp[0]) * masked), jnp.sum(masked))...  16.7 us
    ppermute x1, waiting for transfers between devices, shards(): got = lax.ppermute(theirs, 'core', perm=[(0, 1), (1, 0)])  4.65 us
  transfers between devices with their start and end apart: 3, of which 3 were waited for; matrix products, arithmetic and copies ran while one was open for 0% of the time, Pallas kernels for 8%

profile of v2, /device:TPU:0, one launch (start us, length us, event | category | flops | bytes accessed | tf_op | source)
XLA Modules:
  0.0 231.0 jit_solution(1534176422274839076)
XLA Ops:
  6.5 0.0 reduce-scatter.7.cloned.1.call-start
  7.2 0.7 sub.9
  7.9 1.4 convert_reduce_fusion
  9.3 16.7 %all-reduce.1 = (f32[]{:T(128)}, f32[]{:T(128)}) all-reduce(f32[]{:T(128)} %get-tuple-element.6, f32[]{:T(128)} %get-tuple-element.5), channel_id=1, replica_groups=mesh['dp'=16,'z'=4,'core'=2] {'z','core'}, use_global_device_ids=true, to_apply=%region_1.2 | all-reduce | flops 2 | bytes 16 | tf_op jit(solution)/shard_map/psum | solution.py:62
  27.9 1.7 copy.11
  29.6 3.2 %copy.12 = bf16[1024,1536]{0,1:T(8,128)(2,1)S(1)} copy(bf16[1024,1536]{1,0:T(8,128)(2,1)} %param.7) | data formatting | bytes 6291456 | tf_op args[0]
  32.8 1.2 convert_multiply_fusion.coef_ref
  34.0 19.4 %shard_map.74 = f32[16,4,96,640]{3,2,1,0:T(8,128)} custom-call(s32[1]{0:T(128)} %bitcast.8.sel_ref, f32[1024,1]{1,0:T(8,128)S(1)} %convert_multiply_fusion.coef_ref, bf16[1024,5120]{1,0:T(8,128)(2,1)} %grad_ref.3, bf16[1536,1024]{1,0:T(8,128)(2,1)S(1)} %bitcast.14), custom_call_target="tpu_custom_call" | custom-call | flops 8053063680 | bytes 24117248 | tf_op jit(solution)/shard_map/pallas_call | solution.py:42
  53.4 0.0 collective-permute-start
  53.4 19.3 %shard_map.73 = f32[16,4,96,640]{3,2,1,0:T(8,128)} custom-call(s32[1]{0:T(128)} %bitcast.sel_ref, f32[1024,1]{1,0:T(8,128)S(1)} %convert_multiply_fusion.coef_ref, bf16[1024,5120]{1,0:T(8,128)(2,1)} %grad_ref.3, bf16[1536,1024]{1,0:T(8,128)(2,1)S(1)} %bitcast.15), custom_call_target="tpu_custom_call" | custom-call | flops 8053063680 | bytes 24117248 | tf_op jit(solution)/shard_map/pallas_call | solution.py:42
  72.8 4.7 %collective-permute-done = f32[16,4,96,640]{3,2,1,0:T(8,128)} collective-permute-done((f32[16,4,96,640]{3,2,1,0:T(8,128)}, f32[16,4,96,640]{3,2,1,0:T(8,128)}, u32[]{:S(2)}, u32[]{:S(2)}) %collective-permute-start) | collective-permute-done | bytes 15728672 | tf_op jit(solution)/shard_map/ppermute | solution.py:80
  77.4 16.9 %add.36 = f32[16,4,96,640]{3,2,1,0:T(8,128)} add(f32[16,4,96,640]{3,2,1,0:T(8,128)} %shard_map.73, f32[16,4,96,640]{3,2,1,0:T(8,128)} %collective-permute-done) | non-fusion elementwise | flops 3932160 | bytes 47185920 | tf_op jit(solution)/shard_map/add | solution.py:82
  94.3 0.0 reduce-scatter.7.cloned.1.call-update
  94.3 0.0 reduce-scatter.5.cloned.1.call-start
  94.3 104.5 %reduce-scatter.7.cloned.1.call-done = f32[1,4,96,640]{3,2,1,0:T(8,128)} async-done(((f32[16,4,96,640]{3,2,1,0:T(8,128)}), f32[1,4,96,640]{3,2,1,0:T(8,128)}) %reduce-scatter.7.cloned.1.call-update) | async-done | bytes 983056
  198.8 0.0 reduce-scatter.5.cloned.1.call-update
  198.8 25.3 %reduce-scatter.5.cloned.1.call-done = f32[1,96,640]{2,1,0:T(8,128)} async-done(((f32[4,96,640]{2,1,0:T(8,128)}), f32[1,96,640]{2,1,0:T(8,128)}) %reduce-scatter.5.cloned.1.call-update) | async-done | bytes 245776 | tf_op jit(solution)/shard_map/reduce_scatter | solution.py:84
Async XLA Ops:
  6.5 192.3 %reduce-scatter.7.cloned.1.call-start = ((), (), s32[]{:S(2)}) async-start(), calls=%async_computation.3 | async-start | bytes 16711680
  53.4 24.0 %collective-permute-start = (f32[16,4,96,640]{3,2,1,0:T(8,128)}, f32[16,4,96,640]{3,2,1,0:T(8,128)}, u32[]{:S(2)}, u32[]{:S(2)}) collective-permute-start(f32[16,4,96,640]{3,2,1,0:T(8,128)} %shard_map.74), channel_id=1, source_target_pairs={{0,1},{1,0},{2,3},{3,2},{4,5},{5,4},{6,7},{7,6},{8,9},{9,8},{10,11... | collective-permute-start | bytes 47185928 | tf_op jit(solution)/shard_map/ppermute | solution.py:80
  94.3 129.8 %reduce-scatter.5.cloned.1.call-start = ((), (), s32[]{:S(2)}) async-start(), calls=%async_computation.2 | async-start | bytes 1228800 | tf_op jit(solution)/shard_map/reduce_scatter | solution.py:84
Sparse Core Ops, SparseCore 0:
  94.4 104.3 reduce-scatter.6
  201.4 22.6 reduce-scatter.4

commit v3 on v2

--- a/solution.py
+++ b/solution.py
@@ -9,7 +9,7 @@
 
 CLIP_LOW = 0.0003
 CLIP_HIGH = 0.0004
-ROW_TILE = 384
+ROW_TILE = 1536
 
 
 def half_matmul(sel, coef, grad, hid_t, n_dp, n_z, width):
@@ -80,8 +80,8 @@
     got = lax.ppermute(theirs, "core", perm=[(0, 1), (1, 0)])
     own = half_matmul(mine, token_coef, out_grad, hid_t, n_dp, n_z, col)
     chip = own + got
-    rows = lax.psum_scatter(chip, "dp", scatter_dimension=0, tiled=True)[0]
-    return lax.psum_scatter(rows, "z", scatter_dimension=0, tiled=True)[0]
+    flat = chip.reshape((n_dp * n_z,) + chip.shape[2:])
+    return lax.psum_scatter(flat, ("dp", "z"), scatter_dimension=0, tiled=True)[0]
 
 
 def solution(mesh):

time: 232 us -> 331 us (1.43)
  waiting for transfers between devices: 134 us -> 243 us
  Pallas kernels: 38.8 us -> 29.1 us
    reduce_scatter x1, waiting for transfers between devices: 25.3 us -> 234 us  [shards(): lax.psum_scatter(flat, ('dp', 'z'), scatter_dimension=0, tiled=True)[0]]
    unnamed x3 -> x1, waiting for transfers between devices: 105 us -> 0.02 us
    pallas_call x2, Pallas kernels: 38.8 us -> 29.1 us  [half_matmul(): pl.pallas_call(kernel, grid_spec=grid_spec, out_shape=jax.ShapeDtypeStruc...]
    ppermute x1, waiting for transfers between devices: 4.65 us -> 9.43 us  [shards(): got = lax.ppermute(theirs, 'core', perm=[(0, 1), (1, 0)])]
  transfers between devices with their start and end apart: 3 -> 2, of which waited for: 3 -> 2; matrix products, arithmetic and copies ran while one was open for 0% -> 0% of each run, Pallas kernels for 8% -> 4%
where the time goes in v3:
time: 331 us; the launch traced here: 330 us
  waiting for transfers between devices  243 us (73%)
  Pallas kernels  29.1 us (9%)
  other arithmetic  20.1 us (6%)
  blocking collectives  16.7 us (5%)
  between operations  16.1 us (5%)
  local copies, waits for them, and re-layouts  4.88 us (1%)
    reduce_scatter x1, waiting for transfers between devices, shards(): lax.psum_scatter(flat, ('dp', 'z'), scatter_dimension=0, tiled=True)[0]  234 us
    pallas_call x2, Pallas kernels, half_matmul(): pl.pallas_call(kernel, grid_spec=grid_spec, out_shape=jax.ShapeDtypeStruc...  29.1 us
    add x1, other arithmetic, shards(): chip = own + got  16.9 us
    psum x1, blocking collectives, shards(): lax.psum((jnp.sum((new_logp[0] - old_logp[0]) * masked), jnp.sum(masked))...  16.7 us
    ppermute x1, waiting for transfers between devices, shards(): got = lax.ppermute(theirs, 'core', perm=[(0, 1), (1, 0)])  9.43 us
  transfers between devices with their start and end apart: 2, of which 2 were waited for; matrix products, arithmetic and copies ran while one was open for 0% of the time, Pallas kernels for 4%

profile of v3, /device:TPU:0, one launch (start us, length us, event | category | flops | bytes accessed | tf_op | source)
XLA Modules:
  0.0 330.1 jit_solution(4179687856857474310)
XLA Ops:
  6.5 0.0 reduce-scatter.2.cloned.1.call-start
  7.2 0.7 sub.9
  7.9 1.4 convert_reduce_fusion
  9.3 16.7 %all-reduce = (f32[]{:T(128)}, f32[]{:T(128)}) all-reduce(f32[]{:T(128)} %get-tuple-element.6, f32[]{:T(128)} %get-tuple-element.5), channel_id=1, replica_groups=mesh['dp'=16,'z'=4,'core'=2] {'z','core'}, use_global_device_ids=true, to_apply=%region_1.2 | all-reduce | flops 2 | bytes 16 | tf_op jit(solution)/shard_map/psum | solution.py:62
  27.9 1.7 copy.9
  29.6 3.2 copy.10
  32.8 1.2 convert_multiply_fusion.coef_ref
  34.0 14.5 %shard_map.74 = f32[16,4,96,640]{3,2,1,0:T(8,128)} custom-call(s32[1]{0:T(128)} %bitcast.8.sel_ref, f32[1024,1]{1,0:T(8,128)S(1)} %convert_multiply_fusion.coef_ref, bf16[1024,5120]{1,0:T(8,128)(2,1)} %grad_ref.3, bf16[1536,1024]{1,0:T(8,128)(2,1)S(1)} %bitcast.13), custom_call_target="tpu_custom_call" | custom-call | flops 8053063680 | bytes 24117248 | tf_op jit(solution)/shard_map/pallas_call | solution.py:42
  48.5 0.0 collective-permute-start
  48.5 14.6 %shard_map.73 = f32[16,4,96,640]{3,2,1,0:T(8,128)} custom-call(s32[1]{0:T(128)} %bitcast.sel_ref, f32[1024,1]{1,0:T(8,128)S(1)} %convert_multiply_fusion.coef_ref, bf16[1024,5120]{1,0:T(8,128)(2,1)} %grad_ref.3, bf16[1536,1024]{1,0:T(8,128)(2,1)S(1)} %bitcast.14), custom_call_target="tpu_custom_call" | custom-call | flops 8053063680 | bytes 24117248 | tf_op jit(solution)/shard_map/pallas_call | solution.py:42
  63.1 9.4 %collective-permute-done = f32[16,4,96,640]{3,2,1,0:T(8,128)} collective-permute-done((f32[16,4,96,640]{3,2,1,0:T(8,128)}, f32[16,4,96,640]{3,2,1,0:T(8,128)}, u32[]{:S(2)}, u32[]{:S(2)}) %collective-permute-start) | collective-permute-done | bytes 15728672 | tf_op jit(solution)/shard_map/ppermute | solution.py:80
  72.5 16.9 %add.34 = f32[16,4,96,640]{3,2,1,0:T(8,128)} add(f32[16,4,96,640]{3,2,1,0:T(8,128)} %shard_map.73, f32[16,4,96,640]{3,2,1,0:T(8,128)} %collective-permute-done) | non-fusion elementwise | flops 3932160 | bytes 47185920 | tf_op jit(solution)/shard_map/add | solution.py:82
  89.4 0.0 reduce-scatter.2.cloned.1.call-update
  89.4 233.9 %reduce-scatter.2.cloned.1.call-done = f32[1,96,640]{2,1,0:T(8,128)} async-done(((f32[64,96,640]{2,1,0:T(8,128)}), f32[1,96,640]{2,1,0:T(8,128)}) %reduce-scatter.2.cloned.1.call-update) | async-done | bytes 245776 | tf_op jit(solution)/shard_map/reduce_scatter | solution.py:84
Async XLA Ops:
  6.5 316.8 %reduce-scatter.2.cloned.1.call-start = ((), (), s32[]{:S(2)}) async-start(), calls=%async_computation.1 | async-start | bytes 15974400 | tf_op jit(solution)/shard_map/reduce_scatter | solution.py:84
  48.5 24.0 %collective-permute-start = (f32[16,4,96,640]{3,2,1,0:T(8,128)}, f32[16,4,96,640]{3,2,1,0:T(8,128)}, u32[]{:S(2)}, u32[]{:S(2)}) collective-permute-start(f32[16,4,96,640]{3,2,1,0:T(8,128)} %shard_map.74), channel_id=1, source_target_pairs={{0,1},{1,0},{2,3},{3,2},{4,5},{5,4},{6,7},{7,6},{8,9},{9,8},{10,11... | collective-permute-start | bytes 47185928 | tf_op jit(solution)/shard_map/ppermute | solution.py:80
Sparse Core Ops, SparseCore 0:
  89.5 233.7 reduce-scatter.1

commit v4 on v2

--- a/solution.py
+++ b/solution.py
@@ -12,43 +12,73 @@
 ROW_TILE = 384
 
 
-def half_matmul(sel, coef, grad, hid_t, n_dp, n_z, width):
+def block_matmul(col, coef, grad, hid_t, n_dp, width, addend=None, into=None, slot=0, n_slots=1):
     hb, t = hid_t.shape
     rows = hb // n_dp
     per_tile = ROW_TILE // rows
     n_tiles = hb // ROW_TILE
+    grouped = n_slots > 1
 
-    def kernel(sel_ref, coef_ref, grad_ref, hid_ref, out_ref, scaled_ref):
-        @pl.when(pl.program_id(1) == 0)
+    def kernel(col_ref, coef_ref, grad_ref, hid_ref, *rest):
+        rest = list(rest)
+        add_ref = rest.pop(0) if addend is not None else None
+        if into is not None:
+            rest.pop(0)
+        out_ref, scaled_ref = rest
+
+        @pl.when(pl.program_id(0) == 0)
         def _():
             scaled_ref[...] = (coef_ref[...] * grad_ref[...].astype(jnp.float32)).astype(jnp.bfloat16)
 
         acc = jnp.dot(hid_ref[...], scaled_ref[...], preferred_element_type=jnp.float32)
         for k in range(per_tile):
-            out_ref[k, 0] = acc[k * rows:(k + 1) * rows, :]
+            part = acc[k * rows:(k + 1) * rows, :]
+            if add_ref is not None:
+                part = part + add_ref[k]
+            if grouped:
+                out_ref[k, 0] = part
+            else:
+                out_ref[k] = part
 
+    in_specs = [
+        pl.BlockSpec((t, 1), lambda i, c: (0, 0)),
+        pl.BlockSpec((t, width), lambda i, c: (0, c[0])),
+        pl.BlockSpec((ROW_TILE, t), lambda i, c: (i, 0)),
+    ]
+    args = [col, coef, grad, hid_t]
+    if addend is not None:
+        in_specs.append(pl.BlockSpec((per_tile, rows, width), lambda i, c: (i, 0, 0)))
+        args.append(addend)
+    aliases = {}
+    if into is not None:
+        in_specs.append(pl.BlockSpec(memory_space=pl.ANY))
+        aliases = {len(args): 0}
+        args.append(into)
+    if grouped:
+        out_shape = jax.ShapeDtypeStruct((n_dp, n_slots, rows, width), jnp.float32)
+        out_spec = pl.BlockSpec((per_tile, 1, rows, width), lambda i, c: (i, slot, 0, 0))
+    else:
+        out_shape = jax.ShapeDtypeStruct((n_dp, rows, width), jnp.float32)
+        out_spec = pl.BlockSpec((per_tile, rows, width), lambda i, c: (i, 0, 0))
     grid_spec = pltpu.PrefetchScalarGridSpec(
         num_scalar_prefetch=1,
-        grid=(n_z, n_tiles),
-        in_specs=[
-            pl.BlockSpec((t, 1), lambda z, i, s: (0, 0)),
-            pl.BlockSpec((t, width), lambda z, i, s: (0, z * 2 + s[0])),
-            pl.BlockSpec((ROW_TILE, t), lambda z, i, s: (i, 0)),
-        ],
-        out_specs=pl.BlockSpec((per_tile, 1, rows, width), lambda z, i, s: (i, z, 0, 0)),
+        grid=(n_tiles,),
+        in_specs=in_specs,
+        out_specs=out_spec,
         scratch_shapes=[pltpu.VMEM((t, width), jnp.bfloat16)],
     )
-    flops = 2 * hb * t * width * n_z
+    extra = hb * width * 4 if addend is not None else 0
     return pl.pallas_call(
         kernel,
         grid_spec=grid_spec,
-        out_shape=jax.ShapeDtypeStruct((n_dp, n_z, rows, width), jnp.float32),
+        out_shape=out_shape,
+        input_output_aliases=aliases,
         compiler_params=pltpu.CompilerParams(vmem_limit_bytes=48 * 1024 * 1024),
         cost_estimate=pl.CostEstimate(
-            flops=flops, transcendentals=0,
-            bytes_accessed=hb * t * 2 + t * width * n_z * 2 + hb * width * n_z * 4,
+            flops=2 * hb * t * width, transcendentals=0,
+            bytes_accessed=hb * t * 2 + t * width * 2 + hb * width * 4 + extra,
         ),
-    )(sel, coef, grad, hid_t)
+    )(*args)
 
 
 def shards(hidden_acts, out_grad, old_logp, new_logp, roll_len, resp_mask, advantage):
@@ -73,13 +103,19 @@
     d = out_grad.shape[1]
     col = d // (n_z * n_core)
     hid_t = hidden_acts.T
-    core = lax.axis_index("core")
-    other = jnp.reshape(1 - core, (1,)).astype(jnp.int32)
-    mine = jnp.reshape(core, (1,)).astype(jnp.int32)
-    theirs = half_matmul(other, token_coef, out_grad, hid_t, n_dp, n_z, col)
-    got = lax.ppermute(theirs, "core", perm=[(0, 1), (1, 0)])
-    own = half_matmul(mine, token_coef, out_grad, hid_t, n_dp, n_z, col)
-    chip = own + got
+    core = lax.axis_index("core").astype(jnp.int32)
+
+    def col_index(k, which):
+        return jnp.reshape(k * n_core + which, (1,)).astype(jnp.int32)
+
+    got = []
+    for k in range(n_z):
+        theirs = block_matmul(col_index(k, 1 - core), token_coef, out_grad, hid_t, n_dp, col)
+        got.append(lax.ppermute(theirs, "core", perm=[(0, 1), (1, 0)]))
+    chip = None
+    for k in range(n_z):
+        chip = block_matmul(col_index(k, core), token_coef, out_grad, hid_t, n_dp, col,
+                            addend=got[k], into=chip, slot=k, n_slots=n_z)
     rows = lax.psum_scatter(chip, "dp", scatter_dimension=0, tiled=True)[0]
     return lax.psum_scatter(rows, "z", scatter_dimension=0, tiled=True)[0]
 

time: 232 us -> 228 us (0.983)
  other arithmetic: 20.1 us -> 3.22 us
  Pallas kernels: 38.8 us -> 51.5 us
  local copies, waits for them, and re-layouts: 4.88 us -> 9.05 us
  waiting for transfers between devices: 134 us -> 130 us
    add x1 -> x0, other arithmetic: 16.9 us -> none  [shards(): chip = own + got]
    pallas_call x2 -> x8, Pallas kernels: 38.8 us -> 51.5 us  [block_matmul(): pl.pallas_call(kernel, grid_spec=grid_spec, out_shape=out_shape, input_ou...]
    ppermute x1 -> x4, waiting for transfers between devices: 4.65 us -> 0.01 us  [shards(): got.append(lax.ppermute(theirs, 'core', perm=[(0, 1), (1, 0)]))]
    unnamed x1 -> x11, local copies, waits for them, and re-layouts: 3.18 us -> 7.35 us
  transfers between devices with their start and end apart: 3 -> 6, of which waited for: 3 -> 2; matrix products, arithmetic and copies ran while one was open for 0% -> 0% of each run, Pallas kernels for 8% -> 17%
where the time goes in v4:
time: 228 us; the launch traced here: 227 us
  waiting for transfers between devices  130 us (57%)
  Pallas kernels  51.5 us (23%)
  blocking collectives  16.6 us (7%)
  between operations  16 us (7%)
  local copies, waits for them, and re-layouts  9.05 us (4%)
  other arithmetic  3.22 us (1%)
    unnamed x3, waiting for transfers between devices  105 us
    pallas_call x8, Pallas kernels, block_matmul(): pl.pallas_call(kernel, grid_spec=grid_spec, out_shape=out_shape, input_ou...  51.5 us
    reduce_scatter x1, waiting for transfers between devices, shards(): return lax.psum_scatter(rows, 'z', scatter_dimension=0, tiled=True)[0]  25.3 us
    psum x1, blocking collectives, shards(): lax.psum((jnp.sum((new_logp[0] - old_logp[0]) * masked), jnp.sum(masked))...  16.6 us
    unnamed x11, local copies, waits for them, and re-layouts  7.35 us
  transfers between devices with their start and end apart: 6, of which 2 were waited for; matrix products, arithmetic and copies ran while one was open for 0% of the time, Pallas kernels for 17%

profile of v4, /device:TPU:0, one launch (start us, length us, event | category | flops | bytes accessed | tf_op | source)
XLA Modules:
  0.0 227.3 jit_solution(650631195025531169)
XLA Ops:
  6.5 0.0 reduce-scatter.7.cloned.1.call-start
  7.2 0.7 sub.12
  7.9 1.4 convert_reduce_fusion
  9.3 16.6 %all-reduce.1 = (f32[]{:T(128)}, f32[]{:T(128)}) all-reduce(f32[]{:T(128)} %get-tuple-element.6, f32[]{:T(128)} %get-tuple-element.5), channel_id=1, replica_groups=mesh['dp'=16,'z'=4,'core'=2] {'z','core'}, use_global_device_ids=true, to_apply=%region_1.2 | all-reduce | flops 2 | bytes 16 | tf_op jit(solution)/shard_map/psum | solution.py:92
  27.8 1.7 copy.14
  29.5 3.2 %copy.15 = bf16[1024,1536]{0,1:T(8,128)(2,1)S(1)} copy(bf16[1024,1536]{1,0:T(8,128)(2,1)} %param.7) | data formatting | bytes 6291456 | tf_op args[0]
  32.7 1.2 convert_multiply_fusion.coef_ref
  33.8 0.0 copy-start
  33.8 6.1 %shard_map.76 = f32[16,96,640]{2,1,0:T(8,128)} custom-call(s32[1]{0:T(128)} %bitcast.14.col_ref, f32[1024,1]{1,0:T(8,128)S(1)} %convert_multiply_fusion.coef_ref, bf16[1024,5120]{1,0:T(8,128)(2,1)} %grad_ref.15, bf16[1536,1024]{1,0:T(8,128)(2,1)S(1)} %bitcast.20), custom_call_target="tpu_custom_call" | custom-call | flops 2013265920 | bytes 8388608 | tf_op jit(solution)/shard_map/pallas_call | solution.py:71
  39.9 0.0 copy-done
  39.9 0.0 collective-permute-start.3
  39.9 0.0 copy-start.1
  39.9 1.0 copy-done.1
  41.0 5.9 %shard_map.75 = f32[16,96,640]{2,1,0:T(8,128)} custom-call(s32[1]{0:T(128)} %bitcast.12.col_ref, f32[1024,1]{1,0:T(8,128)S(1)} %copy-done.1, bf16[1024,5120]{1,0:T(8,128)(2,1)} %grad_ref.15, bf16[1536,1024]{1,0:T(8,128)(2,1)S(1)} %bitcast.21), custom_call_target="tpu_custom_call" | custom-call | flops 2013265920 | bytes 8388608 | tf_op jit(solution)/shard_map/pallas_call | solution.py:71
  46.9 0.5 collective-permute-start.2
  47.4 0.0 copy-start.2
  47.4 1.0 copy-done.2
  48.4 6.0 %shard_map.74 = f32[16,96,640]{2,1,0:T(8,128)} custom-call(s32[1]{0:T(128)} %bitcast.10.col_ref, f32[1024,1]{1,0:T(8,128)S(1)} %copy-done.2, bf16[1024,5120]{1,0:T(8,128)(2,1)} %grad_ref.15, bf16[1536,1024]{1,0:T(8,128)(2,1)S(1)} %bitcast.22), custom_call_target="tpu_custom_call" | custom-call | flops 2013265920 | bytes 8388608 | tf_op jit(solution)/shard_map/pallas_call | solution.py:71
  54.4 0.0 collective-permute-start.1
  54.4 0.0 copy-start.3
  54.4 1.0 copy-done.3
  55.4 5.9 %shard_map.73 = f32[16,96,640]{2,1,0:T(8,128)} custom-call(s32[1]{0:T(128)} %bitcast.8.col_ref, f32[1024,1]{1,0:T(8,128)S(1)} %copy-done.3, bf16[1024,5120]{1,0:T(8,128)(2,1)} %grad_ref.15, bf16[1536,1024]{1,0:T(8,128)(2,1)S(1)} %bitcast.23), custom_call_target="tpu_custom_call" | custom-call | flops 2013265920 | bytes 8388608 | tf_op jit(solution)/shard_map/pallas_call | solution.py:71
  61.4 0.5 collective-permute-start
  61.9 0.0 collective-permute-done.3.rest_0_
  61.9 0.0 copy-start.4
  61.9 1.0 copy-done.4
  62.9 6.9 %shard_map.77.rest_1_ = f32[16,4,96,640]{3,2,1,0:T(8,128)} custom-call(s32[1]{0:T(128)} %bitcast.13.col_ref, f32[1024,1]{1,0:T(8,128)S(1)} %copy-done.4, bf16[1024,5120]{1,0:T(8,128)(2,1)} %grad_ref.15, bf16[1536,1024]{1,0:T(8,128)(2,1)S(1)} %bitcast.24, f32[16,96,640]{2,1,0:T(8,128)} %collective-permute-done.3.rest_0_), custom_call_target="tpu_custom_call" | custom-call | flops 2013265920 | bytes 12320768 | tf_op jit(solution)/shard_map/pallas_call | solution.py:71
  69.8 0.0 collective-permute-done.2.rest_0_
  69.8 6.9 %shard_map.78.rest_1_ = f32[16,4,96,640]{3,2,1,0:T(8,128)} custom-call(s32[1]{0:T(128)} %bitcast.11.col_ref, f32[1024,1]{1,0:T(8,128)S(1)} %copy-done.4, bf16[1024,5120]{1,0:T(8,128)(2,1)} %grad_ref.15, bf16[1536,1024]{1,0:T(8,128)(2,1)S(1)} %bitcast.25, f32[16,96,640]{2,1,0:T(8,128)} %collective-permute-done.2.rest_0_, ...), custom_call_target="tpu_custom_call", output_to_operand_aliasing={{}: (5, {})} | custom-call | flops 2013265920 | bytes 12320768 | tf_op jit(solution)/shard_map/pallas_call | solution.py:71
  76.7 0.0 collective-permute-done.1.rest_0_
  76.8 6.9 %shard_map.79.rest_1_ = f32[16,4,96,640]{3,2,1,0:T(8,128)} custom-call(s32[1]{0:T(128)} %bitcast.9.col_ref, f32[1024,1]{1,0:T(8,128)S(1)} %copy-done.4, bf16[1024,5120]{1,0:T(8,128)(2,1)} %grad_ref.15, bf16[1536,1024]{1,0:T(8,128)(2,1)S(1)} %bitcast.26, f32[16,96,640]{2,1,0:T(8,128)} %collective-permute-done.1.rest_0_, ...), custom_call_target="tpu_custom_call", output_to_operand_aliasing={{}: (5, {})} | custom-call | flops 2013265920 | bytes 12320768 | tf_op jit(solution)/shard_map/pallas_call | solution.py:71
  83.7 0.0 collective-permute-done.rest_0_
  83.7 6.9 %shard_map.80 = f32[16,4,96,640]{3,2,1,0:T(8,128)} custom-call(s32[1]{0:T(128)} %bitcast.col_ref, f32[1024,1]{1,0:T(8,128)S(1)} %copy-done.4, bf16[1024,5120]{1,0:T(8,128)(2,1)} %grad_ref.15, bf16[1536,1024]{1,0:T(8,128)(2,1)S(1)} %bitcast.27, f32[16,96,640]{2,1,0:T(8,128)} %collective-permute-done.rest_0_, ...), custom_call_target="tpu_custom_call", output_to_operand_aliasing={{}: (5, {})} | custom-call | flops 2013265920 | bytes 12320768 | tf_op jit(solution)/shard_map/pallas_call | solution.py:71
  90.5 0.0 reduce-scatter.7.cloned.1.call-update
  90.6 0.0 reduce-scatter.5.cloned.1.call-start
  90.6 104.5 %reduce-scatter.7.cloned.1.call-done = f32[1,4,96,640]{3,2,1,0:T(8,128)} async-done(((f32[16,4,96,640]{3,2,1,0:T(8,128)}), f32[1,4,96,640]{3,2,1,0:T(8,128)}) %reduce-scatter.7.cloned.1.call-update) | async-done | bytes 983056
  195.1 0.0 reduce-scatter.5.cloned.1.call-update
  195.2 25.3 %reduce-scatter.5.cloned.1.call-done = f32[1,96,640]{2,1,0:T(8,128)} async-done(((f32[4,96,640]{2,1,0:T(8,128)}), f32[1,96,640]{2,1,0:T(8,128)}) %reduce-scatter.5.cloned.1.call-update) | async-done | bytes 245776 | tf_op jit(solution)/shard_map/reduce_scatter | solution.py:120
Async XLA Ops:
  6.5 188.6 %reduce-scatter.7.cloned.1.call-start = ((), (), s32[]{:S(2)}) async-start(), calls=%async_computation.3 | async-start | bytes 16711680
  33.8 6.1 %copy-start = (f32[1024,1]{1,0:T(8,128)}, f32[1024,1]{1,0:T(8,128)S(1)}, u32[]{:S(2)}) copy-start(f32[1024,1]{1,0:T(8,128)S(1)} %convert_multiply_fusion.coef_ref) | copy-start | bytes 12292
  39.9 21.9 %collective-permute-start.3 = (f32[16,96,640]{2,1,0:T(8,128)}, f32[16,96,640]{2,1,0:T(8,128)}, u32[]{:S(2)}, u32[]{:S(2)}) collective-permute-start(f32[16,96,640]{2,1,0:T(8,128)} %shard_map.76), channel_id=1, source_target_pairs={{0,1},{1,0},{2,3},{3,2},{4,5},{5,4},{6,7},{7,6},{8,9},{9,8},{10,11... | collective-permute-start | bytes 11796488 | tf_op jit(solution)/shard_map/ppermute | solution.py:114
  39.9 1.0 copy-start.1
  46.9 23.0 %collective-permute-start.2 = (f32[16,96,640]{2,1,0:T(8,128)}, f32[16,96,640]{2,1,0:T(8,128)}, u32[]{:S(2)}, u32[]{:S(2)}) collective-permute-start(f32[16,96,640]{2,1,0:T(8,128)} %shard_map.75), channel_id=1, source_target_pairs={{0,1},{1,0},{2,3},{3,2},{4,5},{5,4},{6,7},{7,6},{8,9},{9,8},{10,11... | collective-permute-start | bytes 11796488 | tf_op jit(solution)/shard_map/ppermute | solution.py:114
  47.4 1.0 copy-start.2
  54.4 22.4 %collective-permute-start.1 = (f32[16,96,640]{2,1,0:T(8,128)}, f32[16,96,640]{2,1,0:T(8,128)}, u32[]{:S(2)}, u32[]{:S(2)}) collective-permute-start(f32[16,96,640]{2,1,0:T(8,128)} %shard_map.74), channel_id=1, source_target_pairs={{0,1},{1,0},{2,3},{3,2},{4,5},{5,4},{6,7},{7,6},{8,9},{9,8},{10,11... | collective-permute-start | bytes 11796488 | tf_op jit(solution)/shard_map/ppermute | solution.py:114
  54.4 1.0 copy-start.3
  61.4 22.3 %collective-permute-start = (f32[16,96,640]{2,1,0:T(8,128)}, f32[16,96,640]{2,1,0:T(8,128)}, u32[]{:S(2)}, u32[]{:S(2)}) collective-permute-start(f32[16,96,640]{2,1,0:T(8,128)} %shard_map.73), channel_id=1, source_target_pairs={{0,1},{1,0},{2,3},{3,2},{4,5},{5,4},{6,7},{7,6},{8,9},{9,8},{10,11... | collective-permute-start | bytes 11796488 | tf_op jit(solution)/shard_map/ppermute | solution.py:114
  61.9 1.0 copy-start.4
  90.6 129.9 %reduce-scatter.5.cloned.1.call-start = ((), (), s32[]{:S(2)}) async-start(), calls=%async_computation.2 | async-start | bytes 1228800 | tf_op jit(solution)/shard_map/reduce_scatter | solution.py:120
Sparse Core Ops, SparseCore 0:
  90.7 104.4 reduce-scatter.6
  197.7 22.6 reduce-scatter.4

commit v5 on v4

--- a/solution.py
+++ b/solution.py
@@ -9,7 +9,7 @@
 
 CLIP_LOW = 0.0003
 CLIP_HIGH = 0.0004
-ROW_TILE = 384
+ROW_TILE = 768
 
 
 def block_matmul(col, coef, grad, hid_t, n_dp, width, addend=None, into=None, slot=0, n_slots=1):
@@ -81,6 +81,55 @@
     )(*args)
 
 
+def z_reduce_scatter(x, axis, n):
+    _, r, c = x.shape
+
+    def kernel(x_ref, out_ref, recv, send_sem, recv_sem):
+        me = lax.axis_index(axis)
+        barrier = pltpu.get_barrier_semaphore()
+        for d in range(1, n):
+            peer = lax.rem(me + d, n)
+            pl.semaphore_signal(barrier, inc=1, device_id={axis: peer},
+                                device_id_type=pl.DeviceIdType.MESH)
+        pl.semaphore_wait(barrier, n - 1)
+        copies = []
+        for d in range(1, n):
+            peer = lax.rem(me + d, n)
+            cp = pltpu.make_async_remote_copy(
+                src_ref=x_ref.at[peer], dst_ref=recv.at[me],
+                send_sem=send_sem.at[d], recv_sem=recv_sem.at[me],
+                device_id={axis: peer}, device_id_type=pl.DeviceIdType.MESH)
+            cp.start()
+            copies.append(cp)
+        total = x_ref[me]
+        for d in range(1, n):
+            src = lax.rem(me + n - d, n)
+            incoming = pltpu.make_async_remote_copy(
+                src_ref=x_ref.at[src], dst_ref=recv.at[src],
+                send_sem=send_sem.at[d], recv_sem=recv_sem.at[src],
+                device_id={axis: src}, device_id_type=pl.DeviceIdType.MESH)
+            incoming.wait_recv()
+            total = total + recv[src]
+        for cp in copies:
+            cp.wait_send()
+        out_ref[...] = total
+
+    return pl.pallas_call(
+        kernel,
+        out_shape=jax.ShapeDtypeStruct((r, c), jnp.float32),
+        in_specs=[pl.BlockSpec(memory_space=pltpu.VMEM)],
+        out_specs=pl.BlockSpec(memory_space=pltpu.VMEM),
+        scratch_shapes=[
+            pltpu.VMEM((n, r, c), jnp.float32),
+            pltpu.SemaphoreType.DMA((n,)),
+            pltpu.SemaphoreType.DMA((n,)),
+        ],
+        compiler_params=pltpu.CompilerParams(collective_id=0, has_side_effects=True),
+        cost_estimate=pl.CostEstimate(flops=n * r * c, transcendentals=0,
+                                      bytes_accessed=3 * n * r * c * 4),
+    )(x)
+
+
 def shards(hidden_acts, out_grad, old_logp, new_logp, roll_len, resp_mask, advantage):
     n_dp = lax.axis_size("dp")
     n_z = lax.axis_size("z")
@@ -117,7 +166,7 @@
         chip = block_matmul(col_index(k, core), token_coef, out_grad, hid_t, n_dp, col,
                             addend=got[k], into=chip, slot=k, n_slots=n_z)
     rows = lax.psum_scatter(chip, "dp", scatter_dimension=0, tiled=True)[0]
-    return lax.psum_scatter(rows, "z", scatter_dimension=0, tiled=True)[0]
+    return z_reduce_scatter(rows, "z", n_z)
 
 
 def solution(mesh):

time: 228 us -> 218 us (0.956)
  waiting for transfers between devices: 130 us -> 105 us
  Pallas kernels: 51.5 us -> 65.3 us
    reduce_scatter x1 -> x0, waiting for transfers between devices: 25.3 us -> none  [shards(): return lax.psum_scatter(rows, 'z', scatter_dimension=0, tiled=True)[0]]
    pallas_call x0 -> x1, Pallas kernels: none -> 17 us  [z_reduce_scatter(): pl.pallas_call(kernel, out_shape=jax.ShapeDtypeStruct((r, c), jnp.float32...]
    pallas_call x8, Pallas kernels: 51.5 us -> 48.2 us  [block_matmul(): pl.pallas_call(kernel, grid_spec=grid_spec, out_shape=out_shape, input_ou...]
    unnamed x11 -> x12, local copies, waits for them, and re-layouts: 7.35 us -> 9 us
    unnamed x3 -> x2, waiting for transfers between devices: 105 us -> 105 us
  transfers between devices with their start and end apart: 6 -> 5, of which waited for: 2 -> 1; matrix products, arithmetic and copies ran while one was open for 0% -> 0% of each run, Pallas kernels for 17% -> 17%
where the time goes in v5:
time: 218 us; the launch traced here: 217 us
  waiting for transfers between devices  105 us (48%)
  Pallas kernels  65.3 us (30%)
  blocking collectives  16.6 us (8%)
  between operations  16 us (7%)
  local copies, waits for them, and re-layouts  10.7 us (5%)
  other arithmetic  3.22 us (1%)
    unnamed x2, waiting for transfers between devices  105 us
    pallas_call x8, Pallas kernels, block_matmul(): pl.pallas_call(kernel, grid_spec=grid_spec, out_shape=out_shape, input_ou...  48.2 us
    pallas_call x1, Pallas kernels, z_reduce_scatter(): pl.pallas_call(kernel, out_shape=jax.ShapeDtypeStruct((r, c), jnp.float32...  17 us
    psum x1, blocking collectives, shards(): lax.psum((jnp.sum((new_logp[0] - old_logp[0]) * masked), jnp.sum(masked))...  16.6 us
    unnamed x12, local copies, waits for them, and re-layouts  9 us
  transfers between devices with their start and end apart: 5, of which 1 were waited for; matrix products, arithmetic and copies ran while one was open for 0% of the time, Pallas kernels for 17%

profile of v5, /device:TPU:0, one launch (start us, length us, event | category | flops | bytes accessed | tf_op | source)
XLA Modules:
  0.0 217.4 jit_solution(10728866788521570706)
XLA Ops:
  6.5 0.0 reduce-scatter.4.cloned.1.call-start
  7.2 0.7 sub.12
  7.9 1.4 convert_reduce_fusion
  9.3 16.6 %all-reduce.1 = (f32[]{:T(128)}, f32[]{:T(128)}) all-reduce(f32[]{:T(128)} %get-tuple-element.6, f32[]{:T(128)} %get-tuple-element.5), channel_id=1, replica_groups=mesh['dp'=16,'z'=4,'core'=2] {'z','core'}, use_global_device_ids=true, to_apply=%region_1.2 | all-reduce | flops 2 | bytes 16 | tf_op jit(solution)/shard_map/psum | solution.py:141
  27.8 1.7 copy.14
  29.5 3.2 %copy.15 = bf16[1024,1536]{0,1:T(8,128)(2,1)S(1)} copy(bf16[1024,1536]{1,0:T(8,128)(2,1)} %param.7) | data formatting | bytes 6291456 | tf_op args[0]
  32.7 1.2 convert_multiply_fusion.coef_ref
  33.8 0.0 copy-start
  33.8 5.8 %shard_map.76 = f32[16,96,640]{2,1,0:T(8,128)} custom-call(s32[1]{0:T(128)} %bitcast.14.col_ref, f32[1024,1]{1,0:T(8,128)S(1)} %convert_multiply_fusion.coef_ref, bf16[1024,5120]{1,0:T(8,128)(2,1)} %grad_ref.15, bf16[1536,1024]{1,0:T(8,128)(2,1)S(1)} %bitcast.19), custom_call_target="tpu_custom_call" | custom-call | flops 2013265920 | bytes 8388608 | tf_op jit(solution)/shard_map/pallas_call | solution.py:71
  39.7 0.0 copy-done
  39.7 0.0 collective-permute-start.3
  39.7 0.0 copy-start.1
  39.7 1.0 copy-done.1
  40.7 5.6 %shard_map.75 = f32[16,96,640]{2,1,0:T(8,128)} custom-call(s32[1]{0:T(128)} %bitcast.12.col_ref, f32[1024,1]{1,0:T(8,128)S(1)} %copy-done.1, bf16[1024,5120]{1,0:T(8,128)(2,1)} %grad_ref.15, bf16[1536,1024]{1,0:T(8,128)(2,1)S(1)} %bitcast.20), custom_call_target="tpu_custom_call" | custom-call | flops 2013265920 | bytes 8388608 | tf_op jit(solution)/shard_map/pallas_call | solution.py:71
  46.4 0.5 collective-permute-start.2
  46.9 0.0 copy-start.2
  46.9 1.0 copy-done.2
  47.9 5.7 %shard_map.74 = f32[16,96,640]{2,1,0:T(8,128)} custom-call(s32[1]{0:T(128)} %bitcast.10.col_ref, f32[1024,1]{1,0:T(8,128)S(1)} %copy-done.2, bf16[1024,5120]{1,0:T(8,128)(2,1)} %grad_ref.15, bf16[1536,1024]{1,0:T(8,128)(2,1)S(1)} %bitcast.21), custom_call_target="tpu_custom_call" | custom-call | flops 2013265920 | bytes 8388608 | tf_op jit(solution)/shard_map/pallas_call | solution.py:71
  53.7 0.0 collective-permute-start.1
  53.7 0.0 copy-start.3
  53.7 1.0 copy-done.3
  54.7 5.7 %shard_map.73 = f32[16,96,640]{2,1,0:T(8,128)} custom-call(s32[1]{0:T(128)} %bitcast.8.col_ref, f32[1024,1]{1,0:T(8,128)S(1)} %copy-done.3, bf16[1024,5120]{1,0:T(8,128)(2,1)} %grad_ref.15, bf16[1536,1024]{1,0:T(8,128)(2,1)S(1)} %bitcast.22), custom_call_target="tpu_custom_call" | custom-call | flops 2013265920 | bytes 8388608 | tf_op jit(solution)/shard_map/pallas_call | solution.py:71
  60.4 0.5 collective-permute-start
  60.9 0.0 collective-permute-done.3.rest_0_
  60.9 0.0 copy-start.4
  60.9 1.0 copy-done.4
  61.9 6.4 %shard_map.77.rest_1_ = f32[16,4,96,640]{3,2,1,0:T(8,128)} custom-call(s32[1]{0:T(128)} %bitcast.13.col_ref, f32[1024,1]{1,0:T(8,128)S(1)} %copy-done.4, bf16[1024,5120]{1,0:T(8,128)(2,1)} %grad_ref.15, bf16[1536,1024]{1,0:T(8,128)(2,1)S(1)} %bitcast.23, f32[16,96,640]{2,1,0:T(8,128)} %collective-permute-done.3.rest_0_), custom_call_target="tpu_custom_call" | custom-call | flops 2013265920 | bytes 12320768 | tf_op jit(solution)/shard_map/pallas_call | solution.py:71
  68.3 0.0 collective-permute-done.2.rest_0_
  68.3 6.3 %shard_map.78.rest_1_ = f32[16,4,96,640]{3,2,1,0:T(8,128)} custom-call(s32[1]{0:T(128)} %bitcast.11.col_ref, f32[1024,1]{1,0:T(8,128)S(1)} %copy-done.4, bf16[1024,5120]{1,0:T(8,128)(2,1)} %grad_ref.15, bf16[1536,1024]{1,0:T(8,128)(2,1)S(1)} %bitcast.24, f32[16,96,640]{2,1,0:T(8,128)} %collective-permute-done.2.rest_0_, ...), custom_call_target="tpu_custom_call", output_to_operand_aliasing={{}: (5, {})} | custom-call | flops 2013265920 | bytes 12320768 | tf_op jit(solution)/shard_map/pallas_call | solution.py:71
  74.6 0.0 collective-permute-done.1.rest_0_
  74.7 6.3 %shard_map.79.rest_1_ = f32[16,4,96,640]{3,2,1,0:T(8,128)} custom-call(s32[1]{0:T(128)} %bitcast.9.col_ref, f32[1024,1]{1,0:T(8,128)S(1)} %copy-done.4, bf16[1024,5120]{1,0:T(8,128)(2,1)} %grad_ref.15, bf16[1536,1024]{1,0:T(8,128)(2,1)S(1)} %bitcast.25, f32[16,96,640]{2,1,0:T(8,128)} %collective-permute-done.1.rest_0_, ...), custom_call_target="tpu_custom_call", output_to_operand_aliasing={{}: (5, {})} | custom-call | flops 2013265920 | bytes 12320768 | tf_op jit(solution)/shard_map/pallas_call | solution.py:71
  81.0 0.0 collective-permute-done.rest_0_
  81.0 6.3 %shard_map.80 = f32[16,4,96,640]{3,2,1,0:T(8,128)} custom-call(s32[1]{0:T(128)} %bitcast.col_ref, f32[1024,1]{1,0:T(8,128)S(1)} %copy-done.4, bf16[1024,5120]{1,0:T(8,128)(2,1)} %grad_ref.15, bf16[1536,1024]{1,0:T(8,128)(2,1)S(1)} %bitcast.26, f32[16,96,640]{2,1,0:T(8,128)} %collective-permute-done.rest_0_, ...), custom_call_target="tpu_custom_call", output_to_operand_aliasing={{}: (5, {})} | custom-call | flops 2013265920 | bytes 12320768 | tf_op jit(solution)/shard_map/pallas_call | solution.py:71
  87.3 0.0 reduce-scatter.4.cloned.1.call-update
  87.3 104.5 %reduce-scatter.4.cloned.1.call-done = f32[1,4,96,640]{3,2,1,0:T(8,128)} async-done(((f32[16,4,96,640]{3,2,1,0:T(8,128)}), f32[1,4,96,640]{3,2,1,0:T(8,128)}) %reduce-scatter.4.cloned.1.call-update) | async-done | bytes 983056
  191.8 17.0 %shard_map.81 = f32[96,640]{1,0:T(8,128)} custom-call(f32[4,96,640]{2,1,0:T(8,128)} %bitcast.27), custom_call_target="tpu_custom_call" | custom-call | flops 245760 | bytes 2949120 | tf_op jit(solution)/shard_map/pallas_call | solution.py:117
  208.9 1.7 copy.22
Async XLA Ops:
  6.5 185.3 %reduce-scatter.4.cloned.1.call-start = ((), (), s32[]{:S(2)}) async-start(), calls=%async_computation.1 | async-start | bytes 16711680
  33.8 5.9 %copy-start = (f32[1024,1]{1,0:T(8,128)}, f32[1024,1]{1,0:T(8,128)S(1)}, u32[]{:S(2)}) copy-start(f32[1024,1]{1,0:T(8,128)S(1)} %convert_multiply_fusion.coef_ref) | copy-start | bytes 12292
  39.7 21.2 %collective-permute-start.3 = (f32[16,96,640]{2,1,0:T(8,128)}, f32[16,96,640]{2,1,0:T(8,128)}, u32[]{:S(2)}, u32[]{:S(2)}) collective-permute-start(f32[16,96,640]{2,1,0:T(8,128)} %shard_map.76), channel_id=1, source_target_pairs={{0,1},{1,0},{2,3},{3,2},{4,5},{5,4},{6,7},{7,6},{8,9},{9,8},{10,11... | collective-permute-start | bytes 11796488 | tf_op jit(solution)/shard_map/ppermute | solution.py:163
  39.7 1.0 copy-start.1
  46.4 21.9 %collective-permute-start.2 = (f32[16,96,640]{2,1,0:T(8,128)}, f32[16,96,640]{2,1,0:T(8,128)}, u32[]{:S(2)}, u32[]{:S(2)}) collective-permute-start(f32[16,96,640]{2,1,0:T(8,128)} %shard_map.75), channel_id=1, source_target_pairs={{0,1},{1,0},{2,3},{3,2},{4,5},{5,4},{6,7},{7,6},{8,9},{9,8},{10,11... | collective-permute-start | bytes 11796488 | tf_op jit(solution)/shard_map/ppermute | solution.py:163
  46.9 1.0 copy-start.2
  53.7 21.0 %collective-permute-start.1 = (f32[16,96,640]{2,1,0:T(8,128)}, f32[16,96,640]{2,1,0:T(8,128)}, u32[]{:S(2)}, u32[]{:S(2)}) collective-permute-start(f32[16,96,640]{2,1,0:T(8,128)} %shard_map.74), channel_id=1, source_target_pairs={{0,1},{1,0},{2,3},{3,2},{4,5},{5,4},{6,7},{7,6},{8,9},{9,8},{10,11... | collective-permute-start | bytes 11796488 | tf_op jit(solution)/shard_map/ppermute | solution.py:163
  53.7 1.0 copy-start.3
  60.4 20.6 %collective-permute-start = (f32[16,96,640]{2,1,0:T(8,128)}, f32[16,96,640]{2,1,0:T(8,128)}, u32[]{:S(2)}, u32[]{:S(2)}) collective-permute-start(f32[16,96,640]{2,1,0:T(8,128)} %shard_map.73), channel_id=1, source_target_pairs={{0,1},{1,0},{2,3},{3,2},{4,5},{5,4},{6,7},{7,6},{8,9},{9,8},{10,11... | collective-permute-start | bytes 11796488 | tf_op jit(solution)/shard_map/ppermute | solution.py:163
  60.9 1.0 copy-start.4
Sparse Core Ops, SparseCore 0:
  87.4 104.3 reduce-scatter.3

commit v6 on v5

--- a/solution.py
+++ b/solution.py
@@ -10,6 +10,7 @@
 CLIP_LOW = 0.0003
 CLIP_HIGH = 0.0004
 ROW_TILE = 768
+Z_FIRST = 256
 
 
 def block_matmul(col, coef, grad, hid_t, n_dp, width, addend=None, into=None, slot=0, n_slots=1):
@@ -18,13 +19,18 @@
     per_tile = ROW_TILE // rows
     n_tiles = hb // ROW_TILE
     grouped = n_slots > 1
+    keep = width - Z_FIRST
 
     def kernel(col_ref, coef_ref, grad_ref, hid_ref, *rest):
         rest = list(rest)
         add_ref = rest.pop(0) if addend is not None else None
         if into is not None:
             rest.pop(0)
-        out_ref, scaled_ref = rest
+            rest.pop(0)
+        if grouped:
+            out_ref, zout_ref, scaled_ref = rest
+        else:
+            out_ref, scaled_ref = rest
 
         @pl.when(pl.program_id(0) == 0)
         def _():
@@ -36,7 +42,8 @@
             if add_ref is not None:
                 part = part + add_ref[k]
             if grouped:
-                out_ref[k, 0] = part
+                out_ref[k, 0] = part[:, :keep]
+                zout_ref[0, k] = part[:, keep:]
             else:
                 out_ref[k] = part
 
@@ -51,12 +58,14 @@
         args.append(addend)
     aliases = {}
     if into is not None:
-        in_specs.append(pl.BlockSpec(memory_space=pl.ANY))
-        aliases = {len(args): 0}
-        args.append(into)
+        in_specs += [pl.BlockSpec(memory_space=pl.ANY)] * 2
+        aliases = {len(args): 0, len(args) + 1: 1}
+        args += list(into)
     if grouped:
-        out_shape = jax.ShapeDtypeStruct((n_dp, n_slots, rows, width), jnp.float32)
-        out_spec = pl.BlockSpec((per_tile, 1, rows, width), lambda i, c: (i, slot, 0, 0))
+        out_shape = (jax.ShapeDtypeStruct((n_dp, n_slots, rows, keep), jnp.float32),
+                     jax.ShapeDtypeStruct((n_slots, n_dp, rows, Z_FIRST), jnp.float32))
+        out_spec = (pl.BlockSpec((per_tile, 1, rows, keep), lambda i, c: (i, slot, 0, 0)),
+                    pl.BlockSpec((1, per_tile, rows, Z_FIRST), lambda i, c: (slot, i, 0, 0)))
     else:
         out_shape = jax.ShapeDtypeStruct((n_dp, rows, width), jnp.float32)
         out_spec = pl.BlockSpec((per_tile, rows, width), lambda i, c: (i, 0, 0))
@@ -81,8 +90,11 @@
     )(*args)
 
 
-def z_reduce_scatter(x, axis, n):
-    _, r, c = x.shape
+def z_reduce_scatter(x, axis, n, cid):
+    rest_shape = x.shape[1:]
+    size = 1
+    for s in x.shape:
+        size *= s
 
     def kernel(x_ref, out_ref, recv, send_sem, recv_sem):
         me = lax.axis_index(axis)
@@ -116,17 +128,17 @@
 
     return pl.pallas_call(
         kernel,
-        out_shape=jax.ShapeDtypeStruct((r, c), jnp.float32),
+        out_shape=jax.ShapeDtypeStruct(rest_shape, jnp.float32),
         in_specs=[pl.BlockSpec(memory_space=pltpu.VMEM)],
         out_specs=pl.BlockSpec(memory_space=pltpu.VMEM),
         scratch_shapes=[
-            pltpu.VMEM((n, r, c), jnp.float32),
+            pltpu.VMEM(x.shape, jnp.float32),
             pltpu.SemaphoreType.DMA((n,)),
             pltpu.SemaphoreType.DMA((n,)),
         ],
-        compiler_params=pltpu.CompilerParams(collective_id=0, has_side_effects=True),
-        cost_estimate=pl.CostEstimate(flops=n * r * c, transcendentals=0,
-                                      bytes_accessed=3 * n * r * c * 4),
+        compiler_params=pltpu.CompilerParams(
+            collective_id=cid, has_side_effects=True, vmem_limit_bytes=40 * 1024 * 1024),
+        cost_estimate=pl.CostEstimate(flops=size, transcendentals=0, bytes_accessed=3 * size * 4),
     )(x)
 
 
@@ -165,8 +177,12 @@
     for k in range(n_z):
         chip = block_matmul(col_index(k, core), token_coef, out_grad, hid_t, n_dp, col,
                             addend=got[k], into=chip, slot=k, n_slots=n_z)
-    rows = lax.psum_scatter(chip, "dp", scatter_dimension=0, tiled=True)[0]
-    return z_reduce_scatter(rows, "z", n_z)
+    dp_first, z_first = chip
+    rows = lax.psum_scatter(dp_first, "dp", scatter_dimension=0, tiled=True)[0]
+    late = z_reduce_scatter(z_first, "z", n_z, 0)
+    late = lax.psum_scatter(late, "dp", scatter_dimension=0, tiled=True)[0]
+    early = z_reduce_scatter(rows, "z", n_z, 1)
+    return jnp.concatenate([early, late], axis=1)
 
 
 def solution(mesh):

time: 218 us -> 259 us (1.19)
  Pallas kernels: 65.3 us -> 131 us
  waiting for transfers between devices: 105 us -> 75.6 us
    pallas_call x1 -> x2, Pallas kernels: 17 us -> 83.2 us  [z_reduce_scatter(): pl.pallas_call(kernel, out_shape=jax.ShapeDtypeStruct(rest_shape, jnp.flo...]
    unnamed x2 -> x4, waiting for transfers between devices: 105 us -> 75.6 us
    unnamed x12 -> x15, local copies, waits for them, and re-layouts: 9 us -> 11.2 us
  transfers between devices with their start and end apart: 5 -> 6, of which waited for: 1 -> 2; matrix products, arithmetic and copies ran while one was open for 0% -> 0% of each run, Pallas kernels for 17% -> 46%
where the time goes in v6:
time: 259 us
  Pallas kernels  131 us (51%)
  waiting for transfers between devices  75.6 us (29%)
  blocking collectives  16.7 us (6%)
  between operations  16.1 us (6%)
  local copies, waits for them, and re-layouts  12.9 us (5%)
  other arithmetic  4.82 us (2%)
    pallas_call x2, Pallas kernels, z_reduce_scatter(): pl.pallas_call(kernel, out_shape=jax.ShapeDtypeStruct(rest_shape, jnp.flo...  83.2 us
    unnamed x4, waiting for transfers between devices  75.6 us
    pallas_call x8, Pallas kernels, block_matmul(): pl.pallas_call(kernel, grid_spec=grid_spec, out_shape=out_shape, input_ou...  48.1 us
    psum x1, blocking collectives, shards(): lax.psum((jnp.sum((new_logp[0] - old_logp[0]) * masked), jnp.sum(masked))...  16.7 us
    unnamed x15, local copies, waits for them, and re-layouts  11.2 us
  transfers between devices with their start and end apart: 6, of which 2 were waited for; matrix products, arithmetic and copies ran while one was open for 0% of the time, Pallas kernels for 46%

profile of v6, /device:TPU:0, one launch (start us, length us, event | category | flops | bytes accessed | tf_op | source)
XLA Modules:
  0.0 258.6 jit_solution(15787231362121902337)
XLA Ops:
  6.5 0.0 reduce-scatter.7.cloned.1.call-start
  7.2 0.7 sub.12
  7.9 1.4 convert_reduce_fusion
  9.3 16.7 %all-reduce.2 = (f32[]{:T(128)}, f32[]{:T(128)}) all-reduce(f32[]{:T(128)} %get-tuple-element.22, f32[]{:T(128)} %get-tuple-element.21), channel_id=1, replica_groups=mesh['dp'=16,'z'=4,'core'=2] {'z','core'}, use_global_device_ids=true, to_apply=%region_1.2 | all-reduce | flops 2 | bytes 16 | tf_op jit(solution)/shard_map/psum | solution.py:153
  27.9 1.7 copy.17
  29.6 3.2 %copy.18 = bf16[1024,1536]{0,1:T(8,128)(2,1)S(1)} copy(bf16[1024,1536]{1,0:T(8,128)(2,1)} %param.7) | data formatting | bytes 6291456 | tf_op args[0]
  32.8 1.2 convert_multiply_fusion.coef_ref
  34.0 0.0 copy-start.1
  34.0 5.9 %shard_map.76 = f32[16,96,640]{2,1,0:T(8,128)} custom-call(s32[1]{0:T(128)} %bitcast.14.col_ref, f32[1024,1]{1,0:T(8,128)S(1)} %convert_multiply_fusion.coef_ref, bf16[1024,5120]{1,0:T(8,128)(2,1)} %grad_ref.15, bf16[1536,1024]{1,0:T(8,128)(2,1)S(1)} %bitcast.20), custom_call_target="tpu_custom_call" | custom-call | flops 2013265920 | bytes 8388608 | tf_op jit(solution)/shard_map/pallas_call | solution.py:80
  39.8 0.0 copy-done.1
  39.8 0.0 collective-permute-start.3
  39.8 0.0 copy-start.2
  39.9 1.0 copy-done.2
  40.9 5.7 %shard_map.75 = f32[16,96,640]{2,1,0:T(8,128)} custom-call(s32[1]{0:T(128)} %bitcast.12.col_ref, f32[1024,1]{1,0:T(8,128)S(1)} %copy-done.2, bf16[1024,5120]{1,0:T(8,128)(2,1)} %grad_ref.15, bf16[1536,1024]{1,0:T(8,128)(2,1)S(1)} %bitcast.21), custom_call_target="tpu_custom_call" | custom-call | flops 2013265920 | bytes 8388608 | tf_op jit(solution)/shard_map/pallas_call | solution.py:80
  46.6 0.5 collective-permute-start.2
  47.1 0.0 copy-start.3
  47.1 1.0 copy-done.3
  48.1 5.7 %shard_map.74 = f32[16,96,640]{2,1,0:T(8,128)} custom-call(s32[1]{0:T(128)} %bitcast.10.col_ref, f32[1024,1]{1,0:T(8,128)S(1)} %copy-done.3, bf16[1024,5120]{1,0:T(8,128)(2,1)} %grad_ref.15, bf16[1536,1024]{1,0:T(8,128)(2,1)S(1)} %bitcast.22), custom_call_target="tpu_custom_call" | custom-call | flops 2013265920 | bytes 8388608 | tf_op jit(solution)/shard_map/pallas_call | solution.py:80
  53.8 0.0 collective-permute-start.1
  53.8 0.0 copy-start.4
  53.8 1.0 copy-done.4
  54.8 5.7 %shard_map.73 = f32[16,96,640]{2,1,0:T(8,128)} custom-call(s32[1]{0:T(128)} %bitcast.8.col_ref, f32[1024,1]{1,0:T(8,128)S(1)} %copy-done.4, bf16[1024,5120]{1,0:T(8,128)(2,1)} %grad_ref.15, bf16[1536,1024]{1,0:T(8,128)(2,1)S(1)} %bitcast.23), custom_call_target="tpu_custom_call" | custom-call | flops 2013265920 | bytes 8388608 | tf_op jit(solution)/shard_map/pallas_call | solution.py:80
  60.5 0.5 collective-permute-start
  61.0 0.0 collective-permute-done.3.rest_0_
  61.1 0.0 copy-start.5
  61.1 1.0 copy-done.5
  62.1 6.3 %shard_map.77 = (f32[16,4,96,384]{3,2,1,0:T(8,128)}, f32[4,16,96,256]{3,2,1,0:T(8,128)}) custom-call(s32[1]{0:T(128)} %bitcast.13.col_ref, f32[1024,1]{1,0:T(8,128)S(1)} %copy-done.5, bf16[1024,5120]{1,0:T(8,128)(2,1)} %grad_ref.15, bf16[1536,1024]{1,0:T(8,128)(2,1)S(1)} %bitcast.24, f32[16,96,640]{2,1,0:T(8,128)} %collective-permute-done.3.rest_0_), custom_call_target="tpu_custom_call" | custom-call | flops 2013265920 | bytes 12320768 | tf_op jit(solution)/shard_map/pallas_call | solution.py:80
  68.4 0.0 collective-permute-done.2.rest_0_
  68.4 6.3 %shard_map.78 = (f32[16,4,96,384]{3,2,1,0:T(8,128)}, f32[4,16,96,256]{3,2,1,0:T(8,128)}) custom-call(s32[1]{0:T(128)} %bitcast.11.col_ref, f32[1024,1]{1,0:T(8,128)S(1)} %copy-done.5, bf16[1024,5120]{1,0:T(8,128)(2,1)} %grad_ref.15, bf16[1536,1024]{1,0:T(8,128)(2,1)S(1)} %bitcast.25, ...), custom_call_target="tpu_custom_call", output_to_operand_aliasing={{0}: (5, {}), {1}: (6, {})} | custom-call | flops 2013265920 | bytes 12320768 | tf_op jit(solution)/shard_map/pallas_call | solution.py:80
  74.7 0.0 collective-permute-done.1.rest_0_
  74.7 6.3 %shard_map.79 = (f32[16,4,96,384]{3,2,1,0:T(8,128)}, f32[4,16,96,256]{3,2,1,0:T(8,128)}) custom-call(s32[1]{0:T(128)} %bitcast.9.col_ref, f32[1024,1]{1,0:T(8,128)S(1)} %copy-done.5, bf16[1024,5120]{1,0:T(8,128)(2,1)} %grad_ref.15, bf16[1536,1024]{1,0:T(8,128)(2,1)S(1)} %bitcast.26, ...), custom_call_target="tpu_custom_call", output_to_operand_aliasing={{0}: (5, {}), {1}: (6, {})} | custom-call | flops 2013265920 | bytes 12320768 | tf_op jit(solution)/shard_map/pallas_call | solution.py:80
  81.0 0.0 collective-permute-done.rest_0_
  81.0 6.3 %shard_map.80 = (f32[16,4,96,384]{3,2,1,0:T(8,128)}, f32[4,16,96,256]{3,2,1,0:T(8,128)}) custom-call(s32[1]{0:T(128)} %bitcast.col_ref, f32[1024,1]{1,0:T(8,128)S(1)} %copy-done.5, bf16[1024,5120]{1,0:T(8,128)(2,1)} %grad_ref.15, bf16[1536,1024]{1,0:T(8,128)(2,1)S(1)} %bitcast.27, ...), custom_call_target="tpu_custom_call", output_to_operand_aliasing={{0}: (5, {}), {1}: (6, {})} | custom-call | flops 2013265920 | bytes 12320768 | tf_op jit(solution)/shard_map/pallas_call | solution.py:80
  87.3 0.0 reduce-scatter.7.cloned.1.call-update
  87.4 0.0 reduce-scatter.9.cloned.1.call-start
  87.4 0.0 copy-start
  87.4 2.8 %copy-done = f32[4,16,96,256]{3,2,1,0:T(8,128)S(1)} copy-done((f32[4,16,96,256]{3,2,1,0:T(8,128)S(1)}, f32[4,16,96,256]{3,2,1,0:T(8,128)}, u32[]{:S(2)}) %copy-start) | copy-done | bytes 6291480
  90.2 73.1 %shard_map.82 = f32[16,96,256]{2,1,0:T(8,128)} custom-call(f32[4,16,96,256]{3,2,1,0:T(8,128)S(1)} %copy-done), custom_call_target="tpu_custom_call" | custom-call | flops 1572864 | bytes 18874368 | tf_op jit(solution)/shard_map/pallas_call | solution.py:129
  163.4 0.0 reduce-scatter.9.cloned.1.call-update
  163.4 10.5 %reduce-scatter.7.cloned.1.call-done = f32[1,4,96,384]{3,2,1,0:T(8,128)} async-done(((f32[16,4,96,384]{3,2,1,0:T(8,128)}), f32[1,4,96,384]{3,2,1,0:T(8,128)}) %reduce-scatter.7.cloned.1.call-update) | async-done | bytes 589840
  173.9 0.0 copy-start.6
  173.9 1.1 copy-done.6
  174.9 10.1 %shard_map.81 = f32[96,384]{1,0:T(8,128)S(1)} custom-call(f32[4,96,384]{2,1,0:T(8,128)S(1)} %bitcast.28), custom_call_target="tpu_custom_call" | custom-call | flops 147456 | bytes 1769472 | tf_op jit(solution)/shard_map/pallas_call | solution.py:129
  185.1 65.1 %reduce-scatter.9.cloned.1.call-done = f32[1,96,256]{2,1,0:T(8,128)} async-done(((f32[16,96,256]{2,1,0:T(8,128)}), f32[1,96,256]{2,1,0:T(8,128)}) %reduce-scatter.9.cloned.1.call-update) | async-done | bytes 98320
  250.2 1.6 pad_maximum_fusion
Async XLA Ops:
  6.5 167.3 %reduce-scatter.7.cloned.1.call-start = ((), (), s32[]{:S(2)}) async-start(), calls=%async_computation.2 | async-start | bytes 10027008
  34.0 5.9 %copy-start.1 = (f32[1024,1]{1,0:T(8,128)}, f32[1024,1]{1,0:T(8,128)S(1)}, u32[]{:S(2)}) copy-start(f32[1024,1]{1,0:T(8,128)S(1)} %convert_multiply_fusion.coef_ref) | copy-start | bytes 12292
  39.8 21.2 %collective-permute-start.3 = (f32[16,96,640]{2,1,0:T(8,128)}, f32[16,96,640]{2,1,0:T(8,128)}, u32[]{:S(2)}, u32[]{:S(2)}) collective-permute-start(f32[16,96,640]{2,1,0:T(8,128)} %shard_map.76), channel_id=1, source_target_pairs={{0,1},{1,0},{2,3},{3,2},{4,5},{5,4},{6,7},{7,6},{8,9},{9,8},{10,11... | collective-permute-start | bytes 11796488 | tf_op jit(solution)/shard_map/ppermute | solution.py:175
  39.8 1.0 copy-start.2
  46.6 21.9 %collective-permute-start.2 = (f32[16,96,640]{2,1,0:T(8,128)}, f32[16,96,640]{2,1,0:T(8,128)}, u32[]{:S(2)}, u32[]{:S(2)}) collective-permute-start(f32[16,96,640]{2,1,0:T(8,128)} %shard_map.75), channel_id=1, source_target_pairs={{0,1},{1,0},{2,3},{3,2},{4,5},{5,4},{6,7},{7,6},{8,9},{9,8},{10,11... | collective-permute-start | bytes 11796488 | tf_op jit(solution)/shard_map/ppermute | solution.py:175
  47.1 1.0 copy-start.3
  53.8 21.0 %collective-permute-start.1 = (f32[16,96,640]{2,1,0:T(8,128)}, f32[16,96,640]{2,1,0:T(8,128)}, u32[]{:S(2)}, u32[]{:S(2)}) collective-permute-start(f32[16,96,640]{2,1,0:T(8,128)} %shard_map.74), channel_id=1, source_target_pairs={{0,1},{1,0},{2,3},{3,2},{4,5},{5,4},{6,7},{7,6},{8,9},{9,8},{10,11... | collective-permute-start | bytes 11796488 | tf_op jit(solution)/shard_map/ppermute | solution.py:175
  53.8 1.0 copy-start.4
  60.5 20.5 %collective-permute-start = (f32[16,96,640]{2,1,0:T(8,128)}, f32[16,96,640]{2,1,0:T(8,128)}, u32[]{:S(2)}, u32[]{:S(2)}) collective-permute-start(f32[16,96,640]{2,1,0:T(8,128)} %shard_map.73), channel_id=1, source_target_pairs={{0,1},{1,0},{2,3},{3,2},{4,5},{5,4},{6,7},{7,6},{8,9},{9,8},{10,11... | collective-permute-start | bytes 11796488 | tf_op jit(solution)/shard_map/ppermute | solution.py:175
  61.1 1.0 copy-start.5
  87.4 162.8 %reduce-scatter.9.cloned.1.call-start = ((), (), s32[]{:S(2)}) async-start(), calls=%async_computation.3 | async-start | bytes 1671168
  87.4 2.8 %copy-start = (f32[4,16,96,256]{3,2,1,0:T(8,128)S(1)}, f32[4,16,96,256]{3,2,1,0:T(8,128)}, u32[]{:S(2)}) copy-start(f32[4,16,96,256]{3,2,1,0:T(8,128)} %get-tuple-element.20.x_ref) | copy-start | bytes 18874372
  173.9 1.1 copy-start.6
Sparse Core Ops, SparseCore 0:
  87.5 86.3 reduce-scatter.6
  177.4 72.6 reduce-scatter.8

commit v7 on v5

--- a/solution.py
+++ b/solution.py
@@ -129,6 +129,55 @@
                                       bytes_accessed=3 * n * r * c * 4),
     )(x)
 
+def ctx_sum(vals, n_z, n_core):
+    n = n_z * n_core
+
+    def kernel(v_ref, out_ref, recv, send_sem, recv_sem):
+        me = lax.axis_index("z") * n_core + lax.axis_index("core")
+
+        def peer_of(p):
+            return {"z": p // n_core, "core": p % n_core}
+
+        barrier = pltpu.get_barrier_semaphore()
+        for d in range(1, n):
+            pl.semaphore_signal(barrier, inc=1, device_id=peer_of(lax.rem(me + d, n)),
+                                device_id_type=pl.DeviceIdType.MESH)
+        pl.semaphore_wait(barrier, n - 1)
+        copies = []
+        for d in range(1, n):
+            cp = pltpu.make_async_remote_copy(
+                src_ref=v_ref, dst_ref=recv.at[me],
+                send_sem=send_sem.at[d], recv_sem=recv_sem.at[me],
+                device_id=peer_of(lax.rem(me + d, n)), device_id_type=pl.DeviceIdType.MESH)
+            cp.start()
+            copies.append(cp)
+        recv[me] = v_ref[...]
+        for d in range(1, n):
+            src = lax.rem(me + n - d, n)
+            pltpu.make_async_remote_copy(
+                src_ref=v_ref, dst_ref=recv.at[src],
+                send_sem=send_sem.at[d], recv_sem=recv_sem.at[src],
+                device_id=peer_of(src), device_id_type=pl.DeviceIdType.MESH).wait_recv()
+        total = recv[0]
+        for p in range(1, n):
+            total = total + recv[p]
+        for cp in copies:
+            cp.wait_send()
+        out_ref[...] = total
+
+    return pl.pallas_call(
+        kernel,
+        out_shape=jax.ShapeDtypeStruct(vals.shape, jnp.float32),
+        in_specs=[pl.BlockSpec(memory_space=pltpu.VMEM)],
+        out_specs=pl.BlockSpec(memory_space=pltpu.VMEM),
+        scratch_shapes=[
+            pltpu.VMEM((n,) + vals.shape, jnp.float32),
+            pltpu.SemaphoreType.DMA((n,)),
+            pltpu.SemaphoreType.DMA((n,)),
+        ],
+        compiler_params=pltpu.CompilerParams(collective_id=1, has_side_effects=True),
+    )(vals)
+
 
 def shards(hidden_acts, out_grad, old_logp, new_logp, roll_len, resp_mask, advantage):
     n_dp = lax.axis_size("dp")
@@ -138,9 +187,11 @@
     ctx = lax.axis_index("z") * n_core + lax.axis_index("core")
     places = ctx * width + jnp.arange(width, dtype=jnp.int32)
     masked = jnp.where(places < roll_len[0], resp_mask[0], 0).astype(jnp.float32)
-    gap_sum, count = lax.psum(
-        (jnp.sum((new_logp[0] - old_logp[0]) * masked), jnp.sum(masked)), ("z", "core")
-    )
+    lanes = jnp.arange(128, dtype=jnp.int32)[None, :]
+    local = jnp.where(lanes == 0, jnp.sum((new_logp[0] - old_logp[0]) * masked),
+                      jnp.where(lanes == 1, jnp.sum(masked), 0.0))
+    summed = ctx_sum(jnp.broadcast_to(local, (8, 128)).astype(jnp.float32), n_z, n_core)
+    gap_sum, count = summed[0, 0], summed[0, 1]
     adv = advantage[0, 0]
     length = jnp.maximum(count, 1.0)
     seq_ratio = jnp.exp(gap_sum / length)

time: 218 us -> 215 us (0.986)
  blocking collectives: 16.6 us -> 0 us
  Pallas kernels: 65.3 us -> 73.9 us
    psum x1 -> x0, blocking collectives: 16.6 us -> none  [shards(): lax.psum((jnp.sum((new_logp[0] - old_logp[0]) * masked), jnp.sum(masked))...]
    pallas_call x0 -> x1, Pallas kernels: none -> 8.7 us  [ctx_sum(): pl.pallas_call(kernel, out_shape=jax.ShapeDtypeStruct(vals.shape, jnp.flo...]
where the time goes in v7:
time: 215 us; the launch traced here: 214 us
  waiting for transfers between devices  106 us (49%)
  Pallas kernels  73.9 us (34%)
  between operations  16.2 us (8%)
  local copies, waits for them, and re-layouts  12.7 us (6%)
  other arithmetic  4.36 us (2%)
    unnamed x2, waiting for transfers between devices  106 us
    pallas_call x8, Pallas kernels, block_matmul(): pl.pallas_call(kernel, grid_spec=grid_spec, out_shape=out_shape, input_ou...  48.1 us
    pallas_call x1, Pallas kernels, z_reduce_scatter(): pl.pallas_call(kernel, out_shape=jax.ShapeDtypeStruct((r, c), jnp.float32...  17 us
    unnamed x12, local copies, waits for them, and re-layouts  9 us
    pallas_call x1, Pallas kernels, ctx_sum(): pl.pallas_call(kernel, out_shape=jax.ShapeDtypeStruct(vals.shape, jnp.flo...  8.7 us
  transfers between devices with their start and end apart: 5, of which 1 were waited for; matrix products, arithmetic and copies ran while one was open for 0% of the time, Pallas kernels for 17%

profile of v7, /device:TPU:0, one launch (start us, length us, event | category | flops | bytes accessed | tf_op | source)
XLA Modules:
  0.0 214.2 jit_solution(11867922534173591109)
XLA Ops:
  6.5 0.0 reduce-scatter.4.cloned.1.call-start
  7.2 0.7 sub.12
  7.9 1.3 multiply_reduce_fusion
  9.2 1.2 compare_select_fusion.1
  10.4 0.6 broadcast_in_dim.30.v_ref
  11.0 8.7 %shard_map.73 = f32[8,128]{1,0:T(8,128)} custom-call(f32[8,128]{1,0:T(8,128)} %broadcast_in_dim.30.v_ref), custom_call_target="tpu_custom_call" | custom-call | tf_op jit(solution)/shard_map/pallas_call | solution.py:168
  19.7 1.4 fusion.1
  23.2 1.7 copy.14
  24.9 3.2 %copy.15 = bf16[1024,1536]{0,1:T(8,128)(2,1)S(1)} copy(bf16[1024,1536]{1,0:T(8,128)(2,1)} %param.7) | data formatting | bytes 6291456 | tf_op args[0]
  28.0 1.2 convert_multiply_fusion.coef_ref
  29.2 0.0 copy-start
  29.2 5.8 %shard_map.77 = f32[16,96,640]{2,1,0:T(8,128)} custom-call(s32[1]{0:T(128)} %bitcast.16.col_ref, f32[1024,1]{1,0:T(8,128)S(1)} %convert_multiply_fusion.coef_ref, bf16[1024,5120]{1,0:T(8,128)(2,1)} %grad_ref.15, bf16[1536,1024]{1,0:T(8,128)(2,1)S(1)} %bitcast.21), custom_call_target="tpu_custom_call" | custom-call | flops 2013265920 | bytes 8388608 | tf_op jit(solution)/shard_map/pallas_call | solution.py:71
  35.0 0.0 copy-done
  35.0 0.1 collective-permute-start.3
  35.2 0.0 copy-start.1
  35.2 1.0 copy-done.1
  36.2 5.6 %shard_map.76 = f32[16,96,640]{2,1,0:T(8,128)} custom-call(s32[1]{0:T(128)} %bitcast.14.col_ref, f32[1024,1]{1,0:T(8,128)S(1)} %copy-done.1, bf16[1024,5120]{1,0:T(8,128)(2,1)} %grad_ref.15, bf16[1536,1024]{1,0:T(8,128)(2,1)S(1)} %bitcast.22), custom_call_target="tpu_custom_call" | custom-call | flops 2013265920 | bytes 8388608 | tf_op jit(solution)/shard_map/pallas_call | solution.py:71
  41.8 0.4 collective-permute-start.2
  42.2 0.0 copy-start.2
  42.2 1.0 copy-done.2
  43.3 5.7 %shard_map.75 = f32[16,96,640]{2,1,0:T(8,128)} custom-call(s32[1]{0:T(128)} %bitcast.12.col_ref, f32[1024,1]{1,0:T(8,128)S(1)} %copy-done.2, bf16[1024,5120]{1,0:T(8,128)(2,1)} %grad_ref.15, bf16[1536,1024]{1,0:T(8,128)(2,1)S(1)} %bitcast.23), custom_call_target="tpu_custom_call" | custom-call | flops 2013265920 | bytes 8388608 | tf_op jit(solution)/shard_map/pallas_call | solution.py:71
  49.0 0.1 collective-permute-start.1
  49.1 0.0 copy-start.3
  49.1 1.0 copy-done.3
  50.1 5.7 %shard_map.74 = f32[16,96,640]{2,1,0:T(8,128)} custom-call(s32[1]{0:T(128)} %bitcast.10.col_ref, f32[1024,1]{1,0:T(8,128)S(1)} %copy-done.3, bf16[1024,5120]{1,0:T(8,128)(2,1)} %grad_ref.15, bf16[1536,1024]{1,0:T(8,128)(2,1)S(1)} %bitcast.24), custom_call_target="tpu_custom_call" | custom-call | flops 2013265920 | bytes 8388608 | tf_op jit(solution)/shard_map/pallas_call | solution.py:71
  55.8 0.4 collective-permute-start
  56.2 0.0 collective-permute-done.3.rest_0_
  56.2 0.0 copy-start.4
  56.2 1.0 copy-done.4
  57.3 6.3 %shard_map.78.rest_1_ = f32[16,4,96,640]{3,2,1,0:T(8,128)} custom-call(s32[1]{0:T(128)} %bitcast.15.col_ref, f32[1024,1]{1,0:T(8,128)S(1)} %copy-done.4, bf16[1024,5120]{1,0:T(8,128)(2,1)} %grad_ref.15, bf16[1536,1024]{1,0:T(8,128)(2,1)S(1)} %bitcast.25, f32[16,96,640]{2,1,0:T(8,128)} %collective-permute-done.3.rest_0_), custom_call_target="tpu_custom_call" | custom-call | flops 2013265920 | bytes 12320768 | tf_op jit(solution)/shard_map/pallas_call | solution.py:71
  63.6 0.0 collective-permute-done.2.rest_0_
  63.6 6.3 %shard_map.79.rest_1_ = f32[16,4,96,640]{3,2,1,0:T(8,128)} custom-call(s32[1]{0:T(128)} %bitcast.13.col_ref, f32[1024,1]{1,0:T(8,128)S(1)} %copy-done.4, bf16[1024,5120]{1,0:T(8,128)(2,1)} %grad_ref.15, bf16[1536,1024]{1,0:T(8,128)(2,1)S(1)} %bitcast.26, f32[16,96,640]{2,1,0:T(8,128)} %collective-permute-done.2.rest_0_, ...), custom_call_target="tpu_custom_call", output_to_operand_aliasing={{}: (5, {})} | custom-call | flops 2013265920 | bytes 12320768 | tf_op jit(solution)/shard_map/pallas_call | solution.py:71
  69.9 0.0 collective-permute-done.1.rest_0_
  69.9 6.3 %shard_map.80.rest_1_ = f32[16,4,96,640]{3,2,1,0:T(8,128)} custom-call(s32[1]{0:T(128)} %bitcast.11.col_ref, f32[1024,1]{1,0:T(8,128)S(1)} %copy-done.4, bf16[1024,5120]{1,0:T(8,128)(2,1)} %grad_ref.15, bf16[1536,1024]{1,0:T(8,128)(2,1)S(1)} %bitcast.27, f32[16,96,640]{2,1,0:T(8,128)} %collective-permute-done.1.rest_0_, ...), custom_call_target="tpu_custom_call", output_to_operand_aliasing={{}: (5, {})} | custom-call | flops 2013265920 | bytes 12320768 | tf_op jit(solution)/shard_map/pallas_call | solution.py:71
  76.2 0.0 collective-permute-done.rest_0_
  76.2 6.3 %shard_map.81 = f32[16,4,96,640]{3,2,1,0:T(8,128)} custom-call(s32[1]{0:T(128)} %bitcast.col_ref, f32[1024,1]{1,0:T(8,128)S(1)} %copy-done.4, bf16[1024,5120]{1,0:T(8,128)(2,1)} %grad_ref.15, bf16[1536,1024]{1,0:T(8,128)(2,1)S(1)} %bitcast.28, f32[16,96,640]{2,1,0:T(8,128)} %collective-permute-done.rest_0_, ...), custom_call_target="tpu_custom_call", output_to_operand_aliasing={{}: (5, {})} | custom-call | flops 2013265920 | bytes 12320768 | tf_op jit(solution)/shard_map/pallas_call | solution.py:71
  82.5 0.0 reduce-scatter.4.cloned.1.call-update
  82.6 106.0 %reduce-scatter.4.cloned.1.call-done = f32[1,4,96,640]{3,2,1,0:T(8,128)} async-done(((f32[16,4,96,640]{3,2,1,0:T(8,128)}), f32[1,4,96,640]{3,2,1,0:T(8,128)}) %reduce-scatter.4.cloned.1.call-update) | async-done | bytes 983056
  188.6 17.0 %shard_map.82 = f32[96,640]{1,0:T(8,128)} custom-call(f32[4,96,640]{2,1,0:T(8,128)} %bitcast.29), custom_call_target="tpu_custom_call" | custom-call | flops 245760 | bytes 2949120 | tf_op jit(solution)/shard_map/pallas_call | solution.py:117
  205.7 1.7 copy.22
Async XLA Ops:
  6.5 182.1 %reduce-scatter.4.cloned.1.call-start = ((), (), s32[]{:S(2)}) async-start(), calls=%async_computation.1 | async-start | bytes 16711680
  29.2 5.8 %copy-start = (f32[1024,1]{1,0:T(8,128)}, f32[1024,1]{1,0:T(8,128)S(1)}, u32[]{:S(2)}) copy-start(f32[1024,1]{1,0:T(8,128)S(1)} %convert_multiply_fusion.coef_ref) | copy-start | bytes 12292
  35.0 21.2 %collective-permute-start.3 = (f32[16,96,640]{2,1,0:T(8,128)}, f32[16,96,640]{2,1,0:T(8,128)}, u32[]{:S(2)}, u32[]{:S(2)}) collective-permute-start(f32[16,96,640]{2,1,0:T(8,128)} %shard_map.77), channel_id=1, source_target_pairs={{0,1},{1,0},{2,3},{3,2},{4,5},{5,4},{6,7},{7,6},{8,9},{9,8},{10,11... | collective-permute-start | bytes 11796488 | tf_op jit(solution)/shard_map/ppermute | solution.py:214
  35.2 1.0 copy-start.1
  41.8 21.7 %collective-permute-start.2 = (f32[16,96,640]{2,1,0:T(8,128)}, f32[16,96,640]{2,1,0:T(8,128)}, u32[]{:S(2)}, u32[]{:S(2)}) collective-permute-start(f32[16,96,640]{2,1,0:T(8,128)} %shard_map.76), channel_id=1, source_target_pairs={{0,1},{1,0},{2,3},{3,2},{4,5},{5,4},{6,7},{7,6},{8,9},{9,8},{10,11... | collective-permute-start | bytes 11796488 | tf_op jit(solution)/shard_map/ppermute | solution.py:214
  42.2 1.0 copy-start.2
  49.0 21.0 %collective-permute-start.1 = (f32[16,96,640]{2,1,0:T(8,128)}, f32[16,96,640]{2,1,0:T(8,128)}, u32[]{:S(2)}, u32[]{:S(2)}) collective-permute-start(f32[16,96,640]{2,1,0:T(8,128)} %shard_map.75), channel_id=1, source_target_pairs={{0,1},{1,0},{2,3},{3,2},{4,5},{5,4},{6,7},{7,6},{8,9},{9,8},{10,11... | collective-permute-start | bytes 11796488 | tf_op jit(solution)/shard_map/ppermute | solution.py:214
  49.1 1.0 copy-start.3
  55.8 20.4 %collective-permute-start = (f32[16,96,640]{2,1,0:T(8,128)}, f32[16,96,640]{2,1,0:T(8,128)}, u32[]{:S(2)}, u32[]{:S(2)}) collective-permute-start(f32[16,96,640]{2,1,0:T(8,128)} %shard_map.74), channel_id=1, source_target_pairs={{0,1},{1,0},{2,3},{3,2},{4,5},{5,4},{6,7},{7,6},{8,9},{9,8},{10,11... | collective-permute-start | bytes 11796488 | tf_op jit(solution)/shard_map/ppermute | solution.py:214
  56.2 1.0 copy-start.4
Sparse Core Ops, SparseCore 0:
  82.7 105.8 reduce-scatter.3

commit v8 on v7

--- a/solution.py
+++ b/solution.py
@@ -10,6 +10,7 @@
 CLIP_LOW = 0.0003
 CLIP_HIGH = 0.0004
 ROW_TILE = 768
+Z_FIRST = 128
 
 
 def block_matmul(col, coef, grad, hid_t, n_dp, width, addend=None, into=None, slot=0, n_slots=1):
@@ -18,13 +19,18 @@
     per_tile = ROW_TILE // rows
     n_tiles = hb // ROW_TILE
     grouped = n_slots > 1
+    keep = width - Z_FIRST
 
     def kernel(col_ref, coef_ref, grad_ref, hid_ref, *rest):
         rest = list(rest)
         add_ref = rest.pop(0) if addend is not None else None
         if into is not None:
             rest.pop(0)
-        out_ref, scaled_ref = rest
+            rest.pop(0)
+        if grouped:
+            out_ref, zout_ref, scaled_ref = rest
+        else:
+            out_ref, scaled_ref = rest
 
         @pl.when(pl.program_id(0) == 0)
         def _():
@@ -36,7 +42,8 @@
             if add_ref is not None:
                 part = part + add_ref[k]
             if grouped:
-                out_ref[k, 0] = part
+                out_ref[k, 0] = part[:, :keep]
+                zout_ref[0, k] = part[:, keep:]
             else:
                 out_ref[k] = part
 
@@ -51,12 +58,14 @@
         args.append(addend)
     aliases = {}
     if into is not None:
-        in_specs.append(pl.BlockSpec(memory_space=pl.ANY))
-        aliases = {len(args): 0}
-        args.append(into)
+        in_specs += [pl.BlockSpec(memory_space=pl.ANY)] * 2
+        aliases = {len(args): 0, len(args) + 1: 1}
+        args += list(into)
     if grouped:
-        out_shape = jax.ShapeDtypeStruct((n_dp, n_slots, rows, width), jnp.float32)
-        out_spec = pl.BlockSpec((per_tile, 1, rows, width), lambda i, c: (i, slot, 0, 0))
+        out_shape = (jax.ShapeDtypeStruct((n_dp, n_slots, rows, keep), jnp.float32),
+                     jax.ShapeDtypeStruct((n_slots, n_dp, rows, Z_FIRST), jnp.float32))
+        out_spec = (pl.BlockSpec((per_tile, 1, rows, keep), lambda i, c: (i, slot, 0, 0)),
+                    pl.BlockSpec((1, per_tile, rows, Z_FIRST), lambda i, c: (slot, i, 0, 0)))
     else:
         out_shape = jax.ShapeDtypeStruct((n_dp, rows, width), jnp.float32)
         out_spec = pl.BlockSpec((per_tile, rows, width), lambda i, c: (i, 0, 0))
@@ -81,8 +90,11 @@
     )(*args)
 
 
-def z_reduce_scatter(x, axis, n):
-    _, r, c = x.shape
+def z_reduce_scatter(x, axis, n, cid):
+    rest_shape = x.shape[1:]
+    size = 1
+    for s in x.shape:
+        size *= s
 
     def kernel(x_ref, out_ref, recv, send_sem, recv_sem):
         me = lax.axis_index(axis)
@@ -116,17 +128,17 @@
 
     return pl.pallas_call(
         kernel,
-        out_shape=jax.ShapeDtypeStruct((r, c), jnp.float32),
+        out_shape=jax.ShapeDtypeStruct(rest_shape, jnp.float32),
         in_specs=[pl.BlockSpec(memory_space=pltpu.VMEM)],
         out_specs=pl.BlockSpec(memory_space=pltpu.VMEM),
         scratch_shapes=[
-            pltpu.VMEM((n, r, c), jnp.float32),
+            pltpu.VMEM(x.shape, jnp.float32),
             pltpu.SemaphoreType.DMA((n,)),
             pltpu.SemaphoreType.DMA((n,)),
         ],
-        compiler_params=pltpu.CompilerParams(collective_id=0, has_side_effects=True),
-        cost_estimate=pl.CostEstimate(flops=n * r * c, transcendentals=0,
-                                      bytes_accessed=3 * n * r * c * 4),
+        compiler_params=pltpu.CompilerParams(
+            collective_id=cid, has_side_effects=True, vmem_limit_bytes=40 * 1024 * 1024),
+        cost_estimate=pl.CostEstimate(flops=size, transcendentals=0, bytes_accessed=3 * size * 4),
     )(x)
 
 def ctx_sum(vals, n_z, n_core):
@@ -216,8 +228,12 @@
     for k in range(n_z):
         chip = block_matmul(col_index(k, core), token_coef, out_grad, hid_t, n_dp, col,
                             addend=got[k], into=chip, slot=k, n_slots=n_z)
-    rows = lax.psum_scatter(chip, "dp", scatter_dimension=0, tiled=True)[0]
-    return z_reduce_scatter(rows, "z", n_z)
+    dp_first, z_first = chip
+    rows = lax.psum_scatter(dp_first, "dp", scatter_dimension=0, tiled=True)[0]
+    late = z_reduce_scatter(z_first, "z", n_z, 0)
+    late = z_reduce_scatter(late, "dp", n_dp, 2)
+    early = z_reduce_scatter(rows, "z", n_z, 3)
+    return jnp.concatenate([early, late], axis=1)
 
 
 def solution(mesh):

time: 215 us -> 212 us (0.986)
  waiting for transfers between devices: 106 us -> 45.4 us
  Pallas kernels: 73.9 us -> 131 us
    unnamed x2, waiting for transfers between devices: 106 us -> 45.4 us
    pallas_call x1 -> x3, Pallas kernels: 17 us -> 72.8 us  [z_reduce_scatter(): pl.pallas_call(kernel, out_shape=jax.ShapeDtypeStruct(rest_shape, jnp.flo...]
    unnamed x12 -> x15, local copies, waits for them, and re-layouts: 9 us -> 8.48 us
  transfers between devices with their start and end apart: 5 -> 5, of which waited for: 1 -> 1; matrix products, arithmetic and copies ran while one was open for 0% -> 0% of each run, Pallas kernels for 17% -> 46%
where the time goes in v8:
time: 212 us; the launch traced here: 211 us
  Pallas kernels  131 us (62%)
  waiting for transfers between devices  45.4 us (21%)
  between operations  16.2 us (8%)
  local copies, waits for them, and re-layouts  12.1 us (6%)
  other arithmetic  5.58 us (3%)
    pallas_call x3, Pallas kernels, z_reduce_scatter(): pl.pallas_call(kernel, out_shape=jax.ShapeDtypeStruct(rest_shape, jnp.flo...  72.8 us
    pallas_call x8, Pallas kernels, block_matmul(): pl.pallas_call(kernel, grid_spec=grid_spec, out_shape=out_shape, input_ou...  49.6 us
    unnamed x2, waiting for transfers between devices  45.4 us
    pallas_call x1, Pallas kernels, ctx_sum(): pl.pallas_call(kernel, out_shape=jax.ShapeDtypeStruct(vals.shape, jnp.flo...  8.69 us
    unnamed x15, local copies, waits for them, and re-layouts  8.48 us
  transfers between devices with their start and end apart: 5, of which 1 were waited for; matrix products, arithmetic and copies ran while one was open for 0% of the time, Pallas kernels for 46%

profile of v8, /device:TPU:0, one launch (start us, length us, event | category | flops | bytes accessed | tf_op | source)
XLA Modules:
  0.0 211.3 jit_solution(8934111631909734514)
XLA Ops:
  6.5 0.0 reduce-scatter.4.cloned.1.call-start
  7.2 0.7 sub.12
  7.9 1.4 multiply_reduce_fusion
  9.3 1.3 compare_select_fusion.1
  10.5 0.6 broadcast_in_dim.30.v_ref
  11.1 8.7 %shard_map.73 = f32[8,128]{1,0:T(8,128)} custom-call(f32[8,128]{1,0:T(8,128)} %broadcast_in_dim.30.v_ref), custom_call_target="tpu_custom_call" | custom-call | tf_op jit(solution)/shard_map/pallas_call | solution.py:180
  19.8 1.3 fusion.1
  23.2 1.7 copy.17
  24.9 3.2 %copy.18 = bf16[1024,1536]{0,1:T(8,128)(2,1)S(1)} copy(bf16[1024,1536]{1,0:T(8,128)(2,1)} %param.7) | data formatting | bytes 6291456 | tf_op args[0]
  28.1 0.0 copy-start
  28.1 1.5 convert_multiply_fusion.coef_ref
  29.6 0.0 copy-start.1
  29.6 5.8 %shard_map.77 = f32[16,96,640]{2,1,0:T(8,128)} custom-call(s32[1]{0:T(128)} %bitcast.16.col_ref, f32[1024,1]{1,0:T(8,128)S(1)} %convert_multiply_fusion.coef_ref, bf16[1024,5120]{1,0:T(8,128)(2,1)} %grad_ref.15, bf16[1536,1024]{1,0:T(8,128)(2,1)S(1)} %bitcast.21), custom_call_target="tpu_custom_call" | custom-call | flops 2013265920 | bytes 8388608 | tf_op jit(solution)/shard_map/pallas_call | solution.py:80
  35.5 0.0 copy-done.1
  35.5 0.1 collective-permute-start.3
  35.6 0.0 copy-start.2
  35.6 1.0 copy-done.2
  36.6 5.7 %shard_map.76 = f32[16,96,640]{2,1,0:T(8,128)} custom-call(s32[1]{0:T(128)} %bitcast.14.col_ref, f32[1024,1]{1,0:T(8,128)S(1)} %copy-done.2, bf16[1024,5120]{1,0:T(8,128)(2,1)} %grad_ref.15, bf16[1536,1024]{1,0:T(8,128)(2,1)S(1)} %bitcast.22), custom_call_target="tpu_custom_call" | custom-call | flops 2013265920 | bytes 8388608 | tf_op jit(solution)/shard_map/pallas_call | solution.py:80
  42.3 0.4 collective-permute-start.2
  42.7 0.0 copy-start.3
  42.7 1.0 copy-done.3
  43.8 5.6 %shard_map.75 = f32[16,96,640]{2,1,0:T(8,128)} custom-call(s32[1]{0:T(128)} %bitcast.12.col_ref, f32[1024,1]{1,0:T(8,128)S(1)} %copy-done.3, bf16[1024,5120]{1,0:T(8,128)(2,1)} %grad_ref.15, bf16[1536,1024]{1,0:T(8,128)(2,1)S(1)} %bitcast.23), custom_call_target="tpu_custom_call" | custom-call | flops 2013265920 | bytes 8388608 | tf_op jit(solution)/shard_map/pallas_call | solution.py:80
  49.4 0.1 collective-permute-start.1
  49.5 0.0 copy-done
  49.5 0.0 copy-start.4
  49.5 1.0 copy-done.4
  50.6 5.7 %shard_map.74 = f32[16,96,640]{2,1,0:T(8,128)} custom-call(s32[1]{0:T(128)} %bitcast.10.col_ref, f32[1024,1]{1,0:T(8,128)S(1)} %copy-done.4, bf16[1024,5120]{1,0:T(8,128)(2,1)} %grad_ref.15, bf16[1536,1024]{1,0:T(8,128)(2,1)S(1)} %bitcast.24), custom_call_target="tpu_custom_call" | custom-call | flops 2013265920 | bytes 8388608 | tf_op jit(solution)/shard_map/pallas_call | solution.py:80
  56.2 0.4 collective-permute-start
  56.6 0.0 collective-permute-done.3.rest_0_
  56.6 0.0 copy-start.5
  56.6 1.0 copy-done.5
  57.7 6.6 %shard_map.78 = (f32[16,4,96,512]{3,2,1,0:T(8,128)}, f32[4,16,96,128]{3,2,1,0:T(8,128)S(1)}) custom-call(s32[1]{0:T(128)} %bitcast.15.col_ref, f32[1024,1]{1,0:T(8,128)S(1)} %copy-done.5, bf16[1024,5120]{1,0:T(8,128)(2,1)} %grad_ref.15, bf16[1536,1024]{1,0:T(8,128)(2,1)} %bitcast.25, f32[16,96,640]{2,1,0:T(8,128)} %collective-permute-done.3.rest_0_), custom_call_target="tpu_custom_call" | custom-call | flops 2013265920 | bytes 12320768 | tf_op jit(solution)/shard_map/pallas_call | solution.py:80
  64.3 0.0 collective-permute-done.2.rest_0_
  64.3 6.7 %shard_map.79 = (f32[16,4,96,512]{3,2,1,0:T(8,128)}, f32[4,16,96,128]{3,2,1,0:T(8,128)S(1)}) custom-call(s32[1]{0:T(128)} %bitcast.13.col_ref, f32[1024,1]{1,0:T(8,128)S(1)} %copy-done.5, bf16[1024,5120]{1,0:T(8,128)(2,1)} %grad_ref.15, bf16[1536,1024]{1,0:T(8,128)(2,1)} %bitcast.26, ...), custom_call_target="tpu_custom_call", output_to_operand_aliasing={{0}: (5, {}), {1}: (6, {})} | custom-call | flops 2013265920 | bytes 12320768 | tf_op jit(solution)/shard_map/pallas_call | solution.py:80
  71.1 0.0 collective-permute-done.1.rest_0_
  71.1 6.7 %shard_map.80 = (f32[16,4,96,512]{3,2,1,0:T(8,128)}, f32[4,16,96,128]{3,2,1,0:T(8,128)S(1)}) custom-call(s32[1]{0:T(128)} %bitcast.11.col_ref, f32[1024,1]{1,0:T(8,128)S(1)} %copy-done.5, bf16[1024,5120]{1,0:T(8,128)(2,1)} %grad_ref.15, bf16[1536,1024]{1,0:T(8,128)(2,1)} %bitcast.27, ...), custom_call_target="tpu_custom_call", output_to_operand_aliasing={{0}: (5, {}), {1}: (6, {})} | custom-call | flops 2013265920 | bytes 12320768 | tf_op jit(solution)/shard_map/pallas_call | solution.py:80
  77.7 0.0 collective-permute-done.rest_0_
  77.7 6.7 %shard_map.81 = (f32[16,4,96,512]{3,2,1,0:T(8,128)}, f32[4,16,96,128]{3,2,1,0:T(8,128)S(1)}) custom-call(s32[1]{0:T(128)} %bitcast.col_ref, f32[1024,1]{1,0:T(8,128)S(1)} %copy-done.5, bf16[1024,5120]{1,0:T(8,128)(2,1)} %grad_ref.15, bf16[1536,1024]{1,0:T(8,128)(2,1)} %bitcast.28, ...), custom_call_target="tpu_custom_call", output_to_operand_aliasing={{0}: (5, {}), {1}: (6, {})} | custom-call | flops 2013265920 | bytes 12320768 | tf_op jit(solution)/shard_map/pallas_call | solution.py:80
  84.4 0.0 reduce-scatter.4.cloned.1.call-update
  84.5 38.2 %shard_map.83.x_ref = f32[16,96,128]{2,1,0:T(8,128)S(1)} custom-call(f32[4,16,96,128]{3,2,1,0:T(8,128)S(1)} %get-tuple-element.20.x_ref), custom_call_target="tpu_custom_call" | custom-call | flops 786432 | bytes 9437184 | tf_op jit(solution)/shard_map/pallas_call | solution.py:129
  122.7 21.4 %shard_map.84 = f32[96,128]{1,0:T(8,128)S(1)} custom-call(f32[16,96,128]{2,1,0:T(8,128)S(1)} %shard_map.83.x_ref), custom_call_target="tpu_custom_call" | custom-call | flops 196608 | bytes 2359296 | tf_op jit(solution)/shard_map/pallas_call | solution.py:129
  144.1 45.4 %reduce-scatter.4.cloned.1.call-done = f32[1,4,96,512]{3,2,1,0:T(8,128)} async-done(((f32[16,4,96,512]{3,2,1,0:T(8,128)}), f32[1,4,96,512]{3,2,1,0:T(8,128)}) %reduce-scatter.4.cloned.1.call-update) | async-done | bytes 786448
  189.4 0.0 copy-start.6
  189.4 1.1 copy-done.6
  190.5 13.2 %shard_map.82 = f32[96,512]{1,0:T(8,128)S(1)} custom-call(f32[4,96,512]{2,1,0:T(8,128)S(1)} %bitcast.29), custom_call_target="tpu_custom_call" | custom-call | flops 196608 | bytes 2359296 | tf_op jit(solution)/shard_map/pallas_call | solution.py:129
  203.7 0.7 pad_maximum_fusion
Async XLA Ops:
  6.5 182.9 %reduce-scatter.4.cloned.1.call-start = ((), (), s32[]{:S(2)}) async-start(), calls=%async_computation.1 | async-start | bytes 13369344
  28.1 21.4 %copy-start = (bf16[1024,1536]{0,1:T(8,128)(2,1)}, bf16[1024,1536]{0,1:T(8,128)(2,1)S(1)}, u32[]{:S(2)}) copy-start(bf16[1024,1536]{0,1:T(8,128)(2,1)S(1)} %copy.18) | copy-start | bytes 9437188
  29.6 5.9 %copy-start.1 = (f32[1024,1]{1,0:T(8,128)}, f32[1024,1]{1,0:T(8,128)S(1)}, u32[]{:S(2)}) copy-start(f32[1024,1]{1,0:T(8,128)S(1)} %convert_multiply_fusion.coef_ref) | copy-start | bytes 12292
  35.5 21.2 %collective-permute-start.3 = (f32[16,96,640]{2,1,0:T(8,128)}, f32[16,96,640]{2,1,0:T(8,128)}, u32[]{:S(2)}, u32[]{:S(2)}) collective-permute-start(f32[16,96,640]{2,1,0:T(8,128)} %shard_map.77), channel_id=1, source_target_pairs={{0,1},{1,0},{2,3},{3,2},{4,5},{5,4},{6,7},{7,6},{8,9},{9,8},{10,11... | collective-permute-start | bytes 11796488 | tf_op jit(solution)/shard_map/ppermute | solution.py:226
  35.6 1.0 copy-start.2
  42.3 22.0 %collective-permute-start.2 = (f32[16,96,640]{2,1,0:T(8,128)}, f32[16,96,640]{2,1,0:T(8,128)}, u32[]{:S(2)}, u32[]{:S(2)}) collective-permute-start(f32[16,96,640]{2,1,0:T(8,128)} %shard_map.76), channel_id=1, source_target_pairs={{0,1},{1,0},{2,3},{3,2},{4,5},{5,4},{6,7},{7,6},{8,9},{9,8},{10,11... | collective-permute-start | bytes 11796488 | tf_op jit(solution)/shard_map/ppermute | solution.py:226
  42.7 1.0 copy-start.3
  49.4 21.7 %collective-permute-start.1 = (f32[16,96,640]{2,1,0:T(8,128)}, f32[16,96,640]{2,1,0:T(8,128)}, u32[]{:S(2)}, u32[]{:S(2)}) collective-permute-start(f32[16,96,640]{2,1,0:T(8,128)} %shard_map.75), channel_id=1, source_target_pairs={{0,1},{1,0},{2,3},{3,2},{4,5},{5,4},{6,7},{7,6},{8,9},{9,8},{10,11... | collective-permute-start | bytes 11796488 | tf_op jit(solution)/shard_map/ppermute | solution.py:226
  49.5 1.0 copy-start.4
  56.2 21.5 %collective-permute-start = (f32[16,96,640]{2,1,0:T(8,128)}, f32[16,96,640]{2,1,0:T(8,128)}, u32[]{:S(2)}, u32[]{:S(2)}) collective-permute-start(f32[16,96,640]{2,1,0:T(8,128)} %shard_map.74), channel_id=1, source_target_pairs={{0,1},{1,0},{2,3},{3,2},{4,5},{5,4},{6,7},{7,6},{8,9},{9,8},{10,11... | collective-permute-start | bytes 11796488 | tf_op jit(solution)/shard_map/ppermute | solution.py:226
  56.6 1.0 copy-start.5
  189.4 1.1 copy-start.6
Sparse Core Ops, SparseCore 0:
  84.6 104.7 reduce-scatter.3

commit v9 on v8

--- a/solution.py
+++ b/solution.py
@@ -13,39 +13,38 @@
 Z_FIRST = 128
 
 
-def block_matmul(col, coef, grad, hid_t, n_dp, width, addend=None, into=None, slot=0, n_slots=1):
+def block_matmul(col, coef, grad, hid_t, n_dp, width, lo, hi, addend=None, into=None, slot=0,
+                 n_slots=1, z_major=False):
     hb, t = hid_t.shape
     rows = hb // n_dp
     per_tile = ROW_TILE // rows
     n_tiles = hb // ROW_TILE
     grouped = n_slots > 1
-    keep = width - Z_FIRST
+    w = hi - lo
 
     def kernel(col_ref, coef_ref, grad_ref, hid_ref, *rest):
         rest = list(rest)
         add_ref = rest.pop(0) if addend is not None else None
         if into is not None:
             rest.pop(0)
-            rest.pop(0)
-        if grouped:
-            out_ref, zout_ref, scaled_ref = rest
-        else:
-            out_ref, scaled_ref = rest
+        out_ref, scaled_ref = rest
 
         @pl.when(pl.program_id(0) == 0)
         def _():
-            scaled_ref[...] = (coef_ref[...] * grad_ref[...].astype(jnp.float32)).astype(jnp.bfloat16)
+            scaled_ref[...] = (coef_ref[...] * grad_ref[:, lo:hi].astype(jnp.float32)).astype(
+                jnp.bfloat16)
 
         acc = jnp.dot(hid_ref[...], scaled_ref[...], preferred_element_type=jnp.float32)
         for k in range(per_tile):
             part = acc[k * rows:(k + 1) * rows, :]
             if add_ref is not None:
                 part = part + add_ref[k]
-            if grouped:
-                out_ref[k, 0] = part[:, :keep]
-                zout_ref[0, k] = part[:, keep:]
+            if not grouped:
+                out_ref[k] = part
+            elif z_major:
+                out_ref[0, k] = part
             else:
-                out_ref[k] = part
+                out_ref[k, 0] = part
 
     in_specs = [
         pl.BlockSpec((t, 1), lambda i, c: (0, 0)),
@@ -54,29 +53,30 @@
     ]
     args = [col, coef, grad, hid_t]
     if addend is not None:
-        in_specs.append(pl.BlockSpec((per_tile, rows, width), lambda i, c: (i, 0, 0)))
+        in_specs.append(pl.BlockSpec((per_tile, rows, w), lambda i, c: (i, 0, 0)))
         args.append(addend)
     aliases = {}
     if into is not None:
-        in_specs += [pl.BlockSpec(memory_space=pl.ANY)] * 2
-        aliases = {len(args): 0, len(args) + 1: 1}
-        args += list(into)
-    if grouped:
-        out_shape = (jax.ShapeDtypeStruct((n_dp, n_slots, rows, keep), jnp.float32),
-                     jax.ShapeDtypeStruct((n_slots, n_dp, rows, Z_FIRST), jnp.float32))
-        out_spec = (pl.BlockSpec((per_tile, 1, rows, keep), lambda i, c: (i, slot, 0, 0)),
-                    pl.BlockSpec((1, per_tile, rows, Z_FIRST), lambda i, c: (slot, i, 0, 0)))
+        in_specs.append(pl.BlockSpec(memory_space=pl.ANY))
+        aliases = {len(args): 0}
+        args.append(into)
+    if not grouped:
+        out_shape = jax.ShapeDtypeStruct((n_dp, rows, w), jnp.float32)
+        out_spec = pl.BlockSpec((per_tile, rows, w), lambda i, c: (i, 0, 0))
+    elif z_major:
+        out_shape = jax.ShapeDtypeStruct((n_slots, n_dp, rows, w), jnp.float32)
+        out_spec = pl.BlockSpec((1, per_tile, rows, w), lambda i, c: (slot, i, 0, 0))
     else:
-        out_shape = jax.ShapeDtypeStruct((n_dp, rows, width), jnp.float32)
-        out_spec = pl.BlockSpec((per_tile, rows, width), lambda i, c: (i, 0, 0))
+        out_shape = jax.ShapeDtypeStruct((n_dp, n_slots, rows, w), jnp.float32)
+        out_spec = pl.BlockSpec((per_tile, 1, rows, w), lambda i, c: (i, slot, 0, 0))
     grid_spec = pltpu.PrefetchScalarGridSpec(
         num_scalar_prefetch=1,
         grid=(n_tiles,),
         in_specs=in_specs,
         out_specs=out_spec,
-        scratch_shapes=[pltpu.VMEM((t, width), jnp.bfloat16)],
-    )
-    extra = hb * width * 4 if addend is not None else 0
+        scratch_shapes=[pltpu.VMEM((t, w), jnp.bfloat16)],
+    )
+    extra = hb * w * 4 if addend is not None else 0
     return pl.pallas_call(
         kernel,
         grid_spec=grid_spec,
@@ -84,8 +84,8 @@
         input_output_aliases=aliases,
         compiler_params=pltpu.CompilerParams(vmem_limit_bytes=48 * 1024 * 1024),
         cost_estimate=pl.CostEstimate(
-            flops=2 * hb * t * width, transcendentals=0,
-            bytes_accessed=hb * t * 2 + t * width * 2 + hb * width * 4 + extra,
+            flops=2 * hb * t * w, transcendentals=0,
+            bytes_accessed=hb * t * 2 + t * width * 2 + hb * w * 4 + extra,
         ),
     )(*args)
 
@@ -220,16 +220,24 @@
     def col_index(k, which):
         return jnp.reshape(k * n_core + which, (1,)).astype(jnp.int32)
 
-    got = []
-    for k in range(n_z):
-        theirs = block_matmul(col_index(k, 1 - core), token_coef, out_grad, hid_t, n_dp, col)
-        got.append(lax.ppermute(theirs, "core", perm=[(0, 1), (1, 0)]))
-    chip = None
-    for k in range(n_z):
-        chip = block_matmul(col_index(k, core), token_coef, out_grad, hid_t, n_dp, col,
-                            addend=got[k], into=chip, slot=k, n_slots=n_z)
-    dp_first, z_first = chip
+    swap = [(0, 1), (1, 0)]
+
+    def pre_reduced(lo, hi, z_major):
+        got = []
+        for k in range(n_z):
+            theirs = block_matmul(col_index(k, 1 - core), token_coef, out_grad, hid_t, n_dp, col,
+                                  lo, hi)
+            got.append(lax.ppermute(theirs, "core", perm=swap))
+        chip = None
+        for k in range(n_z):
+            chip = block_matmul(col_index(k, core), token_coef, out_grad, hid_t, n_dp, col, lo, hi,
+                                addend=got[k], into=chip, slot=k, n_slots=n_z, z_major=z_major)
+        return chip
+
+    keep = col - Z_FIRST
+    dp_first = pre_reduced(0, keep, False)
     rows = lax.psum_scatter(dp_first, "dp", scatter_dimension=0, tiled=True)[0]
+    z_first = pre_reduced(keep, col, True)
     late = z_reduce_scatter(z_first, "z", n_z, 0)
     late = z_reduce_scatter(late, "dp", n_dp, 2)
     early = z_reduce_scatter(rows, "z", n_z, 3)

time: 212 us -> 193 us (0.910)
  waiting for transfers between devices: 45.4 us -> 13.9 us
  Pallas kernels: 131 us -> 143 us
    unnamed x2, waiting for transfers between devices: 45.4 us -> 13.9 us
    pallas_call x8 -> x16, Pallas kernels: 49.6 us -> 65.5 us  [block_matmul(): pl.pallas_call(kernel, grid_spec=grid_spec, out_shape=out_shape, input_ou...]
    pallas_call x3, Pallas kernels: 72.8 us -> 69.3 us  [z_reduce_scatter(): pl.pallas_call(kernel, out_shape=jax.ShapeDtypeStruct(rest_shape, jnp.flo...]
  transfers between devices with their start and end apart: 5 -> 9, of which waited for: 1 -> 1; matrix products, arithmetic and copies ran while one was open for 0% -> 0% of each run, Pallas kernels for 46% -> 58%
where the time goes in v9:
time: 193 us; the launch traced here: 192 us
  Pallas kernels  143 us (74%)
  between operations  16.2 us (8%)
  waiting for transfers between devices  13.9 us (7%)
  local copies, waits for them, and re-layouts  11.8 us (6%)
  other arithmetic  4.16 us (2%)
  starting transfers between devices  2.5 us (1%)
    pallas_call x3, Pallas kernels, z_reduce_scatter(): pl.pallas_call(kernel, out_shape=jax.ShapeDtypeStruct(rest_shape, jnp.flo...  69.3 us
    pallas_call x16, Pallas kernels, block_matmul(): pl.pallas_call(kernel, grid_spec=grid_spec, out_shape=out_shape, input_ou...  65.5 us
    unnamed x2, waiting for transfers between devices  13.9 us
    unnamed x15, local copies, waits for them, and re-layouts  8.97 us
    pallas_call x1, Pallas kernels, ctx_sum(): pl.pallas_call(kernel, out_shape=jax.ShapeDtypeStruct(vals.shape, jnp.flo...  8.69 us
  transfers between devices with their start and end apart: 9, of which 1 were waited for; matrix products, arithmetic and copies ran while one was open for 0% of the time, Pallas kernels for 58%

profile of v9, /device:TPU:0, one launch (start us, length us, event | category | flops | bytes accessed | tf_op | source)
XLA Modules:
  0.0 192.0 jit_solution(16401398057989543633)
XLA Ops:
  7.2 0.7 sub.7
  7.9 1.4 multiply_reduce_fusion
  9.3 1.3 compare_select_fusion.1
  10.5 0.6 broadcast_in_dim.30.v_ref
  11.1 8.7 %shard_map.73 = f32[8,128]{1,0:T(8,128)} custom-call(f32[8,128]{1,0:T(8,128)} %broadcast_in_dim.30.v_ref), custom_call_target="tpu_custom_call" | custom-call | tf_op jit(solution)/shard_map/pallas_call | solution.py:180
  19.8 1.3 fusion.1
  23.1 0.9 copy.17
  24.0 4.7 %copy.18 = bf16[1024,1536]{0,1:T(8,128)(2,1)} copy(bf16[1024,1536]{1,0:T(8,128)(2,1)} %param.7) | data formatting | bytes 6291456 | tf_op args[0]
  28.7 0.1 convert_multiply_fusion.coef_ref
  28.9 5.4 %shard_map.77 = f32[16,96,512]{2,1,0:T(8,128)} custom-call(s32[1]{0:T(128)} %bitcast.16.col_ref, f32[1024,1]{1,0:T(8,128)S(1)} %convert_multiply_fusion.coef_ref, bf16[1024,5120]{1,0:T(8,128)(2,1)} %grad_ref.31, bf16[1536,1024]{1,0:T(8,128)(2,1)} %bitcast.21), custom_call_target="tpu_custom_call" | custom-call | flops 1610612736 | bytes 7602176 | tf_op jit(solution)/shard_map/pallas_call | solution.py:80
  34.2 0.1 collective-permute-start.3
  34.3 5.2 %shard_map.76 = f32[16,96,512]{2,1,0:T(8,128)} custom-call(s32[1]{0:T(128)} %bitcast.14.col_ref, f32[1024,1]{1,0:T(8,128)S(1)} %convert_multiply_fusion.coef_ref, bf16[1024,5120]{1,0:T(8,128)(2,1)} %grad_ref.31, bf16[1536,1024]{1,0:T(8,128)(2,1)} %bitcast.22), custom_call_target="tpu_custom_call" | custom-call | flops 1610612736 | bytes 7602176 | tf_op jit(solution)/shard_map/pallas_call | solution.py:80
  39.5 0.4 collective-permute-start.2
  39.9 5.1 %shard_map.75 = f32[16,96,512]{2,1,0:T(8,128)} custom-call(s32[1]{0:T(128)} %bitcast.12.col_ref, f32[1024,1]{1,0:T(8,128)S(1)} %convert_multiply_fusion.coef_ref, bf16[1024,5120]{1,0:T(8,128)(2,1)} %grad_ref.31, bf16[1536,1024]{1,0:T(8,128)(2,1)} %bitcast.23), custom_call_target="tpu_custom_call" | custom-call | flops 1610612736 | bytes 7602176 | tf_op jit(solution)/shard_map/pallas_call | solution.py:80
  45.1 0.1 collective-permute-start.1
  45.2 1.0 copy-done.2
  46.2 5.3 %shard_map.74 = f32[16,96,512]{2,1,0:T(8,128)} custom-call(s32[1]{0:T(128)} %bitcast.10.col_ref, f32[1024,1]{1,0:T(8,128)S(1)} %copy-done.2, bf16[1024,5120]{1,0:T(8,128)(2,1)} %grad_ref.31, bf16[1536,1024]{1,0:T(8,128)(2,1)} %bitcast.24), custom_call_target="tpu_custom_call" | custom-call | flops 1610612736 | bytes 7602176 | tf_op jit(solution)/shard_map/pallas_call | solution.py:80
  51.5 0.4 collective-permute-start
  51.9 0.0 collective-permute-done.3.rest_0_
  51.9 1.0 copy-done.3
  53.0 5.2 %shard_map.78.rest_1_ = f32[16,4,96,512]{3,2,1,0:T(8,128)} custom-call(s32[1]{0:T(128)} %bitcast.15.col_ref, f32[1024,1]{1,0:T(8,128)S(1)} %copy-done.3, bf16[1024,5120]{1,0:T(8,128)(2,1)} %grad_ref.31, bf16[1536,1024]{1,0:T(8,128)(2,1)S(1)} %bitcast.29, f32[16,96,512]{2,1,0:T(8,128)} %collective-permute-done.3.rest_0_), custom_call_target="tpu_custom_call" | custom-call | flops 1610612736 | bytes 10747904 | tf_op jit(solution)/shard_map/pallas_call | solution.py:80
  58.1 0.0 collective-permute-done.2.rest_0_
  58.1 5.2 %shard_map.79.rest_1_ = f32[16,4,96,512]{3,2,1,0:T(8,128)} custom-call(s32[1]{0:T(128)} %bitcast.13.col_ref, f32[1024,1]{1,0:T(8,128)S(1)} %copy-done.3, bf16[1024,5120]{1,0:T(8,128)(2,1)} %grad_ref.31, bf16[1536,1024]{1,0:T(8,128)(2,1)S(1)} %bitcast.30, f32[16,96,512]{2,1,0:T(8,128)} %collective-permute-done.2.rest_0_, ...), custom_call_target="tpu_custom_call", output_to_operand_aliasing={{}: (5, {})} | custom-call | flops 1610612736 | bytes 10747904 | tf_op jit(solution)/shard_map/pallas_call | solution.py:80
  63.4 0.0 collective-permute-done.1.rest_0_
  63.4 5.2 %shard_map.80.rest_1_ = f32[16,4,96,512]{3,2,1,0:T(8,128)} custom-call(s32[1]{0:T(128)} %bitcast.11.col_ref, f32[1024,1]{1,0:T(8,128)S(1)} %copy-done.3, bf16[1024,5120]{1,0:T(8,128)(2,1)} %grad_ref.31, bf16[1536,1024]{1,0:T(8,128)(2,1)S(1)} %bitcast.31, f32[16,96,512]{2,1,0:T(8,128)} %collective-permute-done.1.rest_0_, ...), custom_call_target="tpu_custom_call", output_to_operand_aliasing={{}: (5, {})} | custom-call | flops 1610612736 | bytes 10747904 | tf_op jit(solution)/shard_map/pallas_call | solution.py:80
  68.6 5.2 %shard_map.81 = f32[16,4,96,512]{3,2,1,0:T(8,128)} custom-call(s32[1]{0:T(128)} %bitcast.col_ref, f32[1024,1]{1,0:T(8,128)S(1)} %copy-done.3, bf16[1024,5120]{1,0:T(8,128)(2,1)} %grad_ref.31, bf16[1536,1024]{1,0:T(8,128)(2,1)S(1)} %bitcast.32, f32[16,96,512]{2,1,0:T(8,128)} %collective-permute-done.rest_0_, ...), custom_call_target="tpu_custom_call", output_to_operand_aliasing={{}: (5, {})} | custom-call | flops 1610612736 | bytes 10747904 | tf_op jit(solution)/shard_map/pallas_call | solution.py:80
  73.8 0.0 reduce-scatter.4.cloned.1.call-update
  73.9 1.0 copy-done.4
  74.9 2.7 %shard_map.86 = f32[16,96,128]{2,1,0:T(8,128)S(1)} custom-call(s32[1]{0:T(128)} %bitcast.16.col_ref, f32[1024,1]{1,0:T(8,128)S(1)} %copy-done.4, bf16[1024,5120]{1,0:T(8,128)(2,1)} %grad_ref.31, bf16[1536,1024]{1,0:T(8,128)(2,1)S(1)} %bitcast.33), custom_call_target="tpu_custom_call" | custom-call | flops 402653184 | bytes 5242880 | tf_op jit(solution)/shard_map/pallas_call | solution.py:80
  77.6 0.2 collective-permute-start.7
  77.8 2.7 %shard_map.85 = f32[16,96,128]{2,1,0:T(8,128)S(1)} custom-call(s32[1]{0:T(128)} %bitcast.14.col_ref, f32[1024,1]{1,0:T(8,128)S(1)} %copy-done.4, bf16[1024,5120]{1,0:T(8,128)(2,1)} %grad_ref.31, bf16[1536,1024]{1,0:T(8,128)(2,1)S(1)} %bitcast.34), custom_call_target="tpu_custom_call" | custom-call | flops 402653184 | bytes 5242880 | tf_op jit(solution)/shard_map/pallas_call | solution.py:80
  80.5 0.5 collective-permute-start.6
  80.9 2.7 %shard_map.84 = f32[16,96,128]{2,1,0:T(8,128)S(1)} custom-call(s32[1]{0:T(128)} %bitcast.12.col_ref, f32[1024,1]{1,0:T(8,128)S(1)} %copy-done.4, bf16[1024,5120]{1,0:T(8,128)(2,1)} %grad_ref.31, bf16[1536,1024]{1,0:T(8,128)(2,1)S(1)} %bitcast.35), custom_call_target="tpu_custom_call" | custom-call | flops 402653184 | bytes 5242880 | tf_op jit(solution)/shard_map/pallas_call | solution.py:80
  83.6 0.2 collective-permute-start.5
  83.8 2.7 %shard_map.83 = f32[16,96,128]{2,1,0:T(8,128)S(1)} custom-call(s32[1]{0:T(128)} %bitcast.10.col_ref, f32[1024,1]{1,0:T(8,128)S(1)} %copy-done.5, bf16[1024,5120]{1,0:T(8,128)(2,1)} %grad_ref.31, bf16[1536,1024]{1,0:T(8,128)(2,1)S(1)} %bitcast.36), custom_call_target="tpu_custom_call" | custom-call | flops 402653184 | bytes 5242880 | tf_op jit(solution)/shard_map/pallas_call | solution.py:80
  86.5 0.6 collective-permute-start.4
  87.2 0.0 collective-permute-done.7.rest_0_
  87.2 3.2 %shard_map.87.rest_1_ = f32[4,16,96,128]{3,2,1,0:T(8,128)S(1)} custom-call(s32[1]{0:T(128)} %bitcast.15.col_ref, f32[1024,1]{1,0:T(8,128)S(1)} %copy-done.5, bf16[1024,5120]{1,0:T(8,128)(2,1)} %grad_ref.31, bf16[1536,1024]{1,0:T(8,128)(2,1)} %bitcast.25, f32[16,96,128]{2,1,0:T(8,128)S(1)} %collective-permute-done.7.rest_0_), custom_call_target="tpu_custom_call" | custom-call | flops 402653184 | bytes 6029312 | tf_op jit(solution)/shard_map/pallas_call | solution.py:80
  90.4 3.3 %shard_map.88.rest_1_ = f32[4,16,96,128]{3,2,1,0:T(8,128)S(1)} custom-call(s32[1]{0:T(128)} %bitcast.13.col_ref, f32[1024,1]{1,0:T(8,128)S(1)} %copy-done.5, bf16[1024,5120]{1,0:T(8,128)(2,1)} %grad_ref.31, bf16[1536,1024]{1,0:T(8,128)(2,1)} %bitcast.26, f32[16,96,128]{2,1,0:T(8,128)S(1)} %collective-permute-done.6.rest_0_, ...), custom_call_target="tpu_custom_call", output_to_operand_aliasing={{}: (5, {})} | custom-call | flops 402653184 | bytes 6029312 | tf_op jit(solution)/shard_map/pallas_call | solution.py:80
  93.6 3.2 %shard_map.89.rest_1_ = f32[4,16,96,128]{3,2,1,0:T(8,128)S(1)} custom-call(s32[1]{0:T(128)} %bitcast.11.col_ref, f32[1024,1]{1,0:T(8,128)S(1)} %copy-done.5, bf16[1024,5120]{1,0:T(8,128)(2,1)} %grad_ref.31, bf16[1536,1024]{1,0:T(8,128)(2,1)} %bitcast.27, f32[16,96,128]{2,1,0:T(8,128)S(1)} %collective-permute-done.5.rest_0_, ...), custom_call_target="tpu_custom_call", output_to_operand_aliasing={{}: (5, {})} | custom-call | flops 402653184 | bytes 6029312 | tf_op jit(solution)/shard_map/pallas_call | solution.py:80
  96.9 0.0 collective-permute-done.4.rest_0_
  96.9 3.2 %shard_map.90.x_ref = f32[4,16,96,128]{3,2,1,0:T(8,128)S(1)} custom-call(s32[1]{0:T(128)} %bitcast.col_ref, f32[1024,1]{1,0:T(8,128)S(1)} %copy-done.5, bf16[1024,5120]{1,0:T(8,128)(2,1)} %grad_ref.31, bf16[1536,1024]{1,0:T(8,128)(2,1)} %bitcast.28, f32[16,96,128]{2,1,0:T(8,128)S(1)} %collective-permute-done.4.rest_0_, ...), custom_call_target="tpu_custom_call", output_to_operand_aliasing={{}: (5, {})} | custom-call | flops 402653184 | bytes 6029312 | tf_op jit(solution)/shard_map/pallas_call | solution.py:80
  100.1 38.5 %shard_map.91.x_ref = f32[16,96,128]{2,1,0:T(8,128)S(1)} custom-call(f32[4,16,96,128]{3,2,1,0:T(8,128)S(1)} %shard_map.90.x_ref), custom_call_target="tpu_custom_call" | custom-call | flops 786432 | bytes 9437184 | tf_op jit(solution)/shard_map/pallas_call | solution.py:129
  138.6 18.4 %shard_map.92 = f32[96,128]{1,0:T(8,128)S(1)} custom-call(f32[16,96,128]{2,1,0:T(8,128)S(1)} %shard_map.91.x_ref), custom_call_target="tpu_custom_call" | custom-call | flops 196608 | bytes 2359296 | tf_op jit(solution)/shard_map/pallas_call | solution.py:129
  157.0 13.9 %reduce-scatter.4.cloned.1.call-done = f32[1,4,96,512]{3,2,1,0:T(8,128)} async-done(((f32[16,4,96,512]{3,2,1,0:T(8,128)}), f32[1,4,96,512]{3,2,1,0:T(8,128)}) %reduce-scatter.4.cloned.1.call-update) | async-done | bytes 786448
  170.8 1.1 copy-done.6
  172.0 12.4 %shard_map.82 = f32[96,512]{1,0:T(8,128)S(1)} custom-call(f32[4,96,512]{2,1,0:T(8,128)S(1)} %bitcast.37), custom_call_target="tpu_custom_call" | custom-call | flops 196608 | bytes 2359296 | tf_op jit(solution)/shard_map/pallas_call | solution.py:129
  184.4 0.7 pad_maximum_fusion
  (14 shorter events, 0.0 us)
Async XLA Ops:
  6.5 164.3 %reduce-scatter.4.cloned.1.call-start = ((), (), s32[]{:S(2)}) async-start(), calls=%async_computation.1 | async-start | bytes 13369344
  28.8 11.1 %copy-start.1 = (f32[1024,1]{1,0:T(8,128)}, f32[1024,1]{1,0:T(8,128)S(1)}, u32[]{:S(2)}) copy-start(f32[1024,1]{1,0:T(8,128)S(1)} %convert_multiply_fusion.coef_ref) | copy-start | bytes 12292
  34.2 17.7 %collective-permute-start.3 = (f32[16,96,512]{2,1,0:T(8,128)}, f32[16,96,512]{2,1,0:T(8,128)}, u32[]{:S(2)}, u32[]{:S(2)}) collective-permute-start(f32[16,96,512]{2,1,0:T(8,128)} %shard_map.77), channel_id=1, source_target_pairs={{0,1},{1,0},{2,3},{3,2},{4,5},{5,4},{6,7},{7,6},{8,9},{9,8},{10,11... | collective-permute-start | bytes 9437192 | tf_op jit(solution)/shard_map/ppermute | solution.py:230
  39.5 18.6 %collective-permute-start.2 = (f32[16,96,512]{2,1,0:T(8,128)}, f32[16,96,512]{2,1,0:T(8,128)}, u32[]{:S(2)}, u32[]{:S(2)}) collective-permute-start(f32[16,96,512]{2,1,0:T(8,128)} %shard_map.76), channel_id=1, source_target_pairs={{0,1},{1,0},{2,3},{3,2},{4,5},{5,4},{6,7},{7,6},{8,9},{9,8},{10,11... | collective-permute-start | bytes 9437192 | tf_op jit(solution)/shard_map/ppermute | solution.py:230
  45.1 18.3 %collective-permute-start.1 = (f32[16,96,512]{2,1,0:T(8,128)}, f32[16,96,512]{2,1,0:T(8,128)}, u32[]{:S(2)}, u32[]{:S(2)}) collective-permute-start(f32[16,96,512]{2,1,0:T(8,128)} %shard_map.75), channel_id=1, source_target_pairs={{0,1},{1,0},{2,3},{3,2},{4,5},{5,4},{6,7},{7,6},{8,9},{9,8},{10,11... | collective-permute-start | bytes 9437192 | tf_op jit(solution)/shard_map/ppermute | solution.py:230
  45.2 1.0 copy-start.2
  46.2 5.7 %copy-start = (bf16[1024,1536]{0,1:T(8,128)(2,1)S(1)}, bf16[1024,1536]{0,1:T(8,128)(2,1)}, u32[]{:S(2)}) copy-start(bf16[1024,1536]{0,1:T(8,128)(2,1)} %copy.18) | copy-start | bytes 9437188
  51.5 17.1 %collective-permute-start = (f32[16,96,512]{2,1,0:T(8,128)}, f32[16,96,512]{2,1,0:T(8,128)}, u32[]{:S(2)}, u32[]{:S(2)}) collective-permute-start(f32[16,96,512]{2,1,0:T(8,128)} %shard_map.74), channel_id=1, source_target_pairs={{0,1},{1,0},{2,3},{3,2},{4,5},{5,4},{6,7},{7,6},{8,9},{9,8},{10,11... | collective-permute-start | bytes 9437192 | tf_op jit(solution)/shard_map/ppermute | solution.py:230
  51.9 1.0 copy-start.3
  73.9 1.0 copy-start.4
  77.6 9.6 %collective-permute-start.7 = (f32[16,96,128]{2,1,0:T(8,128)S(1)}, f32[16,96,128]{2,1,0:T(8,128)S(1)}, u32[]{:S(2)}, u32[]{:S(2)}) collective-permute-start(f32[16,96,128]{2,1,0:T(8,128)S(1)} %shard_map.86), channel_id=1, source_target_pairs={{0,1},{1,0},{2,3},{3,2},{4,5},{5,4},{6,7},{7,6},{8,9},{9,8},{10,11... | collective-permute-start | bytes 2359304 | tf_op jit(solution)/shard_map/ppermute | solution.py:230
  80.4 3.4 %copy-start.5 = (f32[1024,1]{1,0:T(8,128)S(1)}, f32[1024,1]{1,0:T(8,128)}, u32[]{:S(2)}) copy-start(f32[1024,1]{1,0:T(8,128)} %copy-done.1) | copy-start | bytes 12292
  80.5 9.9 %collective-permute-start.6 = (f32[16,96,128]{2,1,0:T(8,128)S(1)}, f32[16,96,128]{2,1,0:T(8,128)S(1)}, u32[]{:S(2)}, u32[]{:S(2)}) collective-permute-start(f32[16,96,128]{2,1,0:T(8,128)S(1)} %shard_map.85), channel_id=1, source_target_pairs={{0,1},{1,0},{2,3},{3,2},{4,5},{5,4},{6,7},{7,6},{8,9},{9,8},{10,11... | collective-permute-start | bytes 2359304 | tf_op jit(solution)/shard_map/ppermute | solution.py:230
  83.6 10.0 %collective-permute-start.5 = (f32[16,96,128]{2,1,0:T(8,128)S(1)}, f32[16,96,128]{2,1,0:T(8,128)S(1)}, u32[]{:S(2)}, u32[]{:S(2)}) collective-permute-start(f32[16,96,128]{2,1,0:T(8,128)S(1)} %shard_map.84), channel_id=1, source_target_pairs={{0,1},{1,0},{2,3},{3,2},{4,5},{5,4},{6,7},{7,6},{8,9},{9,8},{10,11... | collective-permute-start | bytes 2359304 | tf_op jit(solution)/shard_map/ppermute | solution.py:230
  86.5 10.3 %collective-permute-start.4 = (f32[16,96,128]{2,1,0:T(8,128)S(1)}, f32[16,96,128]{2,1,0:T(8,128)S(1)}, u32[]{:S(2)}, u32[]{:S(2)}) collective-permute-start(f32[16,96,128]{2,1,0:T(8,128)S(1)} %shard_map.83), channel_id=1, source_target_pairs={{0,1},{1,0},{2,3},{3,2},{4,5},{5,4},{6,7},{7,6},{8,9},{9,8},{10,11... | collective-permute-start | bytes 2359304 | tf_op jit(solution)/shard_map/ppermute | solution.py:230
  170.8 1.1 copy-start.6
Sparse Core Ops, SparseCore 0:
  74.0 96.8 reduce-scatter.3

commit v10 on v9

--- a/solution.py
+++ b/solution.py
@@ -13,13 +13,12 @@
 Z_FIRST = 128
 
 
-def block_matmul(col, coef, grad, hid_t, n_dp, width, lo, hi, addend=None, into=None, slot=0,
-                 n_slots=1, z_major=False):
+def block_matmul(col, coef, grad, hid_t, n_dp, width, lo, hi, n_blocks, addend=None, into=None,
+                 slot=0, n_slots=1, z_major=False):
     hb, t = hid_t.shape
     rows = hb // n_dp
     per_tile = ROW_TILE // rows
     n_tiles = hb // ROW_TILE
-    grouped = n_slots > 1
     w = hi - lo
 
     def kernel(col_ref, coef_ref, grad_ref, hid_ref, *rest):
@@ -29,7 +28,7 @@
             rest.pop(0)
         out_ref, scaled_ref = rest
 
-        @pl.when(pl.program_id(0) == 0)
+        @pl.when(pl.program_id(1) == 0)
         def _():
             scaled_ref[...] = (coef_ref[...] * grad_ref[:, lo:hi].astype(jnp.float32)).astype(
                 jnp.bfloat16)
@@ -37,46 +36,46 @@
         acc = jnp.dot(hid_ref[...], scaled_ref[...], preferred_element_type=jnp.float32)
         for k in range(per_tile):
             part = acc[k * rows:(k + 1) * rows, :]
-            if add_ref is not None:
-                part = part + add_ref[k]
-            if not grouped:
-                out_ref[k] = part
-            elif z_major:
+            if add_ref is None:
+                out_ref[0, k] = part
+                continue
+            part = part + add_ref[0, k]
+            if z_major:
                 out_ref[0, k] = part
             else:
                 out_ref[k, 0] = part
 
     in_specs = [
-        pl.BlockSpec((t, 1), lambda i, c: (0, 0)),
-        pl.BlockSpec((t, width), lambda i, c: (0, c[0])),
-        pl.BlockSpec((ROW_TILE, t), lambda i, c: (i, 0)),
+        pl.BlockSpec((t, 1), lambda b, i, c: (0, 0)),
+        pl.BlockSpec((t, width), lambda b, i, c: (0, c[0] + 2 * b)),
+        pl.BlockSpec((ROW_TILE, t), lambda b, i, c: (i, 0)),
     ]
     args = [col, coef, grad, hid_t]
     if addend is not None:
-        in_specs.append(pl.BlockSpec((per_tile, rows, w), lambda i, c: (i, 0, 0)))
+        in_specs.append(pl.BlockSpec((1, per_tile, rows, w), lambda b, i, c: (b, i, 0, 0)))
         args.append(addend)
     aliases = {}
     if into is not None:
         in_specs.append(pl.BlockSpec(memory_space=pl.ANY))
         aliases = {len(args): 0}
         args.append(into)
-    if not grouped:
-        out_shape = jax.ShapeDtypeStruct((n_dp, rows, w), jnp.float32)
-        out_spec = pl.BlockSpec((per_tile, rows, w), lambda i, c: (i, 0, 0))
+    if addend is None:
+        out_shape = jax.ShapeDtypeStruct((n_blocks, n_dp, rows, w), jnp.float32)
+        out_spec = pl.BlockSpec((1, per_tile, rows, w), lambda b, i, c: (b, i, 0, 0))
     elif z_major:
         out_shape = jax.ShapeDtypeStruct((n_slots, n_dp, rows, w), jnp.float32)
-        out_spec = pl.BlockSpec((1, per_tile, rows, w), lambda i, c: (slot, i, 0, 0))
+        out_spec = pl.BlockSpec((1, per_tile, rows, w), lambda b, i, c: (slot + b, i, 0, 0))
     else:
         out_shape = jax.ShapeDtypeStruct((n_dp, n_slots, rows, w), jnp.float32)
-        out_spec = pl.BlockSpec((per_tile, 1, rows, w), lambda i, c: (i, slot, 0, 0))
+        out_spec = pl.BlockSpec((per_tile, 1, rows, w), lambda b, i, c: (i, slot + b, 0, 0))
     grid_spec = pltpu.PrefetchScalarGridSpec(
         num_scalar_prefetch=1,
-        grid=(n_tiles,),
+        grid=(n_blocks, n_tiles),
         in_specs=in_specs,
         out_specs=out_spec,
         scratch_shapes=[pltpu.VMEM((t, w), jnp.bfloat16)],
     )
-    extra = hb * w * 4 if addend is not None else 0
+    extra = hb * w * 4 * n_blocks if addend is not None else 0
     return pl.pallas_call(
         kernel,
         grid_spec=grid_spec,
@@ -84,8 +83,8 @@
         input_output_aliases=aliases,
         compiler_params=pltpu.CompilerParams(vmem_limit_bytes=48 * 1024 * 1024),
         cost_estimate=pl.CostEstimate(
-            flops=2 * hb * t * w, transcendentals=0,
-            bytes_accessed=hb * t * 2 + t * width * 2 + hb * w * 4 + extra,
+            flops=2 * hb * t * w * n_blocks, transcendentals=0,
+            bytes_accessed=hb * t * 2 + (t * width * 2 + hb * w * 4) * n_blocks + extra,
         ),
     )(*args)
 
@@ -222,22 +221,23 @@
 
     swap = [(0, 1), (1, 0)]
 
-    def pre_reduced(lo, hi, z_major):
+    def pre_reduced(lo, hi, z_major, per_call):
         got = []
-        for k in range(n_z):
+        for k in range(0, n_z, per_call):
             theirs = block_matmul(col_index(k, 1 - core), token_coef, out_grad, hid_t, n_dp, col,
-                                  lo, hi)
+                                  lo, hi, per_call)
             got.append(lax.ppermute(theirs, "core", perm=swap))
         chip = None
-        for k in range(n_z):
+        for j, k in enumerate(range(0, n_z, per_call)):
             chip = block_matmul(col_index(k, core), token_coef, out_grad, hid_t, n_dp, col, lo, hi,
-                                addend=got[k], into=chip, slot=k, n_slots=n_z, z_major=z_major)
+                                per_call, addend=got[j], into=chip, slot=k, n_slots=n_z,
+                                z_major=z_major)
         return chip
 
     keep = col - Z_FIRST
-    dp_first = pre_reduced(0, keep, False)
+    dp_first = pre_reduced(0, keep, False, 2)
     rows = lax.psum_scatter(dp_first, "dp", scatter_dimension=0, tiled=True)[0]
-    z_first = pre_reduced(keep, col, True)
+    z_first = pre_reduced(keep, col, True, 1)
     late = z_reduce_scatter(z_first, "z", n_z, 0)
     late = z_reduce_scatter(late, "dp", n_dp, 2)
     early = z_reduce_scatter(rows, "z", n_z, 3)

time: 193 us -> 192 us (level)
  waiting for transfers between devices: 13.9 us -> 11.4 us
  local copies, waits for them, and re-layouts: 11.8 us -> 14.2 us
    unnamed x2, waiting for transfers between devices: 13.9 us -> 10.3 us
    pallas_call x16 -> x12, Pallas kernels: 65.5 us -> 62.3 us  [block_matmul(): pl.pallas_call(kernel, grid_spec=grid_spec, out_shape=out_shape, input_ou...]
    unnamed x15 -> x19, local copies, waits for them, and re-layouts: 8.97 us -> 10.6 us
  transfers between devices with their start and end apart: 9 -> 7, of which waited for: 1 -> 2; matrix products, arithmetic and copies ran while one was open for 0% -> 0% of each run, Pallas kernels for 58% -> 54%
where the time goes in v10:
time: 192 us; the launch traced here: 191 us
  Pallas kernels  142 us (74%)
  between operations  16.2 us (8%)
  local copies, waits for them, and re-layouts  14.2 us (7%)
  waiting for transfers between devices  11.4 us (6%)
  other arithmetic  5.58 us (3%)
    pallas_call x3, Pallas kernels, z_reduce_scatter(): pl.pallas_call(kernel, out_shape=jax.ShapeDtypeStruct(rest_shape, jnp.flo...  71.2 us
    pallas_call x12, Pallas kernels, block_matmul(): pl.pallas_call(kernel, grid_spec=grid_spec, out_shape=out_shape, input_ou...  62.3 us
    unnamed x19, local copies, waits for them, and re-layouts  10.6 us
    unnamed x2, waiting for transfers between devices  10.3 us
    pallas_call x1, Pallas kernels, ctx_sum(): pl.pallas_call(kernel, out_shape=jax.ShapeDtypeStruct(vals.shape, jnp.flo...  8.69 us
  transfers between devices with their start and end apart: 7, of which 2 were waited for; matrix products, arithmetic and copies ran while one was open for 0% of the time, Pallas kernels for 54%

profile of v10, /device:TPU:0, one launch (start us, length us, event | category | flops | bytes accessed | tf_op | source)
XLA Modules:
  0.0 191.2 jit_solution(6112398601940501389)
XLA Ops:
  7.2 0.7 sub.14
  7.9 1.4 multiply_reduce_fusion
  9.3 1.3 compare_select_fusion.1
  10.5 0.6 broadcast_in_dim.30.v_ref
  11.1 8.7 %shard_map.73 = f32[8,128]{1,0:T(8,128)} custom-call(f32[8,128]{1,0:T(8,128)} %broadcast_in_dim.30.v_ref), custom_call_target="tpu_custom_call" | custom-call | tf_op jit(solution)/shard_map/pallas_call | solution.py:179
  19.8 1.3 fusion.1
  23.2 1.7 copy.15
  24.9 3.2 %copy.16 = bf16[1024,1536]{0,1:T(8,128)(2,1)S(1)} copy(bf16[1024,1536]{1,0:T(8,128)(2,1)} %param.7) | data formatting | bytes 6291456 | tf_op args[0]
  28.1 1.5 convert_multiply_fusion.coef_ref
  29.6 0.0 copy-start.1
  29.6 8.0 %shard_map.75 = f32[2,16,96,512]{3,2,1,0:T(8,128)} custom-call(s32[1]{0:T(128)} %bitcast.12.col_ref, f32[1024,1]{1,0:T(8,128)S(1)} %convert_multiply_fusion.coef_ref, bf16[1024,5120]{1,0:T(8,128)(2,1)} %grad_ref.23, bf16[1536,1024]{1,0:T(8,128)(2,1)S(1)} %bitcast.21), custom_call_target="tpu_custom_call" | custom-call | flops 3221225472 | bytes 12058624 | tf_op jit(solution)/shard_map/pallas_call | solution.py:79
  37.7 0.1 collective-permute-start.1
  37.8 1.0 copy-done.2
  38.8 7.8 %shard_map.74 = f32[2,16,96,512]{3,2,1,0:T(8,128)} custom-call(s32[1]{0:T(128)} %bitcast.10.col_ref, f32[1024,1]{1,0:T(8,128)S(1)} %copy-done.2, bf16[1024,5120]{1,0:T(8,128)(2,1)} %grad_ref.23, bf16[1536,1024]{1,0:T(8,128)(2,1)S(1)} %bitcast.22), custom_call_target="tpu_custom_call" | custom-call | flops 3221225472 | bytes 12058624 | tf_op jit(solution)/shard_map/pallas_call | solution.py:79
  46.7 0.4 collective-permute-start
  47.1 1.1 collective-permute-done.1.rest_0_
  48.2 1.0 copy-done.3
  49.2 9.5 %shard_map.76.rest_1_ = f32[16,4,96,512]{3,2,1,0:T(8,128)} custom-call(s32[1]{0:T(128)} %bitcast.11.col_ref, f32[1024,1]{1,0:T(8,128)S(1)} %copy-done.3, bf16[1024,5120]{1,0:T(8,128)(2,1)} %grad_ref.23, bf16[1536,1024]{1,0:T(8,128)(2,1)S(1)} %bitcast.23, f32[2,16,96,512]{3,2,1,0:T(8,128)} %collective-permute-done.1.rest_0_), custom_call_target="tpu_custom_call" | custom-call | flops 3221225472 | bytes 18350080 | tf_op jit(solution)/shard_map/pallas_call | solution.py:79
  58.7 0.0 collective-permute-done.rest_0_
  58.7 9.5 %shard_map.77 = f32[16,4,96,512]{3,2,1,0:T(8,128)} custom-call(s32[1]{0:T(128)} %bitcast.col_ref, f32[1024,1]{1,0:T(8,128)S(1)} %copy-done.3, bf16[1024,5120]{1,0:T(8,128)(2,1)} %grad_ref.23, bf16[1536,1024]{1,0:T(8,128)(2,1)S(1)} %bitcast.24, f32[2,16,96,512]{3,2,1,0:T(8,128)} %collective-permute-done.rest_0_, ...), custom_call_target="tpu_custom_call", output_to_operand_aliasing={{}: (5, {})} | custom-call | flops 3221225472 | bytes 18350080 | tf_op jit(solution)/shard_map/pallas_call | solution.py:79
  68.2 0.0 reduce-scatter.4.cloned.1.call-update
  68.2 1.0 copy-done.4
  69.2 3.4 %shard_map.82 = f32[1,16,96,128]{3,2,1,0:T(8,128)} custom-call(s32[1]{0:T(128)} %bitcast.12.col_ref, f32[1024,1]{1,0:T(8,128)S(1)} %copy-done.4, bf16[1024,5120]{1,0:T(8,128)(2,1)} %grad_ref.23, bf16[1536,1024]{1,0:T(8,128)(2,1)S(1)} %bitcast.25), custom_call_target="tpu_custom_call" | custom-call | flops 402653184 | bytes 5242880 | tf_op jit(solution)/shard_map/pallas_call | solution.py:79
  72.7 0.1 collective-permute-start.5
  72.8 1.0 copy-done.5
  73.9 3.4 %shard_map.81 = f32[1,16,96,128]{3,2,1,0:T(8,128)} custom-call(s32[1]{0:T(128)} %bitcast.18.col_ref, f32[1024,1]{1,0:T(8,128)S(1)} %copy-done.5, bf16[1024,5120]{1,0:T(8,128)(2,1)} %grad_ref.23, bf16[1536,1024]{1,0:T(8,128)(2,1)S(1)} %bitcast.26), custom_call_target="tpu_custom_call" | custom-call | flops 402653184 | bytes 5242880 | tf_op jit(solution)/shard_map/pallas_call | solution.py:79
  77.3 0.4 collective-permute-start.4
  77.6 3.7 %shard_map.80 = f32[1,16,96,128]{3,2,1,0:T(8,128)} custom-call(s32[1]{0:T(128)} %bitcast.10.col_ref, f32[1024,1]{1,0:T(8,128)S(1)} %copy-done.5, bf16[1024,5120]{1,0:T(8,128)(2,1)} %grad_ref.23, bf16[1536,1024]{1,0:T(8,128)(2,1)S(1)} %bitcast.27), custom_call_target="tpu_custom_call" | custom-call | flops 402653184 | bytes 5242880 | tf_op jit(solution)/shard_map/pallas_call | solution.py:79
  81.3 0.1 collective-permute-start.3
  81.4 0.0 copy-done
  81.4 1.0 copy-done.6
  82.4 3.4 %shard_map.79 = f32[1,16,96,128]{3,2,1,0:T(8,128)} custom-call(s32[1]{0:T(128)} %bitcast.16.col_ref, f32[1024,1]{1,0:T(8,128)S(1)} %copy-done.6, bf16[1024,5120]{1,0:T(8,128)(2,1)} %grad_ref.23, bf16[1536,1024]{1,0:T(8,128)(2,1)S(1)} %bitcast.28), custom_call_target="tpu_custom_call" | custom-call | flops 402653184 | bytes 5242880 | tf_op jit(solution)/shard_map/pallas_call | solution.py:79
  85.9 0.5 collective-permute-start.2
  86.3 0.0 collective-permute-done.5.rest_0_
  86.3 1.1 copy-done.7
  87.4 3.3 %shard_map.83.rest_1_ = f32[4,16,96,128]{3,2,1,0:T(8,128)S(1)} custom-call(s32[1]{0:T(128)} %bitcast.11.col_ref, f32[1024,1]{1,0:T(8,128)S(1)} %copy-done.7, bf16[1024,5120]{1,0:T(8,128)(2,1)} %grad_ref.23, bf16[1536,1024]{1,0:T(8,128)(2,1)} %bitcast.29, f32[1,16,96,128]{3,2,1,0:T(8,128)} %collective-permute-done.5.rest_0_), custom_call_target="tpu_custom_call" | custom-call | flops 402653184 | bytes 6029312 | tf_op jit(solution)/shard_map/pallas_call | solution.py:79
  90.7 0.0 collective-permute-done.4.rest_0_
  90.7 3.4 %shard_map.84.rest_1_ = f32[4,16,96,128]{3,2,1,0:T(8,128)S(1)} custom-call(s32[1]{0:T(128)} %bitcast.17.col_ref, f32[1024,1]{1,0:T(8,128)S(1)} %copy-done.7, bf16[1024,5120]{1,0:T(8,128)(2,1)} %grad_ref.23, bf16[1536,1024]{1,0:T(8,128)(2,1)} %bitcast.30, f32[1,16,96,128]{3,2,1,0:T(8,128)} %collective-permute-done.4.rest_0_, ...), custom_call_target="tpu_custom_call", output_to_operand_aliasing={{}: (5, {})} | custom-call | flops 402653184 | bytes 6029312 | tf_op jit(solution)/shard_map/pallas_call | solution.py:79
  94.1 0.0 collective-permute-done.3.rest_0_
  94.1 3.6 %shard_map.85.rest_1_ = f32[4,16,96,128]{3,2,1,0:T(8,128)S(1)} custom-call(s32[1]{0:T(128)} %bitcast.col_ref, f32[1024,1]{1,0:T(8,128)S(1)} %copy-done.7, bf16[1024,5120]{1,0:T(8,128)(2,1)} %grad_ref.23, bf16[1536,1024]{1,0:T(8,128)(2,1)} %bitcast.31, f32[1,16,96,128]{3,2,1,0:T(8,128)} %collective-permute-done.3.rest_0_, ...), custom_call_target="tpu_custom_call", output_to_operand_aliasing={{}: (5, {})} | custom-call | flops 402653184 | bytes 6029312 | tf_op jit(solution)/shard_map/pallas_call | solution.py:79
  97.8 0.0 collective-permute-done.2.rest_0_
  97.8 3.3 %shard_map.86.x_ref = f32[4,16,96,128]{3,2,1,0:T(8,128)S(1)} custom-call(s32[1]{0:T(128)} %bitcast.15.col_ref, f32[1024,1]{1,0:T(8,128)S(1)} %copy-done.7, bf16[1024,5120]{1,0:T(8,128)(2,1)} %grad_ref.23, bf16[1536,1024]{1,0:T(8,128)(2,1)} %bitcast.32, f32[1,16,96,128]{3,2,1,0:T(8,128)S(1)} %collective-permute-done.2.rest_0_, ...), custom_call_target="tpu_custom_call", output_to_operand_aliasing={{}: (5, {})} | custom-call | flops 402653184 | bytes 6029312 | tf_op jit(solution)/shard_map/pallas_call | solution.py:79
  101.0 38.2 %shard_map.87.x_ref = f32[16,96,128]{2,1,0:T(8,128)S(1)} custom-call(f32[4,16,96,128]{3,2,1,0:T(8,128)S(1)} %shard_map.86.x_ref), custom_call_target="tpu_custom_call" | custom-call | flops 786432 | bytes 9437184 | tf_op jit(solution)/shard_map/pallas_call | solution.py:128
  139.2 20.7 %shard_map.88 = f32[96,128]{1,0:T(8,128)S(1)} custom-call(f32[16,96,128]{2,1,0:T(8,128)S(1)} %shard_map.87.x_ref), custom_call_target="tpu_custom_call" | custom-call | flops 196608 | bytes 2359296 | tf_op jit(solution)/shard_map/pallas_call | solution.py:128
  159.9 10.3 %reduce-scatter.4.cloned.1.call-done = f32[1,4,96,512]{3,2,1,0:T(8,128)} async-done(((f32[16,4,96,512]{3,2,1,0:T(8,128)}), f32[1,4,96,512]{3,2,1,0:T(8,128)}) %reduce-scatter.4.cloned.1.call-update) | async-done | bytes 786448
  170.2 1.1 copy-done.8
  171.3 12.3 %shard_map.78 = f32[96,512]{1,0:T(8,128)S(1)} custom-call(f32[4,96,512]{2,1,0:T(8,128)S(1)} %bitcast.33), custom_call_target="tpu_custom_call" | custom-call | flops 196608 | bytes 2359296 | tf_op jit(solution)/shard_map/pallas_call | solution.py:128
  183.6 0.7 pad_maximum_fusion
  (10 shorter events, 0.0 us)
Async XLA Ops:
  6.5 163.6 %reduce-scatter.4.cloned.1.call-start = ((), (), s32[]{:S(2)}) async-start(), calls=%async_computation.1 | async-start | bytes 13369344
  28.1 53.3 %copy-start = (bf16[1024,1536]{0,1:T(8,128)(2,1)}, bf16[1024,1536]{0,1:T(8,128)(2,1)S(1)}, u32[]{:S(2)}) copy-start(bf16[1024,1536]{0,1:T(8,128)(2,1)S(1)} %copy.16) | copy-start | bytes 9437188
  29.6 8.0 %copy-start.1 = (f32[1024,1]{1,0:T(8,128)}, f32[1024,1]{1,0:T(8,128)S(1)}, u32[]{:S(2)}) copy-start(f32[1024,1]{1,0:T(8,128)S(1)} %convert_multiply_fusion.coef_ref) | copy-start | bytes 12292
  37.7 10.5 %collective-permute-start.1 = (f32[2,16,96,512]{3,2,1,0:T(8,128)}, f32[2,16,96,512]{3,2,1,0:T(8,128)}, u32[]{:S(2)}, u32[]{:S(2)}) collective-permute-start(f32[2,16,96,512]{3,2,1,0:T(8,128)} %shard_map.75), channel_id=1, source_target_pairs={{0,1},{1,0},{2,3},{3,2},{4,5},{5,4},{6,7},{7,6},{8,9},{9,8},{10,11... | collective-permute-start | bytes 18874376 | tf_op jit(solution)/shard_map/ppermute | solution.py:229
  37.8 1.0 copy-start.2
  46.7 12.0 %collective-permute-start = (f32[2,16,96,512]{3,2,1,0:T(8,128)}, f32[2,16,96,512]{3,2,1,0:T(8,128)}, u32[]{:S(2)}, u32[]{:S(2)}) collective-permute-start(f32[2,16,96,512]{3,2,1,0:T(8,128)} %shard_map.74), channel_id=1, source_target_pairs={{0,1},{1,0},{2,3},{3,2},{4,5},{5,4},{6,7},{7,6},{8,9},{9,8},{10,11... | collective-permute-start | bytes 18874376 | tf_op jit(solution)/shard_map/ppermute | solution.py:229
  48.2 1.0 copy-start.3
  68.2 1.0 copy-start.4
  72.7 13.7 %collective-permute-start.5 = (f32[1,16,96,128]{3,2,1,0:T(8,128)}, f32[1,16,96,128]{3,2,1,0:T(8,128)}, u32[]{:S(2)}, u32[]{:S(2)}) collective-permute-start(f32[1,16,96,128]{3,2,1,0:T(8,128)} %shard_map.82), channel_id=1, source_target_pairs={{0,1},{1,0},{2,3},{3,2},{4,5},{5,4},{6,7},{7,6},{8,9},{9,8},{10,11... | collective-permute-start | bytes 2359304 | tf_op jit(solution)/shard_map/ppermute | solution.py:229
  72.8 1.0 copy-start.5
  77.3 13.4 %collective-permute-start.4 = (f32[1,16,96,128]{3,2,1,0:T(8,128)}, f32[1,16,96,128]{3,2,1,0:T(8,128)}, u32[]{:S(2)}, u32[]{:S(2)}) collective-permute-start(f32[1,16,96,128]{3,2,1,0:T(8,128)} %shard_map.81), channel_id=1, source_target_pairs={{0,1},{1,0},{2,3},{3,2},{4,5},{5,4},{6,7},{7,6},{8,9},{9,8},{10,11... | collective-permute-start | bytes 2359304 | tf_op jit(solution)/shard_map/ppermute | solution.py:229
  81.3 12.8 %collective-permute-start.3 = (f32[1,16,96,128]{3,2,1,0:T(8,128)}, f32[1,16,96,128]{3,2,1,0:T(8,128)}, u32[]{:S(2)}, u32[]{:S(2)}) collective-permute-start(f32[1,16,96,128]{3,2,1,0:T(8,128)} %shard_map.80), channel_id=1, source_target_pairs={{0,1},{1,0},{2,3},{3,2},{4,5},{5,4},{6,7},{7,6},{8,9},{9,8},{10,11... | collective-permute-start | bytes 2359304 | tf_op jit(solution)/shard_map/ppermute | solution.py:229
  81.4 1.0 copy-start.6
  85.9 11.9 %collective-permute-start.2 = (f32[1,16,96,128]{3,2,1,0:T(8,128)}, f32[1,16,96,128]{3,2,1,0:T(8,128)S(1)}, u32[]{:S(2)}, u32[]{:S(2)}) collective-permute-start(f32[1,16,96,128]{3,2,1,0:T(8,128)} %shard_map.79), channel_id=1, source_target_pairs={{0,1},{1,0},{2,3},{3,2},{4,5},{5,4},{6,7},{7,6},{8,9},{9,8},{10,11... | collective-permute-start | bytes 2359304 | tf_op jit(solution)/shard_map/ppermute | solution.py:229
  86.3 1.1 copy-start.7
  170.2 1.1 copy-start.8
Sparse Core Ops, SparseCore 0:
  68.3 101.8 reduce-scatter.3

commit v11 on v10

--- a/solution.py
+++ b/solution.py
@@ -9,7 +9,7 @@
 
 CLIP_LOW = 0.0003
 CLIP_HIGH = 0.0004
-ROW_TILE = 768
+ROW_TILE = 1536
 Z_FIRST = 128
 
 
@@ -237,7 +237,7 @@
     keep = col - Z_FIRST
     dp_first = pre_reduced(0, keep, False, 2)
     rows = lax.psum_scatter(dp_first, "dp", scatter_dimension=0, tiled=True)[0]
-    z_first = pre_reduced(keep, col, True, 1)
+    z_first = pre_reduced(keep, col, True, n_z)
     late = z_reduce_scatter(z_first, "z", n_z, 0)
     late = z_reduce_scatter(late, "dp", n_dp, 2)
     early = z_reduce_scatter(rows, "z", n_z, 3)

time: 192 us -> 188 us (0.979)
  Pallas kernels: 142 us -> 120 us
  waiting for transfers between devices: 11.4 us -> 31.9 us
    pallas_call x12 -> x6, Pallas kernels: 62.3 us -> 44.5 us  [block_matmul(): pl.pallas_call(kernel, grid_spec=grid_spec, out_shape=out_shape, input_ou...]
    unnamed x2, waiting for transfers between devices: 10.3 us -> 24.2 us
    ppermute x6 -> x3, waiting for transfers between devices: 1.12 us -> 7.73 us  [pre_reduced(): got.append(lax.ppermute(theirs, 'core', perm=swap))]
    pallas_call x3, Pallas kernels: 71.2 us -> 67.2 us  [z_reduce_scatter(): pl.pallas_call(kernel, out_shape=jax.ShapeDtypeStruct(rest_shape, jnp.flo...]
    unnamed x19 -> x15, local copies, waits for them, and re-layouts: 10.6 us -> 9.06 us
  transfers between devices with their start and end apart: 7 -> 4, of which waited for: 2 -> 4; matrix products, arithmetic and copies ran while one was open for 0% -> 0% of each run, Pallas kernels for 54% -> 45%
where the time goes in v11:
time: 188 us; the launch traced here: 187 us
  Pallas kernels  120 us (64%)
  waiting for transfers between devices  31.9 us (17%)
  between operations  16.2 us (9%)
  local copies, waits for them, and re-layouts  12.7 us (7%)
  other arithmetic  5.48 us (3%)
    pallas_call x3, Pallas kernels, z_reduce_scatter(): pl.pallas_call(kernel, out_shape=jax.ShapeDtypeStruct(rest_shape, jnp.flo...  67.2 us
    pallas_call x6, Pallas kernels, block_matmul(): pl.pallas_call(kernel, grid_spec=grid_spec, out_shape=out_shape, input_ou...  44.5 us
    unnamed x2, waiting for transfers between devices  24.2 us
    unnamed x15, local copies, waits for them, and re-layouts  9.06 us
    pallas_call x1, Pallas kernels, ctx_sum(): pl.pallas_call(kernel, out_shape=jax.ShapeDtypeStruct(vals.shape, jnp.flo...  8.7 us
    ppermute x3, waiting for transfers between devices, pre_reduced(): got.append(lax.ppermute(theirs, 'core', perm=swap))  7.73 us
  transfers between devices with their start and end apart: 4, of which 4 were waited for; matrix products, arithmetic and copies ran while one was open for 0% of the time, Pallas kernels for 45%

profile of v11, /device:TPU:0, one launch (start us, length us, event | category | flops | bytes accessed | tf_op | source)
XLA Modules:
  0.0 187.5 jit_solution(17154878026226210301)
XLA Ops:
  6.5 0.0 reduce-scatter.4.cloned.1.call-start
  7.2 0.7 sub.11
  7.9 1.3 multiply_reduce_fusion
  9.2 1.2 compare_select_fusion.1
  10.4 0.6 broadcast_in_dim.30.v_ref
  11.0 8.7 %shard_map.73 = f32[8,128]{1,0:T(8,128)} custom-call(f32[8,128]{1,0:T(8,128)} %broadcast_in_dim.30.v_ref), custom_call_target="tpu_custom_call" | custom-call | tf_op jit(solution)/shard_map/pallas_call | solution.py:179
  19.7 1.3 fusion.1
  23.1 1.7 copy.12
  24.8 3.2 %copy.13 = bf16[1024,1536]{0,1:T(8,128)(2,1)S(1)} copy(bf16[1024,1536]{1,0:T(8,128)(2,1)} %param.7) | data formatting | bytes 6291456 | tf_op args[0]
  28.0 0.0 copy-start
  28.0 1.5 convert_multiply_fusion.coef_ref
  29.6 0.0 copy-start.1
  29.6 7.1 %shard_map.75 = f32[2,16,96,512]{3,2,1,0:T(8,128)} custom-call(s32[1]{0:T(128)} %bitcast.12.col_ref, f32[1024,1]{1,0:T(8,128)S(1)} %convert_multiply_fusion.coef_ref, bf16[1024,5120]{1,0:T(8,128)(2,1)} %grad_ref.11, bf16[1536,1024]{1,0:T(8,128)(2,1)S(1)} %bitcast.17), custom_call_target="tpu_custom_call" | custom-call | flops 3221225472 | bytes 12058624 | tf_op jit(solution)/shard_map/pallas_call | solution.py:79
  36.6 0.0 copy-done.1
  36.6 0.1 collective-permute-start.1
  36.7 0.0 copy-start.2
  36.7 1.0 copy-done.2
  37.8 6.8 %shard_map.74 = f32[2,16,96,512]{3,2,1,0:T(8,128)} custom-call(s32[1]{0:T(128)} %bitcast.10.col_ref, f32[1024,1]{1,0:T(8,128)S(1)} %copy-done.2, bf16[1024,5120]{1,0:T(8,128)(2,1)} %grad_ref.11, bf16[1536,1024]{1,0:T(8,128)(2,1)S(1)} %bitcast.18), custom_call_target="tpu_custom_call" | custom-call | flops 3221225472 | bytes 12058624 | tf_op jit(solution)/shard_map/pallas_call | solution.py:79
  44.6 0.4 collective-permute-start
  45.0 2.1 %collective-permute-done.1.rest_0_ = f32[2,16,96,512]{3,2,1,0:T(8,128)} collective-permute-done((f32[2,16,96,512]{3,2,1,0:T(8,128)}, f32[2,16,96,512]{3,2,1,0:T(8,128)}, u32[]{:S(2)}, u32[]{:S(2)}) %collective-permute-start.1) | collective-permute-done | bytes 6291488 | tf_op jit(solution)/shard_map/ppermute | solution.py:229
  47.1 0.0 copy-start.3
  47.1 1.0 copy-done.3
  48.2 7.9 %shard_map.76.rest_1_ = f32[16,4,96,512]{3,2,1,0:T(8,128)} custom-call(s32[1]{0:T(128)} %bitcast.11.col_ref, f32[1024,1]{1,0:T(8,128)S(1)} %copy-done.3, bf16[1024,5120]{1,0:T(8,128)(2,1)} %grad_ref.11, bf16[1536,1024]{1,0:T(8,128)(2,1)S(1)} %bitcast.19, f32[2,16,96,512]{3,2,1,0:T(8,128)} %collective-permute-done.1.rest_0_), custom_call_target="tpu_custom_call" | custom-call | flops 3221225472 | bytes 18350080 | tf_op jit(solution)/shard_map/pallas_call | solution.py:79
  56.0 0.1 collective-permute-done.rest_0_
  56.1 0.0 copy-done
  56.1 7.8 %shard_map.77 = f32[16,4,96,512]{3,2,1,0:T(8,128)} custom-call(s32[1]{0:T(128)} %bitcast.col_ref, f32[1024,1]{1,0:T(8,128)S(1)} %copy-done.3, bf16[1024,5120]{1,0:T(8,128)(2,1)} %grad_ref.11, bf16[1536,1024]{1,0:T(8,128)(2,1)S(1)} %bitcast.20, f32[2,16,96,512]{3,2,1,0:T(8,128)} %collective-permute-done.rest_0_, ...), custom_call_target="tpu_custom_call", output_to_operand_aliasing={{}: (5, {})} | custom-call | flops 3221225472 | bytes 18350080 | tf_op jit(solution)/shard_map/pallas_call | solution.py:79
  64.0 0.0 copy-start.4
  64.0 0.0 reduce-scatter.4.cloned.1.call-update
  64.0 1.0 copy-done.4
  65.0 7.1 %shard_map.79 = f32[4,16,96,128]{3,2,1,0:T(8,128)S(1)} custom-call(s32[1]{0:T(128)} %bitcast.12.col_ref, f32[1024,1]{1,0:T(8,128)S(1)} %copy-done.4, bf16[1024,5120]{1,0:T(8,128)(2,1)} %grad_ref.11, bf16[1536,1024]{1,0:T(8,128)(2,1)} %bitcast.21), custom_call_target="tpu_custom_call" | custom-call | flops 1610612736 | bytes 11534336 | tf_op jit(solution)/shard_map/pallas_call | solution.py:79
  72.1 0.2 collective-permute-start.2
  72.3 5.5 %collective-permute-done.2.rest_0_ = f32[4,16,96,128]{3,2,1,0:T(8,128)S(1)} collective-permute-done((f32[4,16,96,128]{3,2,1,0:T(8,128)S(1)}, f32[4,16,96,128]{3,2,1,0:T(8,128)S(1)}, u32[]{:S(2)}, u32[]{:S(2)}) %collective-permute-start.2) | collective-permute-done | bytes 3145760 | tf_op jit(solution)/shard_map/ppermute | solution.py:229
  77.9 0.0 copy-start.6
  77.9 1.6 copy-done.6
  79.5 7.8 %shard_map.80.x_ref = f32[4,16,96,128]{3,2,1,0:T(8,128)S(1)} custom-call(s32[1]{0:T(128)} %bitcast.11.col_ref, f32[1024,1]{1,0:T(8,128)S(1)} %copy-done.4, bf16[1024,5120]{1,0:T(8,128)(2,1)} %grad_ref.11, bf16[1536,1024]{1,0:T(8,128)(2,1)} %bitcast.22, f32[4,16,96,128]{3,2,1,0:T(8,128)} %copy-done.6), custom_call_target="tpu_custom_call" | custom-call | flops 1610612736 | bytes 14680064 | tf_op jit(solution)/shard_map/pallas_call | solution.py:79
  87.3 38.3 %shard_map.81.x_ref = f32[16,96,128]{2,1,0:T(8,128)S(1)} custom-call(f32[4,16,96,128]{3,2,1,0:T(8,128)S(1)} %shard_map.80.x_ref), custom_call_target="tpu_custom_call" | custom-call | flops 786432 | bytes 9437184 | tf_op jit(solution)/shard_map/pallas_call | solution.py:128
  125.6 15.7 %shard_map.82 = f32[96,128]{1,0:T(8,128)S(1)} custom-call(f32[16,96,128]{2,1,0:T(8,128)S(1)} %shard_map.81.x_ref), custom_call_target="tpu_custom_call" | custom-call | flops 196608 | bytes 2359296 | tf_op jit(solution)/shard_map/pallas_call | solution.py:128
  141.4 24.2 %reduce-scatter.4.cloned.1.call-done = f32[1,4,96,512]{3,2,1,0:T(8,128)} async-done(((f32[16,4,96,512]{3,2,1,0:T(8,128)}), f32[1,4,96,512]{3,2,1,0:T(8,128)}) %reduce-scatter.4.cloned.1.call-update) | async-done | bytes 786448
  165.6 0.0 copy-start.5
  165.6 1.1 copy-done.5
  166.7 13.2 %shard_map.78 = f32[96,512]{1,0:T(8,128)S(1)} custom-call(f32[4,96,512]{2,1,0:T(8,128)S(1)} %bitcast.23), custom_call_target="tpu_custom_call" | custom-call | flops 196608 | bytes 2359296 | tf_op jit(solution)/shard_map/pallas_call | solution.py:128
  179.9 0.7 pad_maximum_fusion
Async XLA Ops:
  6.5 159.0 %reduce-scatter.4.cloned.1.call-start = ((), (), s32[]{:S(2)}) async-start(), calls=%async_computation.1 | async-start | bytes 13369344
  28.0 28.1 %copy-start = (bf16[1024,1536]{0,1:T(8,128)(2,1)}, bf16[1024,1536]{0,1:T(8,128)(2,1)S(1)}, u32[]{:S(2)}) copy-start(bf16[1024,1536]{0,1:T(8,128)(2,1)S(1)} %copy.13) | copy-start | bytes 9437188
  29.6 7.1 %copy-start.1 = (f32[1024,1]{1,0:T(8,128)}, f32[1024,1]{1,0:T(8,128)S(1)}, u32[]{:S(2)}) copy-start(f32[1024,1]{1,0:T(8,128)S(1)} %convert_multiply_fusion.coef_ref) | copy-start | bytes 12292
  36.6 10.5 %collective-permute-start.1 = (f32[2,16,96,512]{3,2,1,0:T(8,128)}, f32[2,16,96,512]{3,2,1,0:T(8,128)}, u32[]{:S(2)}, u32[]{:S(2)}) collective-permute-start(f32[2,16,96,512]{3,2,1,0:T(8,128)} %shard_map.75), channel_id=1, source_target_pairs={{0,1},{1,0},{2,3},{3,2},{4,5},{5,4},{6,7},{7,6},{8,9},{9,8},{10,11... | collective-permute-start | bytes 18874376 | tf_op jit(solution)/shard_map/ppermute | solution.py:229
  36.7 1.0 copy-start.2
  44.6 11.5 %collective-permute-start = (f32[2,16,96,512]{3,2,1,0:T(8,128)}, f32[2,16,96,512]{3,2,1,0:T(8,128)}, u32[]{:S(2)}, u32[]{:S(2)}) collective-permute-start(f32[2,16,96,512]{3,2,1,0:T(8,128)} %shard_map.74), channel_id=1, source_target_pairs={{0,1},{1,0},{2,3},{3,2},{4,5},{5,4},{6,7},{7,6},{8,9},{9,8},{10,11... | collective-permute-start | bytes 18874376 | tf_op jit(solution)/shard_map/ppermute | solution.py:229
  47.1 1.0 copy-start.3
  64.0 1.0 copy-start.4
  72.1 5.7 %collective-permute-start.2 = (f32[4,16,96,128]{3,2,1,0:T(8,128)S(1)}, f32[4,16,96,128]{3,2,1,0:T(8,128)S(1)}, u32[]{:S(2)}, u32[]{:S(2)}) collective-permute-start(f32[4,16,96,128]{3,2,1,0:T(8,128)S(1)} %shard_map.79), channel_id=1, source_target_pairs={{0,1},{1,0},{2,3},{3,2},{4,5},{5,4},{6,7},{7,6},{8,9},{9,8},{10,11... | collective-permute-start | bytes 9437192 | tf_op jit(solution)/shard_map/ppermute | solution.py:229
  77.9 1.6 copy-start.6
  165.6 1.1 copy-start.5
Sparse Core Ops, SparseCore 0:
  64.1 101.4 reduce-scatter.3

commit v12 on v11

--- a/solution.py
+++ b/solution.py
@@ -21,7 +21,7 @@
     n_tiles = hb // ROW_TILE
     w = hi - lo
 
-    def kernel(col_ref, coef_ref, grad_ref, hid_ref, *rest):
+    def kernel(col_ref, w_ref, grad_ref, hid_ref, *rest):
         rest = list(rest)
         add_ref = rest.pop(0) if addend is not None else None
         if into is not None:
@@ -30,7 +30,7 @@
 
         @pl.when(pl.program_id(1) == 0)
         def _():
-            scaled_ref[...] = (coef_ref[...] * grad_ref[:, lo:hi].astype(jnp.float32)).astype(
+            scaled_ref[...] = (w_ref[0] * grad_ref[:, lo:hi].astype(jnp.float32)).astype(
                 jnp.bfloat16)
 
         acc = jnp.dot(hid_ref[...], scaled_ref[...], preferred_element_type=jnp.float32)
@@ -46,7 +46,7 @@
                 out_ref[k, 0] = part
 
     in_specs = [
-        pl.BlockSpec((t, 1), lambda b, i, c: (0, 0)),
+        pl.BlockSpec(memory_space=pltpu.SMEM),
         pl.BlockSpec((t, width), lambda b, i, c: (0, c[0] + 2 * b)),
         pl.BlockSpec((ROW_TILE, t), lambda b, i, c: (i, 0)),
     ]
@@ -210,10 +210,10 @@
         jnp.float32
     )
     seq_weight = -adv * seq_ratio * active / length
-    token_coef = (masked * seq_weight)[:, None]
+    token_coef = jnp.reshape(seq_weight, (1,)).astype(jnp.float32)
     d = out_grad.shape[1]
     col = d // (n_z * n_core)
-    hid_t = hidden_acts.T
+    hid_t = (hidden_acts * masked[:, None].astype(hidden_acts.dtype)).T
     core = lax.axis_index("core").astype(jnp.int32)
 
     def col_index(k, which):

time: 188 us -> 189 us (level)
  local copies, waits for them, and re-layouts: 12.7 us -> 9.39 us
  waiting for transfers between devices: 31.9 us -> 35 us
    ppermute x3, waiting for transfers between devices: 7.73 us -> 10.2 us  [pre_reduced(): got.append(lax.ppermute(theirs, 'core', perm=swap))]
    transpose x0 -> x1, other arithmetic: none -> 2.09 us  [shards(): hid_t = (hidden_acts * masked[:, None].astype(hidden_acts.dtype)).T]
    unnamed x15 -> x7, local copies, waits for them, and re-layouts: 9.06 us -> 7.46 us
  transfers between devices with their start and end apart: 4 -> 4, of which waited for: 4 -> 4; matrix products, arithmetic and copies ran while one was open for 0% -> 0% of each run, Pallas kernels for 45% -> 44%
where the time goes in v12:
time: 189 us; the launch traced here: 188 us
  Pallas kernels  120 us (63%)
  waiting for transfers between devices  35 us (19%)
  between operations  16.1 us (9%)
  local copies, waits for them, and re-layouts  9.39 us (5%)
  other arithmetic  6.85 us (4%)
    pallas_call x3, Pallas kernels, z_reduce_scatter(): pl.pallas_call(kernel, out_shape=jax.ShapeDtypeStruct(rest_shape, jnp.flo...  67.9 us
    pallas_call x6, Pallas kernels, block_matmul(): pl.pallas_call(kernel, grid_spec=grid_spec, out_shape=out_shape, input_ou...  43.7 us
    unnamed x2, waiting for transfers between devices  24.7 us
    ppermute x3, waiting for transfers between devices, pre_reduced(): got.append(lax.ppermute(theirs, 'core', perm=swap))  10.2 us
    pallas_call x1, Pallas kernels, ctx_sum(): pl.pallas_call(kernel, out_shape=jax.ShapeDtypeStruct(vals.shape, jnp.flo...  8.7 us
    unnamed x7, local copies, waits for them, and re-layouts  7.46 us
  transfers between devices with their start and end apart: 4, of which 4 were waited for; matrix products, arithmetic and copies ran while one was open for 0% of the time, Pallas kernels for 44%

profile of v12, /device:TPU:0, one launch (start us, length us, event | category | flops | bytes accessed | tf_op | source)
XLA Modules:
  0.0 188.4 jit_solution(12257720443918700867)
XLA Ops:
  6.5 0.0 reduce-scatter.4.cloned.1.call-start
  7.2 0.7 sub.11
  7.9 1.4 multiply_reduce_fusion
  9.3 1.3 compare_select_fusion.1
  10.6 0.6 broadcast_in_dim.27.v_ref
  11.1 8.7 %shard_map.73 = f32[8,128]{1,0:T(8,128)} custom-call(f32[8,128]{1,0:T(8,128)} %broadcast_in_dim.27.v_ref), custom_call_target="tpu_custom_call" | custom-call | tf_op jit(solution)/shard_map/pallas_call | solution.py:179
  19.9 1.3 fusion.1
  23.2 0.7 convert_convert_fusion
  23.9 4.7 %copy.10 = bf16[1024,1536]{0,1:T(8,128)(2,1)} copy(bf16[1024,1536]{1,0:T(8,128)(2,1)} %param.7) | data formatting | bytes 6291456 | tf_op args[0]
  28.6 2.1 %multiply_bitcast_fusion.hid_ref = bf16[1536,1024]{1,0:T(8,128)(2,1)S(1)} fusion(bf16[1024,1536]{0,1:T(8,128)(2,1)} %copy.10, bf16[1024]{0:T(1024)(128)(2,1)S(1)} %convert_convert_fusion), kind=kLoop, calls=%fused_computation | loop fusion | flops 1572864 | bytes 6293504 | tf_op jit(solution)/shard_map/transpose | solution.py:216
  30.7 0.0 copy-start
  30.7 7.7 %shard_map.75 = f32[2,16,96,512]{3,2,1,0:T(8,128)} custom-call(s32[1]{0:T(128)} %bitcast.12.col_ref, f32[1]{0:T(128)} %bitcast.8.w_ref, bf16[1024,5120]{1,0:T(8,128)(2,1)} %grad_ref.11, bf16[1536,1024]{1,0:T(8,128)(2,1)S(1)} %multiply_bitcast_fusion.hid_ref), custom_call_target="tpu_custom_call" | custom-call | flops 3221225472 | bytes 12058624 | tf_op jit(solution)/shard_map/pallas_call | solution.py:79
  38.3 0.1 collective-permute-start.1
  38.5 6.6 %shard_map.74 = f32[2,16,96,512]{3,2,1,0:T(8,128)} custom-call(s32[1]{0:T(128)} %bitcast.10.col_ref, f32[1]{0:T(128)} %bitcast.8.w_ref, bf16[1024,5120]{1,0:T(8,128)(2,1)} %grad_ref.11, bf16[1536,1024]{1,0:T(8,128)(2,1)S(1)} %multiply_bitcast_fusion.hid_ref), custom_call_target="tpu_custom_call" | custom-call | flops 3221225472 | bytes 12058624 | tf_op jit(solution)/shard_map/pallas_call | solution.py:79
  45.1 0.4 collective-permute-start
  45.5 3.4 %collective-permute-done.1.rest_0_ = f32[2,16,96,512]{3,2,1,0:T(8,128)} collective-permute-done((f32[2,16,96,512]{3,2,1,0:T(8,128)}, f32[2,16,96,512]{3,2,1,0:T(8,128)}, u32[]{:S(2)}, u32[]{:S(2)}) %collective-permute-start.1) | collective-permute-done | bytes 6291488 | tf_op jit(solution)/shard_map/ppermute | solution.py:229
  48.8 7.6 %shard_map.76.rest_1_ = f32[16,4,96,512]{3,2,1,0:T(8,128)} custom-call(s32[1]{0:T(128)} %bitcast.11.col_ref, f32[1]{0:T(128)} %bitcast.8.w_ref, bf16[1024,5120]{1,0:T(8,128)(2,1)} %grad_ref.11, bf16[1536,1024]{1,0:T(8,128)(2,1)S(1)} %multiply_bitcast_fusion.hid_ref, f32[2,16,96,512]{3,2,1,0:T(8,128)} %collective-permute-done.1.rest_0_), custom_call_target="tpu_custom_call" | custom-call | flops 3221225472 | bytes 18350080 | tf_op jit(solution)/shard_map/pallas_call | solution.py:79
  56.5 1.4 collective-permute-done.rest_0_
  57.8 0.0 copy-done
  57.8 7.6 %shard_map.77 = f32[16,4,96,512]{3,2,1,0:T(8,128)} custom-call(s32[1]{0:T(128)} %bitcast.col_ref, f32[1]{0:T(128)} %bitcast.8.w_ref, bf16[1024,5120]{1,0:T(8,128)(2,1)} %grad_ref.11, bf16[1536,1024]{1,0:T(8,128)(2,1)S(1)} %multiply_bitcast_fusion.hid_ref, f32[2,16,96,512]{3,2,1,0:T(8,128)} %collective-permute-done.rest_0_, ...), custom_call_target="tpu_custom_call", output_to_operand_aliasing={{}: (5, {})} | custom-call | flops 3221225472 | bytes 18350080 | tf_op jit(solution)/shard_map/pallas_call | solution.py:79
  65.5 0.0 reduce-scatter.4.cloned.1.call-update
  65.5 6.8 %shard_map.79 = f32[4,16,96,128]{3,2,1,0:T(8,128)S(1)} custom-call(s32[1]{0:T(128)} %bitcast.12.col_ref, f32[1]{0:T(128)} %bitcast.8.w_ref, bf16[1024,5120]{1,0:T(8,128)(2,1)} %grad_ref.11, bf16[1536,1024]{1,0:T(8,128)(2,1)} %copy-done), custom_call_target="tpu_custom_call" | custom-call | flops 1610612736 | bytes 11534336 | tf_op jit(solution)/shard_map/pallas_call | solution.py:79
  72.3 0.2 collective-permute-start.2
  72.5 5.5 %collective-permute-done.2.rest_0_ = f32[4,16,96,128]{3,2,1,0:T(8,128)S(1)} collective-permute-done((f32[4,16,96,128]{3,2,1,0:T(8,128)S(1)}, f32[4,16,96,128]{3,2,1,0:T(8,128)S(1)}, u32[]{:S(2)}, u32[]{:S(2)}) %collective-permute-start.2) | collective-permute-done | bytes 3145760 | tf_op jit(solution)/shard_map/ppermute | solution.py:229
  78.0 0.0 copy-start.2
  78.0 1.7 copy-done.2
  79.7 7.4 %shard_map.80.x_ref = f32[4,16,96,128]{3,2,1,0:T(8,128)S(1)} custom-call(s32[1]{0:T(128)} %bitcast.11.col_ref, f32[1]{0:T(128)} %bitcast.8.w_ref, bf16[1024,5120]{1,0:T(8,128)(2,1)} %grad_ref.11, bf16[1536,1024]{1,0:T(8,128)(2,1)} %copy-done, f32[4,16,96,128]{3,2,1,0:T(8,128)} %copy-done.2), custom_call_target="tpu_custom_call" | custom-call | flops 1610612736 | bytes 14680064 | tf_op jit(solution)/shard_map/pallas_call | solution.py:79
  87.1 38.4 %shard_map.81.x_ref = f32[16,96,128]{2,1,0:T(8,128)S(1)} custom-call(f32[4,16,96,128]{3,2,1,0:T(8,128)S(1)} %shard_map.80.x_ref), custom_call_target="tpu_custom_call" | custom-call | flops 786432 | bytes 9437184 | tf_op jit(solution)/shard_map/pallas_call | solution.py:128
  125.5 16.3 %shard_map.82 = f32[96,128]{1,0:T(8,128)S(1)} custom-call(f32[16,96,128]{2,1,0:T(8,128)S(1)} %shard_map.81.x_ref), custom_call_target="tpu_custom_call" | custom-call | flops 196608 | bytes 2359296 | tf_op jit(solution)/shard_map/pallas_call | solution.py:128
  141.8 24.7 %reduce-scatter.4.cloned.1.call-done = f32[1,4,96,512]{3,2,1,0:T(8,128)} async-done(((f32[16,4,96,512]{3,2,1,0:T(8,128)}), f32[1,4,96,512]{3,2,1,0:T(8,128)}) %reduce-scatter.4.cloned.1.call-update) | async-done | bytes 786448
  166.5 0.0 copy-start.1
  166.5 1.1 copy-done.1
  167.6 13.2 %shard_map.78 = f32[96,512]{1,0:T(8,128)S(1)} custom-call(f32[4,96,512]{2,1,0:T(8,128)S(1)} %bitcast.18), custom_call_target="tpu_custom_call" | custom-call | flops 196608 | bytes 2359296 | tf_op jit(solution)/shard_map/pallas_call | solution.py:128
  180.8 0.7 pad_maximum_fusion
Async XLA Ops:
  6.5 160.0 %reduce-scatter.4.cloned.1.call-start = ((), (), s32[]{:S(2)}) async-start(), calls=%async_computation.1 | async-start | bytes 13369344
  30.7 27.2 %copy-start = (bf16[1536,1024]{1,0:T(8,128)(2,1)}, bf16[1536,1024]{1,0:T(8,128)(2,1)S(1)}, u32[]{:S(2)}) copy-start(bf16[1536,1024]{1,0:T(8,128)(2,1)S(1)} %multiply_bitcast_fusion.hid_ref) | copy-start | bytes 9437188
  38.3 10.5 %collective-permute-start.1 = (f32[2,16,96,512]{3,2,1,0:T(8,128)}, f32[2,16,96,512]{3,2,1,0:T(8,128)}, u32[]{:S(2)}, u32[]{:S(2)}) collective-permute-start(f32[2,16,96,512]{3,2,1,0:T(8,128)} %shard_map.75), channel_id=1, source_target_pairs={{0,1},{1,0},{2,3},{3,2},{4,5},{5,4},{6,7},{7,6},{8,9},{9,8},{10,11... | collective-permute-start | bytes 18874376 | tf_op jit(solution)/shard_map/ppermute | solution.py:229
  45.1 12.8 %collective-permute-start = (f32[2,16,96,512]{3,2,1,0:T(8,128)}, f32[2,16,96,512]{3,2,1,0:T(8,128)}, u32[]{:S(2)}, u32[]{:S(2)}) collective-permute-start(f32[2,16,96,512]{3,2,1,0:T(8,128)} %shard_map.74), channel_id=1, source_target_pairs={{0,1},{1,0},{2,3},{3,2},{4,5},{5,4},{6,7},{7,6},{8,9},{9,8},{10,11... | collective-permute-start | bytes 18874376 | tf_op jit(solution)/shard_map/ppermute | solution.py:229
  72.3 5.7 %collective-permute-start.2 = (f32[4,16,96,128]{3,2,1,0:T(8,128)S(1)}, f32[4,16,96,128]{3,2,1,0:T(8,128)S(1)}, u32[]{:S(2)}, u32[]{:S(2)}) collective-permute-start(f32[4,16,96,128]{3,2,1,0:T(8,128)S(1)} %shard_map.79), channel_id=1, source_target_pairs={{0,1},{1,0},{2,3},{3,2},{4,5},{5,4},{6,7},{7,6},{8,9},{9,8},{10,11... | collective-permute-start | bytes 9437192 | tf_op jit(solution)/shard_map/ppermute | solution.py:229
  78.0 1.7 copy-start.2
  166.5 1.1 copy-start.1
Sparse Core Ops, SparseCore 0:
  65.6 100.8 reduce-scatter.3

commit v13 on v11

--- a/solution.py
+++ b/solution.py
@@ -140,10 +140,12 @@
         cost_estimate=pl.CostEstimate(flops=size, transcendentals=0, bytes_accessed=3 * size * 4),
     )(x)
 
-def ctx_sum(vals, n_z, n_core):
+def ctx_sum(vals, hidden, n_z, n_core):
     n = n_z * n_core
 
-    def kernel(v_ref, out_ref, recv, send_sem, recv_sem):
+    t, hb = hidden.shape
+
+    def kernel(v_ref, hid_ref, out_ref, ht_ref, recv, send_sem, recv_sem):
         me = lax.axis_index("z") * n_core + lax.axis_index("core")
 
         def peer_of(p):
@@ -153,6 +155,12 @@
         for d in range(1, n):
             pl.semaphore_signal(barrier, inc=1, device_id=peer_of(lax.rem(me + d, n)),
                                 device_id_type=pl.DeviceIdType.MESH)
+
+        @pl.loop(0, hb // 128)
+        def _(j):
+            cols = pl.ds(pl.multiple_of(j * 128, 128), 128)
+            ht_ref[cols, :] = hid_ref[:, cols].T
+
         pl.semaphore_wait(barrier, n - 1)
         copies = []
         for d in range(1, n):
@@ -178,16 +186,18 @@
 
     return pl.pallas_call(
         kernel,
-        out_shape=jax.ShapeDtypeStruct(vals.shape, jnp.float32),
-        in_specs=[pl.BlockSpec(memory_space=pltpu.VMEM)],
-        out_specs=pl.BlockSpec(memory_space=pltpu.VMEM),
+        out_shape=(jax.ShapeDtypeStruct(vals.shape, jnp.float32),
+                   jax.ShapeDtypeStruct((hb, t), hidden.dtype)),
+        in_specs=[pl.BlockSpec(memory_space=pltpu.VMEM)] * 2,
+        out_specs=(pl.BlockSpec(memory_space=pltpu.VMEM),) * 2,
         scratch_shapes=[
             pltpu.VMEM((n,) + vals.shape, jnp.float32),
             pltpu.SemaphoreType.DMA((n,)),
             pltpu.SemaphoreType.DMA((n,)),
         ],
-        compiler_params=pltpu.CompilerParams(collective_id=1, has_side_effects=True),
-    )(vals)
+        compiler_params=pltpu.CompilerParams(
+            collective_id=1, has_side_effects=True, vmem_limit_bytes=32 * 1024 * 1024),
+    )(vals, hidden)
 
 
 def shards(hidden_acts, out_grad, old_logp, new_logp, roll_len, resp_mask, advantage):
@@ -201,7 +211,8 @@
     lanes = jnp.arange(128, dtype=jnp.int32)[None, :]
     local = jnp.where(lanes == 0, jnp.sum((new_logp[0] - old_logp[0]) * masked),
                       jnp.where(lanes == 1, jnp.sum(masked), 0.0))
-    summed = ctx_sum(jnp.broadcast_to(local, (8, 128)).astype(jnp.float32), n_z, n_core)
+    summed, hid_t = ctx_sum(jnp.broadcast_to(local, (8, 128)).astype(jnp.float32), hidden_acts,
+                            n_z, n_core)
     gap_sum, count = summed[0, 0], summed[0, 1]
     adv = advantage[0, 0]
     length = jnp.maximum(count, 1.0)
@@ -213,7 +224,6 @@
     token_coef = (masked * seq_weight)[:, None]
     d = out_grad.shape[1]
     col = d // (n_z * n_core)
-    hid_t = hidden_acts.T
     core = lax.axis_index("core").astype(jnp.int32)
 
     def col_index(k, which):

time: 188 us -> 184 us (0.979)
  local copies, waits for them, and re-layouts: 12.7 us -> 10.2 us
    unnamed x15 -> x16, local copies, waits for them, and re-layouts: 9.06 us -> 7.76 us
  transfers between devices with their start and end apart: 4 -> 4, of which waited for: 4 -> 4; matrix products, arithmetic and copies ran while one was open for 0% -> 0% of each run, Pallas kernels for 45% -> 46%
where the time goes in v13:
time: 184 us; the launch traced here: 183 us
  Pallas kernels  119 us (65%)
  waiting for transfers between devices  31.9 us (17%)
  between operations  16.2 us (9%)
  local copies, waits for them, and re-layouts  10.2 us (6%)
  other arithmetic  5.24 us (3%)
    pallas_call x3, Pallas kernels, z_reduce_scatter(): pl.pallas_call(kernel, out_shape=jax.ShapeDtypeStruct(rest_shape, jnp.flo...  67.2 us
    pallas_call x6, Pallas kernels, block_matmul(): pl.pallas_call(kernel, grid_spec=grid_spec, out_shape=out_shape, input_ou...  44.5 us
    unnamed x2, waiting for transfers between devices  24.1 us
    unnamed x16, local copies, waits for them, and re-layouts  7.76 us
    ppermute x3, waiting for transfers between devices, pre_reduced(): got.append(lax.ppermute(theirs, 'core', perm=swap))  7.72 us
    pallas_call x1, Pallas kernels, ctx_sum(): pl.pallas_call(kernel, out_shape=(jax.ShapeDtypeStruct(vals.shape, jnp.fl...  7.43 us
  transfers between devices with their start and end apart: 4, of which 4 were waited for; matrix products, arithmetic and copies ran while one was open for 0% of the time, Pallas kernels for 46%

profile of v13, /device:TPU:0, one launch (start us, length us, event | category | flops | bytes accessed | tf_op | source)
XLA Modules:
  0.0 183.3 jit_solution(2300830169345273606)
XLA Ops:
  6.5 0.0 reduce-scatter.4.cloned.1.call-start
  7.2 0.7 sub.11
  7.9 1.4 multiply_reduce_fusion
  9.3 1.3 compare_select_fusion.1
  10.6 0.0 copy-start.5
  10.6 1.9 %copy-done.5 = bf16[1024,1536]{1,0:T(8,128)(2,1)S(1)} copy-done((bf16[1024,1536]{1,0:T(8,128)(2,1)S(1)}, bf16[1024,1536]{1,0:T(8,128)(2,1)}, u32[]{:S(2)}) %copy-start.5) | copy-done | bytes 3145752
  12.5 7.4 %shard_map.73 = (f32[8,128]{1,0:T(8,128)S(1)}, bf16[1536,1024]{1,0:T(8,128)(2,1)S(1)}) custom-call(f32[8,128]{1,0:T(8,128)S(1)} %broadcast_in_dim.30.v_ref, bf16[1024,1536]{1,0:T(8,128)(2,1)S(1)} %copy-done.5), custom_call_target="tpu_custom_call" | custom-call | tf_op jit(solution)/shard_map/pallas_call | solution.py:187
  19.9 0.0 copy-start
  19.9 0.7 fusion.1
  22.7 1.7 copy.10
  24.4 1.1 convert_multiply_fusion.coef_ref
  25.5 0.0 copy-start.1
  25.6 7.1 %shard_map.75 = f32[2,16,96,512]{3,2,1,0:T(8,128)} custom-call(s32[1]{0:T(128)} %bitcast.11.col_ref, f32[1024,1]{1,0:T(8,128)S(1)} %convert_multiply_fusion.coef_ref, bf16[1024,5120]{1,0:T(8,128)(2,1)} %grad_ref.11, bf16[1536,1024]{1,0:T(8,128)(2,1)S(1)} %get-tuple-element.8.hid_ref), custom_call_target="tpu_custom_call" | custom-call | flops 3221225472 | bytes 12058624 | tf_op jit(solution)/shard_map/pallas_call | solution.py:79
  32.6 0.0 copy-done.1
  32.6 0.1 collective-permute-start.1
  32.7 0.0 copy-start.2
  32.7 1.0 copy-done.2
  33.8 6.8 %shard_map.74 = f32[2,16,96,512]{3,2,1,0:T(8,128)} custom-call(s32[1]{0:T(128)} %bitcast.9.col_ref, f32[1024,1]{1,0:T(8,128)S(1)} %copy-done.2, bf16[1024,5120]{1,0:T(8,128)(2,1)} %grad_ref.11, bf16[1536,1024]{1,0:T(8,128)(2,1)S(1)} %get-tuple-element.8.hid_ref), custom_call_target="tpu_custom_call" | custom-call | flops 3221225472 | bytes 12058624 | tf_op jit(solution)/shard_map/pallas_call | solution.py:79
  40.6 0.4 collective-permute-start
  41.0 2.1 %collective-permute-done.1.rest_0_ = f32[2,16,96,512]{3,2,1,0:T(8,128)} collective-permute-done((f32[2,16,96,512]{3,2,1,0:T(8,128)}, f32[2,16,96,512]{3,2,1,0:T(8,128)}, u32[]{:S(2)}, u32[]{:S(2)}) %collective-permute-start.1) | collective-permute-done | bytes 6291488 | tf_op jit(solution)/shard_map/ppermute | solution.py:239
  43.1 0.0 copy-start.3
  43.1 1.0 copy-done.3
  44.2 7.9 %shard_map.76.rest_1_ = f32[16,4,96,512]{3,2,1,0:T(8,128)} custom-call(s32[1]{0:T(128)} %bitcast.10.col_ref, f32[1024,1]{1,0:T(8,128)S(1)} %copy-done.3, bf16[1024,5120]{1,0:T(8,128)(2,1)} %grad_ref.11, bf16[1536,1024]{1,0:T(8,128)(2,1)S(1)} %get-tuple-element.8.hid_ref, f32[2,16,96,512]{3,2,1,0:T(8,128)} %collective-permute-done.1.rest_0_), custom_call_target="tpu_custom_call" | custom-call | flops 3221225472 | bytes 18350080 | tf_op jit(solution)/shard_map/pallas_call | solution.py:79
  52.0 0.1 collective-permute-done.rest_0_
  52.1 0.0 copy-done
  52.1 7.8 %shard_map.77 = f32[16,4,96,512]{3,2,1,0:T(8,128)} custom-call(s32[1]{0:T(128)} %bitcast.col_ref, f32[1024,1]{1,0:T(8,128)S(1)} %copy-done.3, bf16[1024,5120]{1,0:T(8,128)(2,1)} %grad_ref.11, bf16[1536,1024]{1,0:T(8,128)(2,1)S(1)} %get-tuple-element.8.hid_ref, f32[2,16,96,512]{3,2,1,0:T(8,128)} %collective-permute-done.rest_0_, ...), custom_call_target="tpu_custom_call", output_to_operand_aliasing={{}: (5, {})} | custom-call | flops 3221225472 | bytes 18350080 | tf_op jit(solution)/shard_map/pallas_call | solution.py:79
  59.9 0.0 copy-start.4
  59.9 0.0 reduce-scatter.4.cloned.1.call-update
  60.0 1.0 copy-done.4
  61.0 7.1 %shard_map.79 = f32[4,16,96,128]{3,2,1,0:T(8,128)S(1)} custom-call(s32[1]{0:T(128)} %bitcast.11.col_ref, f32[1024,1]{1,0:T(8,128)S(1)} %copy-done.4, bf16[1024,5120]{1,0:T(8,128)(2,1)} %grad_ref.11, bf16[1536,1024]{1,0:T(8,128)(2,1)} %copy-done), custom_call_target="tpu_custom_call" | custom-call | flops 1610612736 | bytes 11534336 | tf_op jit(solution)/shard_map/pallas_call | solution.py:79
  68.1 0.2 collective-permute-start.2
  68.3 5.5 %collective-permute-done.2.rest_0_ = f32[4,16,96,128]{3,2,1,0:T(8,128)S(1)} collective-permute-done((f32[4,16,96,128]{3,2,1,0:T(8,128)S(1)}, f32[4,16,96,128]{3,2,1,0:T(8,128)S(1)}, u32[]{:S(2)}, u32[]{:S(2)}) %collective-permute-start.2) | collective-permute-done | bytes 3145760 | tf_op jit(solution)/shard_map/ppermute | solution.py:239
  73.8 0.0 copy-start.7
  73.8 1.6 copy-done.7
  75.5 7.8 %shard_map.80.x_ref = f32[4,16,96,128]{3,2,1,0:T(8,128)S(1)} custom-call(s32[1]{0:T(128)} %bitcast.10.col_ref, f32[1024,1]{1,0:T(8,128)S(1)} %copy-done.4, bf16[1024,5120]{1,0:T(8,128)(2,1)} %grad_ref.11, bf16[1536,1024]{1,0:T(8,128)(2,1)} %copy-done, f32[4,16,96,128]{3,2,1,0:T(8,128)} %copy-done.7), custom_call_target="tpu_custom_call" | custom-call | flops 1610612736 | bytes 14680064 | tf_op jit(solution)/shard_map/pallas_call | solution.py:79
  83.3 38.3 %shard_map.81.x_ref = f32[16,96,128]{2,1,0:T(8,128)S(1)} custom-call(f32[4,16,96,128]{3,2,1,0:T(8,128)S(1)} %shard_map.80.x_ref), custom_call_target="tpu_custom_call" | custom-call | flops 786432 | bytes 9437184 | tf_op jit(solution)/shard_map/pallas_call | solution.py:128
  121.6 15.7 %shard_map.82 = f32[96,128]{1,0:T(8,128)S(1)} custom-call(f32[16,96,128]{2,1,0:T(8,128)S(1)} %shard_map.81.x_ref), custom_call_target="tpu_custom_call" | custom-call | flops 196608 | bytes 2359296 | tf_op jit(solution)/shard_map/pallas_call | solution.py:128
  137.4 24.1 %reduce-scatter.4.cloned.1.call-done = f32[1,4,96,512]{3,2,1,0:T(8,128)} async-done(((f32[16,4,96,512]{3,2,1,0:T(8,128)}), f32[1,4,96,512]{3,2,1,0:T(8,128)}) %reduce-scatter.4.cloned.1.call-update) | async-done | bytes 786448
  161.5 0.0 copy-start.6
  161.5 1.1 copy-done.6
  162.6 13.2 %shard_map.78 = f32[96,512]{1,0:T(8,128)S(1)} custom-call(f32[4,96,512]{2,1,0:T(8,128)S(1)} %bitcast.16), custom_call_target="tpu_custom_call" | custom-call | flops 196608 | bytes 2359296 | tf_op jit(solution)/shard_map/pallas_call | solution.py:128
  175.8 0.7 pad_maximum_fusion
  (1 shorter events, 0.0 us)
Async XLA Ops:
  6.5 155.0 %reduce-scatter.4.cloned.1.call-start = ((), (), s32[]{:S(2)}) async-start(), calls=%async_computation.1 | async-start | bytes 13369344
  10.6 1.9 %copy-start.5 = (bf16[1024,1536]{1,0:T(8,128)(2,1)S(1)}, bf16[1024,1536]{1,0:T(8,128)(2,1)}, u32[]{:S(2)}) copy-start(bf16[1024,1536]{1,0:T(8,128)(2,1)} %hid_ref.1) | copy-start | bytes 9437188
  19.9 32.2 %copy-start = (bf16[1536,1024]{1,0:T(8,128)(2,1)}, bf16[1536,1024]{1,0:T(8,128)(2,1)S(1)}, u32[]{:S(2)}) copy-start(bf16[1536,1024]{1,0:T(8,128)(2,1)S(1)} %get-tuple-element.8.hid_ref) | copy-start | bytes 9437188
  25.5 7.1 %copy-start.1 = (f32[1024,1]{1,0:T(8,128)}, f32[1024,1]{1,0:T(8,128)S(1)}, u32[]{:S(2)}) copy-start(f32[1024,1]{1,0:T(8,128)S(1)} %convert_multiply_fusion.coef_ref) | copy-start | bytes 12292
  32.6 10.5 %collective-permute-start.1 = (f32[2,16,96,512]{3,2,1,0:T(8,128)}, f32[2,16,96,512]{3,2,1,0:T(8,128)}, u32[]{:S(2)}, u32[]{:S(2)}) collective-permute-start(f32[2,16,96,512]{3,2,1,0:T(8,128)} %shard_map.75), channel_id=1, source_target_pairs={{0,1},{1,0},{2,3},{3,2},{4,5},{5,4},{6,7},{7,6},{8,9},{9,8},{10,11... | collective-permute-start | bytes 18874376 | tf_op jit(solution)/shard_map/ppermute | solution.py:239
  32.7 1.0 copy-start.2
  40.6 11.5 %collective-permute-start = (f32[2,16,96,512]{3,2,1,0:T(8,128)}, f32[2,16,96,512]{3,2,1,0:T(8,128)}, u32[]{:S(2)}, u32[]{:S(2)}) collective-permute-start(f32[2,16,96,512]{3,2,1,0:T(8,128)} %shard_map.74), channel_id=1, source_target_pairs={{0,1},{1,0},{2,3},{3,2},{4,5},{5,4},{6,7},{7,6},{8,9},{9,8},{10,11... | collective-permute-start | bytes 18874376 | tf_op jit(solution)/shard_map/ppermute | solution.py:239
  43.1 1.0 copy-start.3
  59.9 1.0 copy-start.4
  68.1 5.7 %collective-permute-start.2 = (f32[4,16,96,128]{3,2,1,0:T(8,128)S(1)}, f32[4,16,96,128]{3,2,1,0:T(8,128)S(1)}, u32[]{:S(2)}, u32[]{:S(2)}) collective-permute-start(f32[4,16,96,128]{3,2,1,0:T(8,128)S(1)} %shard_map.79), channel_id=1, source_target_pairs={{0,1},{1,0},{2,3},{3,2},{4,5},{5,4},{6,7},{7,6},{8,9},{9,8},{10,11... | collective-permute-start | bytes 9437192 | tf_op jit(solution)/shard_map/ppermute | solution.py:239
  73.8 1.6 copy-start.7
  161.5 1.1 copy-start.6
Sparse Core Ops, SparseCore 0:
  60.1 101.3 reduce-scatter.3

commit v14 on v13

--- a/solution.py
+++ b/solution.py
@@ -140,12 +140,12 @@
         cost_estimate=pl.CostEstimate(flops=size, transcendentals=0, bytes_accessed=3 * size * 4),
     )(x)
 
-def ctx_sum(vals, hidden, n_z, n_core):
+def ctx_sum(new_lp, old_lp, mask, roll_len, hidden, n_z, n_core):
     n = n_z * n_core
-
     t, hb = hidden.shape
 
-    def kernel(v_ref, hid_ref, out_ref, ht_ref, recv, send_sem, recv_sem):
+    def kernel(new_ref, old_ref, mask_ref, len_ref, hid_ref, out_ref, live_ref, ht_ref,
+               mine, staged, recv, copy_sem, send_sem, recv_sem):
         me = lax.axis_index("z") * n_core + lax.axis_index("core")
 
         def peer_of(p):
@@ -155,26 +155,36 @@
         for d in range(1, n):
             pl.semaphore_signal(barrier, inc=1, device_id=peer_of(lax.rem(me + d, n)),
                                 device_id_type=pl.DeviceIdType.MESH)
+        places = me * t + lax.broadcasted_iota(jnp.int32, (8, t), 1)
+        live = jnp.where(places < len_ref[0], mask_ref[...], 0).astype(jnp.float32)
+        gap = jnp.sum((new_ref[0:1, :] - old_ref[0:1, :]) * live[0:1, :])
+        count = jnp.sum(live[0:1, :])
+        lanes = lax.broadcasted_iota(jnp.int32, (8, 128), 1)
+        mine[...] = jnp.where(lanes == 0, gap, jnp.where(lanes == 1, count, 0.0))
+        local = pltpu.make_async_copy(mine, staged, copy_sem)
+        local.start()
+        live_ref[...] = live.T[:, 0:1]
 
         @pl.loop(0, hb // 128)
         def _(j):
             cols = pl.ds(pl.multiple_of(j * 128, 128), 128)
             ht_ref[cols, :] = hid_ref[:, cols].T
 
+        local.wait()
         pl.semaphore_wait(barrier, n - 1)
         copies = []
         for d in range(1, n):
             cp = pltpu.make_async_remote_copy(
-                src_ref=v_ref, dst_ref=recv.at[me],
+                src_ref=staged, dst_ref=recv.at[me],
                 send_sem=send_sem.at[d], recv_sem=recv_sem.at[me],
                 device_id=peer_of(lax.rem(me + d, n)), device_id_type=pl.DeviceIdType.MESH)
             cp.start()
             copies.append(cp)
-        recv[me] = v_ref[...]
+        recv[me] = staged[...]
         for d in range(1, n):
             src = lax.rem(me + n - d, n)
             pltpu.make_async_remote_copy(
-                src_ref=v_ref, dst_ref=recv.at[src],
+                src_ref=staged, dst_ref=recv.at[src],
                 send_sem=send_sem.at[d], recv_sem=recv_sem.at[src],
                 device_id=peer_of(src), device_id_type=pl.DeviceIdType.MESH).wait_recv()
         total = recv[0]
@@ -184,20 +194,25 @@
             cp.wait_send()
         out_ref[...] = total
 
+    vmem = pl.BlockSpec(memory_space=pltpu.VMEM)
     return pl.pallas_call(
         kernel,
-        out_shape=(jax.ShapeDtypeStruct(vals.shape, jnp.float32),
+        out_shape=(jax.ShapeDtypeStruct((8, 128), jnp.float32),
+                   jax.ShapeDtypeStruct((t, 1), jnp.float32),
                    jax.ShapeDtypeStruct((hb, t), hidden.dtype)),
-        in_specs=[pl.BlockSpec(memory_space=pltpu.VMEM)] * 2,
-        out_specs=(pl.BlockSpec(memory_space=pltpu.VMEM),) * 2,
+        in_specs=[vmem, vmem, vmem, pl.BlockSpec(memory_space=pltpu.SMEM), vmem],
+        out_specs=(vmem, vmem, vmem),
         scratch_shapes=[
-            pltpu.VMEM((n,) + vals.shape, jnp.float32),
+            pltpu.VMEM((8, 128), jnp.float32),
+            pltpu.VMEM((8, 128), jnp.float32),
+            pltpu.VMEM((n, 8, 128), jnp.float32),
+            pltpu.SemaphoreType.DMA,
             pltpu.SemaphoreType.DMA((n,)),
             pltpu.SemaphoreType.DMA((n,)),
         ],
         compiler_params=pltpu.CompilerParams(
             collective_id=1, has_side_effects=True, vmem_limit_bytes=32 * 1024 * 1024),
-    )(vals, hidden)
+    )(new_lp, old_lp, mask, roll_len, hidden)
 
 
 def shards(hidden_acts, out_grad, old_logp, new_logp, roll_len, resp_mask, advantage):
@@ -206,13 +221,10 @@
     n_core = lax.axis_size("core")
     width = old_logp.shape[1]
     ctx = lax.axis_index("z") * n_core + lax.axis_index("core")
-    places = ctx * width + jnp.arange(width, dtype=jnp.int32)
-    masked = jnp.where(places < roll_len[0], resp_mask[0], 0).astype(jnp.float32)
-    lanes = jnp.arange(128, dtype=jnp.int32)[None, :]
-    local = jnp.where(lanes == 0, jnp.sum((new_logp[0] - old_logp[0]) * masked),
-                      jnp.where(lanes == 1, jnp.sum(masked), 0.0))
-    summed, hid_t = ctx_sum(jnp.broadcast_to(local, (8, 128)).astype(jnp.float32), hidden_acts,
-                            n_z, n_core)
+    rows8 = (8, width)
+    summed, live_col, hid_t = ctx_sum(
+        jnp.broadcast_to(new_logp, rows8), jnp.broadcast_to(old_logp, rows8),
+        jnp.broadcast_to(resp_mask, rows8), roll_len, hidden_acts, n_z, n_core)
     gap_sum, count = summed[0, 0], summed[0, 1]
     adv = advantage[0, 0]
     length = jnp.maximum(count, 1.0)
@@ -221,7 +233,7 @@
         jnp.float32
     )
     seq_weight = -adv * seq_ratio * active / length
-    token_coef = (masked * seq_weight)[:, None]
+    token_coef = live_col * seq_weight
     d = out_grad.shape[1]
     col = d // (n_z * n_core)
     core = lax.axis_index("core").astype(jnp.int32)

time: 184 us -> 183 us (level)
  other arithmetic: 5.24 us -> 2.61 us
  local copies, waits for them, and re-layouts: 10.2 us -> 12.3 us
    broadcast_in_dim x1 -> x3, local copies, waits for them, and re-layouts: 0.01 us -> 2.07 us  [the longest x1 0.69 us: shards(): jnp.broadcast_to(new_logp, rows8)]
    unnamed x16 -> x18, local copies, waits for them, and re-layouts: 7.76 us -> 9.58 us
where the time goes in v14:
time: 183 us
  Pallas kernels  119 us (65%)
  waiting for transfers between devices  31.5 us (17%)
  between operations  16.2 us (9%)
  local copies, waits for them, and re-layouts  12.3 us (7%)
  other arithmetic  2.61 us (1%)
    pallas_call x3, Pallas kernels, z_reduce_scatter(): pl.pallas_call(kernel, out_shape=jax.ShapeDtypeStruct(rest_shape, jnp.flo...  67.3 us
    pallas_call x6, Pallas kernels, block_matmul(): pl.pallas_call(kernel, grid_spec=grid_spec, out_shape=out_shape, input_ou...  44.4 us
    unnamed x2, waiting for transfers between devices  23.8 us
    unnamed x18, local copies, waits for them, and re-layouts  9.58 us
    pallas_call x1, Pallas kernels, ctx_sum(): pl.pallas_call(kernel, out_shape=(jax.ShapeDtypeStruct((8, 128), jnp.floa...  7.72 us
    ppermute x3, waiting for transfers between devices, pre_reduced(): got.append(lax.ppermute(theirs, 'core', perm=swap))  7.72 us
  transfers between devices with their start and end apart: 4, of which 4 were waited for; matrix products, arithmetic and copies ran while one was open for 0% of the time, Pallas kernels for 46%

profile of v14, /device:TPU:0, one launch (start us, length us, event | category | flops | bytes accessed | tf_op | source)
XLA Modules:
  0.0 182.7 jit_solution(18438423061575862968)
XLA Ops:
  6.5 0.0 reduce-scatter.4.cloned.1.call-start
  7.2 0.7 broadcast_in_dim.22.new_ref
  7.9 0.7 broadcast_in_dim.24.old_ref
  8.6 0.7 broadcast_in_dim.26.mask_ref
  9.3 0.0 copy-start.5
  9.3 1.9 %copy-done.5 = bf16[1024,1536]{1,0:T(8,128)(2,1)S(1)} copy-done((bf16[1024,1536]{1,0:T(8,128)(2,1)S(1)}, bf16[1024,1536]{1,0:T(8,128)(2,1)}, u32[]{:S(2)}) %copy-start.5) | copy-done | bytes 3145752
  11.1 7.7 %shard_map.73 = (f32[8,128]{1,0:T(8,128)S(1)}, f32[1024,1]{1,0:T(8,128)S(1)}, bf16[1536,1024]{1,0:T(8,128)(2,1)S(1)}) custom-call(f32[8,1024]{1,0:T(8,128)S(1)} %broadcast_in_dim.22.new_ref, f32[8,1024]{1,0:T(8,128)S(1)} %broadcast_in_dim.24.old_ref, s32[8,1024]{1,0:T(8,128)S(1)} %broadcast_in_dim.26.mask_ref, s32[1]{0:T(128)S(6)} %copy.10.len_ref, ...), custom_call_target="tpu_custom_call" | custom-call | tf_op jit(solution)/shard_map/pallas_call | solution.py:198
  18.9 0.0 copy-start.7
  18.9 0.8 copy-done.7
  19.7 0.0 copy-start
  19.7 0.7 fusion
  22.4 1.9 %broadcast_multiply_fusion.coef_ref = f32[1024,1]{1,0:T(8,128)} fusion(f32[1024,1]{1,0:T(8,128)} %copy-done.7, f32[]{:T(128)S(6)} %div.7), kind=kLoop, calls=%fused_computation | loop fusion | flops 1024 | bytes 8196 | tf_op jit(solution)/shard_map/mul | solution.py:236
  24.3 0.0 copy-start.1
  24.3 1.0 copy-done.1
  25.3 6.8 %shard_map.75 = f32[2,16,96,512]{3,2,1,0:T(8,128)} custom-call(s32[1]{0:T(128)} %bitcast.10.col_ref, f32[1024,1]{1,0:T(8,128)S(1)} %copy-done.1, bf16[1024,5120]{1,0:T(8,128)(2,1)} %grad_ref.11, bf16[1536,1024]{1,0:T(8,128)(2,1)S(1)} %get-tuple-element.10.hid_ref), custom_call_target="tpu_custom_call" | custom-call | flops 3221225472 | bytes 12058624 | tf_op jit(solution)/shard_map/pallas_call | solution.py:79
  32.2 0.1 collective-permute-start.1
  32.3 0.0 copy-start.2
  32.3 1.0 copy-done.2
  33.3 6.8 %shard_map.74 = f32[2,16,96,512]{3,2,1,0:T(8,128)} custom-call(s32[1]{0:T(128)} %bitcast.8.col_ref, f32[1024,1]{1,0:T(8,128)S(1)} %copy-done.2, bf16[1024,5120]{1,0:T(8,128)(2,1)} %grad_ref.11, bf16[1536,1024]{1,0:T(8,128)(2,1)S(1)} %get-tuple-element.10.hid_ref), custom_call_target="tpu_custom_call" | custom-call | flops 3221225472 | bytes 12058624 | tf_op jit(solution)/shard_map/pallas_call | solution.py:79
  40.2 0.4 collective-permute-start
  40.6 2.1 %collective-permute-done.1.rest_0_ = f32[2,16,96,512]{3,2,1,0:T(8,128)} collective-permute-done((f32[2,16,96,512]{3,2,1,0:T(8,128)}, f32[2,16,96,512]{3,2,1,0:T(8,128)}, u32[]{:S(2)}, u32[]{:S(2)}) %collective-permute-start.1) | collective-permute-done | bytes 6291488 | tf_op jit(solution)/shard_map/ppermute | solution.py:251
  42.7 0.0 copy-start.3
  42.7 1.0 copy-done.3
  43.7 7.9 %shard_map.76.rest_1_ = f32[16,4,96,512]{3,2,1,0:T(8,128)} custom-call(s32[1]{0:T(128)} %bitcast.9.col_ref, f32[1024,1]{1,0:T(8,128)S(1)} %copy-done.3, bf16[1024,5120]{1,0:T(8,128)(2,1)} %grad_ref.11, bf16[1536,1024]{1,0:T(8,128)(2,1)S(1)} %get-tuple-element.10.hid_ref, f32[2,16,96,512]{3,2,1,0:T(8,128)} %collective-permute-done.1.rest_0_), custom_call_target="tpu_custom_call" | custom-call | flops 3221225472 | bytes 18350080 | tf_op jit(solution)/shard_map/pallas_call | solution.py:79
  51.6 0.1 collective-permute-done.rest_0_
  51.7 0.0 copy-done
  51.7 7.9 %shard_map.77 = f32[16,4,96,512]{3,2,1,0:T(8,128)} custom-call(s32[1]{0:T(128)} %bitcast.col_ref, f32[1024,1]{1,0:T(8,128)S(1)} %copy-done.3, bf16[1024,5120]{1,0:T(8,128)(2,1)} %grad_ref.11, bf16[1536,1024]{1,0:T(8,128)(2,1)S(1)} %get-tuple-element.10.hid_ref, f32[2,16,96,512]{3,2,1,0:T(8,128)} %collective-permute-done.rest_0_, ...), custom_call_target="tpu_custom_call", output_to_operand_aliasing={{}: (5, {})} | custom-call | flops 3221225472 | bytes 18350080 | tf_op jit(solution)/shard_map/pallas_call | solution.py:79
  59.6 0.0 copy-start.4
  59.6 0.0 reduce-scatter.4.cloned.1.call-update
  59.6 1.0 copy-done.4
  60.7 7.1 %shard_map.79 = f32[4,16,96,128]{3,2,1,0:T(8,128)S(1)} custom-call(s32[1]{0:T(128)} %bitcast.10.col_ref, f32[1024,1]{1,0:T(8,128)S(1)} %copy-done.4, bf16[1024,5120]{1,0:T(8,128)(2,1)} %grad_ref.11, bf16[1536,1024]{1,0:T(8,128)(2,1)} %copy-done), custom_call_target="tpu_custom_call" | custom-call | flops 1610612736 | bytes 11534336 | tf_op jit(solution)/shard_map/pallas_call | solution.py:79
  67.8 0.2 collective-permute-start.2
  68.0 5.5 %collective-permute-done.2.rest_0_ = f32[4,16,96,128]{3,2,1,0:T(8,128)S(1)} collective-permute-done((f32[4,16,96,128]{3,2,1,0:T(8,128)S(1)}, f32[4,16,96,128]{3,2,1,0:T(8,128)S(1)}, u32[]{:S(2)}, u32[]{:S(2)}) %collective-permute-start.2) | collective-permute-done | bytes 3145760 | tf_op jit(solution)/shard_map/ppermute | solution.py:251
  73.5 0.0 copy-start.8
  73.5 1.6 copy-done.8
  75.1 7.8 %shard_map.80.x_ref = f32[4,16,96,128]{3,2,1,0:T(8,128)S(1)} custom-call(s32[1]{0:T(128)} %bitcast.9.col_ref, f32[1024,1]{1,0:T(8,128)S(1)} %copy-done.4, bf16[1024,5120]{1,0:T(8,128)(2,1)} %grad_ref.11, bf16[1536,1024]{1,0:T(8,128)(2,1)} %copy-done, f32[4,16,96,128]{3,2,1,0:T(8,128)} %copy-done.8), custom_call_target="tpu_custom_call" | custom-call | flops 1610612736 | bytes 14680064 | tf_op jit(solution)/shard_map/pallas_call | solution.py:79
  83.0 38.3 %shard_map.81.x_ref = f32[16,96,128]{2,1,0:T(8,128)S(1)} custom-call(f32[4,16,96,128]{3,2,1,0:T(8,128)S(1)} %shard_map.80.x_ref), custom_call_target="tpu_custom_call" | custom-call | flops 786432 | bytes 9437184 | tf_op jit(solution)/shard_map/pallas_call | solution.py:128
  121.3 15.8 %shard_map.82 = f32[96,128]{1,0:T(8,128)S(1)} custom-call(f32[16,96,128]{2,1,0:T(8,128)S(1)} %shard_map.81.x_ref), custom_call_target="tpu_custom_call" | custom-call | flops 196608 | bytes 2359296 | tf_op jit(solution)/shard_map/pallas_call | solution.py:128
  137.1 23.8 %reduce-scatter.4.cloned.1.call-done = f32[1,4,96,512]{3,2,1,0:T(8,128)} async-done(((f32[16,4,96,512]{3,2,1,0:T(8,128)}), f32[1,4,96,512]{3,2,1,0:T(8,128)}) %reduce-scatter.4.cloned.1.call-update) | async-done | bytes 786448
  160.9 0.0 copy-start.6
  160.9 1.1 copy-done.6
  162.0 13.2 %shard_map.78 = f32[96,512]{1,0:T(8,128)S(1)} custom-call(f32[4,96,512]{2,1,0:T(8,128)S(1)} %bitcast.13), custom_call_target="tpu_custom_call" | custom-call | flops 196608 | bytes 2359296 | tf_op jit(solution)/shard_map/pallas_call | solution.py:128
  175.2 0.7 pad_maximum_fusion
Async XLA Ops:
  6.5 154.4 %reduce-scatter.4.cloned.1.call-start = ((), (), s32[]{:S(2)}) async-start(), calls=%async_computation.1 | async-start | bytes 13369344
  9.3 1.9 %copy-start.5 = (bf16[1024,1536]{1,0:T(8,128)(2,1)S(1)}, bf16[1024,1536]{1,0:T(8,128)(2,1)}, u32[]{:S(2)}) copy-start(bf16[1024,1536]{1,0:T(8,128)(2,1)} %hid_ref.1) | copy-start | bytes 9437188
  18.9 0.8 copy-start.7
  19.7 32.0 %copy-start = (bf16[1536,1024]{1,0:T(8,128)(2,1)}, bf16[1536,1024]{1,0:T(8,128)(2,1)S(1)}, u32[]{:S(2)}) copy-start(bf16[1536,1024]{1,0:T(8,128)(2,1)S(1)} %get-tuple-element.10.hid_ref) | copy-start | bytes 9437188
  24.3 1.0 copy-start.1
  32.2 10.5 %collective-permute-start.1 = (f32[2,16,96,512]{3,2,1,0:T(8,128)}, f32[2,16,96,512]{3,2,1,0:T(8,128)}, u32[]{:S(2)}, u32[]{:S(2)}) collective-permute-start(f32[2,16,96,512]{3,2,1,0:T(8,128)} %shard_map.75), channel_id=1, source_target_pairs={{0,1},{1,0},{2,3},{3,2},{4,5},{5,4},{6,7},{7,6},{8,9},{9,8},{10,11... | collective-permute-start | bytes 18874376 | tf_op jit(solution)/shard_map/ppermute | solution.py:251
  32.3 1.0 copy-start.2
  40.2 11.5 %collective-permute-start = (f32[2,16,96,512]{3,2,1,0:T(8,128)}, f32[2,16,96,512]{3,2,1,0:T(8,128)}, u32[]{:S(2)}, u32[]{:S(2)}) collective-permute-start(f32[2,16,96,512]{3,2,1,0:T(8,128)} %shard_map.74), channel_id=1, source_target_pairs={{0,1},{1,0},{2,3},{3,2},{4,5},{5,4},{6,7},{7,6},{8,9},{9,8},{10,11... | collective-permute-start | bytes 18874376 | tf_op jit(solution)/shard_map/ppermute | solution.py:251
  42.7 1.0 copy-start.3
  59.6 1.0 copy-start.4
  67.8 5.7 %collective-permute-start.2 = (f32[4,16,96,128]{3,2,1,0:T(8,128)S(1)}, f32[4,16,96,128]{3,2,1,0:T(8,128)S(1)}, u32[]{:S(2)}, u32[]{:S(2)}) collective-permute-start(f32[4,16,96,128]{3,2,1,0:T(8,128)S(1)} %shard_map.79), channel_id=1, source_target_pairs={{0,1},{1,0},{2,3},{3,2},{4,5},{5,4},{6,7},{7,6},{8,9},{9,8},{10,11... | collective-permute-start | bytes 9437192 | tf_op jit(solution)/shard_map/ppermute | solution.py:251
  73.5 1.6 copy-start.8
  160.9 1.1 copy-start.6
Sparse Core Ops, SparseCore 0:
  59.8 101.0 reduce-scatter.3

commit v15 on v14

--- a/solution.py
+++ b/solution.py
@@ -21,7 +21,7 @@
     n_tiles = hb // ROW_TILE
     w = hi - lo
 
-    def kernel(col_ref, coef_ref, grad_ref, hid_ref, *rest):
+    def kernel(col_ref, w_ref, grad_ref, hid_ref, *rest):
         rest = list(rest)
         add_ref = rest.pop(0) if addend is not None else None
         if into is not None:
@@ -30,7 +30,7 @@
 
         @pl.when(pl.program_id(1) == 0)
         def _():
-            scaled_ref[...] = (coef_ref[...] * grad_ref[:, lo:hi].astype(jnp.float32)).astype(
+            scaled_ref[...] = (w_ref[0] * grad_ref[:, lo:hi].astype(jnp.float32)).astype(
                 jnp.bfloat16)
 
         acc = jnp.dot(hid_ref[...], scaled_ref[...], preferred_element_type=jnp.float32)
@@ -46,7 +46,7 @@
                 out_ref[k, 0] = part
 
     in_specs = [
-        pl.BlockSpec((t, 1), lambda b, i, c: (0, 0)),
+        pl.BlockSpec(memory_space=pltpu.SMEM),
         pl.BlockSpec((t, width), lambda b, i, c: (0, c[0] + 2 * b)),
         pl.BlockSpec((ROW_TILE, t), lambda b, i, c: (i, 0)),
     ]
@@ -163,12 +163,14 @@
         mine[...] = jnp.where(lanes == 0, gap, jnp.where(lanes == 1, count, 0.0))
         local = pltpu.make_async_copy(mine, staged, copy_sem)
         local.start()
-        live_ref[...] = live.T[:, 0:1]
+        live_col = live.T[:, 0:1]
+        live_ref[...] = live_col
+        live_hid = live_col.astype(hid_ref.dtype)
 
         @pl.loop(0, hb // 128)
         def _(j):
             cols = pl.ds(pl.multiple_of(j * 128, 128), 128)
-            ht_ref[cols, :] = hid_ref[:, cols].T
+            ht_ref[cols, :] = (hid_ref[:, cols] * live_hid).T
 
         local.wait()
         pl.semaphore_wait(barrier, n - 1)
@@ -233,7 +235,7 @@
         jnp.float32
     )
     seq_weight = -adv * seq_ratio * active / length
-    token_coef = live_col * seq_weight
+    token_coef = jnp.reshape(seq_weight, (1,)).astype(jnp.float32)
     d = out_grad.shape[1]
     col = d // (n_z * n_core)
     core = lax.axis_index("core").astype(jnp.int32)

time: 183 us -> 180 us (0.984)
  local copies, waits for them, and re-layouts: 12.3 us -> 7.41 us
  waiting for transfers between devices: 31.5 us -> 34.7 us
  other arithmetic: 2.61 us -> 0.71 us
    unnamed x18 -> x8, local copies, waits for them, and re-layouts: 9.58 us -> 4.66 us
    ppermute x3, waiting for transfers between devices: 7.72 us -> 10.2 us  [pre_reduced(): got.append(lax.ppermute(theirs, 'core', perm=swap))]
    mul x1 -> x0, other arithmetic: 1.9 us -> none  [shards(): token_coef = live_col * seq_weight]
where the time goes in v15:
time: 180 us
  Pallas kernels  120 us (67%)
  waiting for transfers between devices  34.7 us (19%)
  between operations  16.2 us (9%)
  local copies, waits for them, and re-layouts  7.41 us (4%)
    pallas_call x3, Pallas kernels, z_reduce_scatter(): pl.pallas_call(kernel, out_shape=jax.ShapeDtypeStruct(rest_shape, jnp.flo...  67.7 us
    pallas_call x6, Pallas kernels, block_matmul(): pl.pallas_call(kernel, grid_spec=grid_spec, out_shape=out_shape, input_ou...  42.8 us
    unnamed x2, waiting for transfers between devices  24.6 us
    ppermute x3, waiting for transfers between devices, pre_reduced(): got.append(lax.ppermute(theirs, 'core', perm=swap))  10.2 us
    pallas_call x1, Pallas kernels, ctx_sum(): pl.pallas_call(kernel, out_shape=(jax.ShapeDtypeStruct((8, 128), jnp.floa...  9.53 us
    unnamed x8, local copies, waits for them, and re-layouts  4.66 us
  transfers between devices with their start and end apart: 4, of which 4 were waited for; matrix products, arithmetic and copies ran while one was open for 0% of the time, Pallas kernels for 46%

profile of v15, /device:TPU:0, one launch (start us, length us, event | category | flops | bytes accessed | tf_op | source)
XLA Modules:
  0.0 179.8 jit_solution(10004068170597244665)
XLA Ops:
  6.5 0.0 reduce-scatter.4.cloned.1.call-start
  7.2 0.7 broadcast_in_dim.22.new_ref
  7.9 0.7 broadcast_in_dim.24.old_ref
  8.6 0.7 broadcast_in_dim.26.mask_ref
  9.3 0.0 copy-start.1
  9.3 1.9 %copy-done.1 = bf16[1024,1536]{1,0:T(8,128)(2,1)S(1)} copy-done((bf16[1024,1536]{1,0:T(8,128)(2,1)S(1)}, bf16[1024,1536]{1,0:T(8,128)(2,1)}, u32[]{:S(2)}) %copy-start.1) | copy-done | bytes 3145752
  11.1 9.5 %shard_map.73 = (f32[8,128]{1,0:T(8,128)S(1)}, f32[1024,1]{1,0:T(8,128)}, bf16[1536,1024]{1,0:T(8,128)(2,1)S(1)}) custom-call(f32[8,1024]{1,0:T(8,128)S(1)} %broadcast_in_dim.22.new_ref, f32[8,1024]{1,0:T(8,128)S(1)} %broadcast_in_dim.24.old_ref, s32[8,1024]{1,0:T(8,128)S(1)} %broadcast_in_dim.26.mask_ref, s32[1]{0:T(128)S(6)} %copy.10.len_ref, ...), custom_call_target="tpu_custom_call" | custom-call | tf_op jit(solution)/shard_map/pallas_call | solution.py:200
  20.7 0.0 copy-start
  20.7 0.7 fusion
  23.4 6.7 %shard_map.75 = f32[2,16,96,512]{3,2,1,0:T(8,128)} custom-call(s32[1]{0:T(128)} %bitcast.11.col_ref, f32[1]{0:T(128)} %bitcast.8.w_ref, bf16[1024,5120]{1,0:T(8,128)(2,1)} %grad_ref.11, bf16[1536,1024]{1,0:T(8,128)(2,1)S(1)} %get-tuple-element.8.hid_ref), custom_call_target="tpu_custom_call" | custom-call | flops 3221225472 | bytes 12058624 | tf_op jit(solution)/shard_map/pallas_call | solution.py:79
  30.1 0.1 collective-permute-start.1
  30.2 6.6 %shard_map.74 = f32[2,16,96,512]{3,2,1,0:T(8,128)} custom-call(s32[1]{0:T(128)} %bitcast.9.col_ref, f32[1]{0:T(128)} %bitcast.8.w_ref, bf16[1024,5120]{1,0:T(8,128)(2,1)} %grad_ref.11, bf16[1536,1024]{1,0:T(8,128)(2,1)S(1)} %get-tuple-element.8.hid_ref), custom_call_target="tpu_custom_call" | custom-call | flops 3221225472 | bytes 12058624 | tf_op jit(solution)/shard_map/pallas_call | solution.py:79
  36.9 0.4 collective-permute-start
  37.3 3.4 %collective-permute-done.1.rest_0_ = f32[2,16,96,512]{3,2,1,0:T(8,128)} collective-permute-done((f32[2,16,96,512]{3,2,1,0:T(8,128)}, f32[2,16,96,512]{3,2,1,0:T(8,128)}, u32[]{:S(2)}, u32[]{:S(2)}) %collective-permute-start.1) | collective-permute-done | bytes 6291488 | tf_op jit(solution)/shard_map/ppermute | solution.py:253
  40.6 7.7 %shard_map.76.rest_1_ = f32[16,4,96,512]{3,2,1,0:T(8,128)} custom-call(s32[1]{0:T(128)} %bitcast.10.col_ref, f32[1]{0:T(128)} %bitcast.8.w_ref, bf16[1024,5120]{1,0:T(8,128)(2,1)} %grad_ref.11, bf16[1536,1024]{1,0:T(8,128)(2,1)S(1)} %get-tuple-element.8.hid_ref, f32[2,16,96,512]{3,2,1,0:T(8,128)} %collective-permute-done.1.rest_0_), custom_call_target="tpu_custom_call" | custom-call | flops 3221225472 | bytes 18350080 | tf_op jit(solution)/shard_map/pallas_call | solution.py:79
  48.3 1.3 collective-permute-done.rest_0_
  49.6 0.0 copy-done
  49.6 7.6 %shard_map.77 = f32[16,4,96,512]{3,2,1,0:T(8,128)} custom-call(s32[1]{0:T(128)} %bitcast.col_ref, f32[1]{0:T(128)} %bitcast.8.w_ref, bf16[1024,5120]{1,0:T(8,128)(2,1)} %grad_ref.11, bf16[1536,1024]{1,0:T(8,128)(2,1)S(1)} %get-tuple-element.8.hid_ref, f32[2,16,96,512]{3,2,1,0:T(8,128)} %collective-permute-done.rest_0_, ...), custom_call_target="tpu_custom_call", output_to_operand_aliasing={{}: (5, {})} | custom-call | flops 3221225472 | bytes 18350080 | tf_op jit(solution)/shard_map/pallas_call | solution.py:79
  57.2 0.0 reduce-scatter.4.cloned.1.call-update
  57.3 6.8 %shard_map.79 = f32[4,16,96,128]{3,2,1,0:T(8,128)S(1)} custom-call(s32[1]{0:T(128)} %bitcast.11.col_ref, f32[1]{0:T(128)} %bitcast.8.w_ref, bf16[1024,5120]{1,0:T(8,128)(2,1)} %grad_ref.11, bf16[1536,1024]{1,0:T(8,128)(2,1)} %copy-done), custom_call_target="tpu_custom_call" | custom-call | flops 1610612736 | bytes 11534336 | tf_op jit(solution)/shard_map/pallas_call | solution.py:79
  64.1 0.2 collective-permute-start.2
  64.3 5.5 %collective-permute-done.2.rest_0_ = f32[4,16,96,128]{3,2,1,0:T(8,128)S(1)} collective-permute-done((f32[4,16,96,128]{3,2,1,0:T(8,128)S(1)}, f32[4,16,96,128]{3,2,1,0:T(8,128)S(1)}, u32[]{:S(2)}, u32[]{:S(2)}) %collective-permute-start.2) | collective-permute-done | bytes 3145760 | tf_op jit(solution)/shard_map/ppermute | solution.py:253
  69.8 0.0 copy-start.3
  69.8 1.6 copy-done.3
  71.4 7.4 %shard_map.80.x_ref = f32[4,16,96,128]{3,2,1,0:T(8,128)S(1)} custom-call(s32[1]{0:T(128)} %bitcast.10.col_ref, f32[1]{0:T(128)} %bitcast.8.w_ref, bf16[1024,5120]{1,0:T(8,128)(2,1)} %grad_ref.11, bf16[1536,1024]{1,0:T(8,128)(2,1)} %copy-done, f32[4,16,96,128]{3,2,1,0:T(8,128)} %copy-done.3), custom_call_target="tpu_custom_call" | custom-call | flops 1610612736 | bytes 14680064 | tf_op jit(solution)/shard_map/pallas_call | solution.py:79
  78.9 38.3 %shard_map.81.x_ref = f32[16,96,128]{2,1,0:T(8,128)S(1)} custom-call(f32[4,16,96,128]{3,2,1,0:T(8,128)S(1)} %shard_map.80.x_ref), custom_call_target="tpu_custom_call" | custom-call | flops 786432 | bytes 9437184 | tf_op jit(solution)/shard_map/pallas_call | solution.py:128
  117.2 16.2 %shard_map.82 = f32[96,128]{1,0:T(8,128)S(1)} custom-call(f32[16,96,128]{2,1,0:T(8,128)S(1)} %shard_map.81.x_ref), custom_call_target="tpu_custom_call" | custom-call | flops 196608 | bytes 2359296 | tf_op jit(solution)/shard_map/pallas_call | solution.py:128
  133.4 24.5 %reduce-scatter.4.cloned.1.call-done = f32[1,4,96,512]{3,2,1,0:T(8,128)} async-done(((f32[16,4,96,512]{3,2,1,0:T(8,128)}), f32[1,4,96,512]{3,2,1,0:T(8,128)}) %reduce-scatter.4.cloned.1.call-update) | async-done | bytes 786448
  158.0 0.0 copy-start.2
  158.0 1.1 copy-done.2
  159.1 13.1 %shard_map.78 = f32[96,512]{1,0:T(8,128)S(1)} custom-call(f32[4,96,512]{2,1,0:T(8,128)S(1)} %bitcast.14), custom_call_target="tpu_custom_call" | custom-call | flops 196608 | bytes 2359296 | tf_op jit(solution)/shard_map/pallas_call | solution.py:128
  172.2 0.7 pad_maximum_fusion
Async XLA Ops:
  6.5 151.5 %reduce-scatter.4.cloned.1.call-start = ((), (), s32[]{:S(2)}) async-start(), calls=%async_computation.1 | async-start | bytes 13369344
  9.3 1.9 %copy-start.1 = (bf16[1024,1536]{1,0:T(8,128)(2,1)S(1)}, bf16[1024,1536]{1,0:T(8,128)(2,1)}, u32[]{:S(2)}) copy-start(bf16[1024,1536]{1,0:T(8,128)(2,1)} %hid_ref.1) | copy-start | bytes 9437188
  20.7 28.9 %copy-start = (bf16[1536,1024]{1,0:T(8,128)(2,1)}, bf16[1536,1024]{1,0:T(8,128)(2,1)S(1)}, u32[]{:S(2)}) copy-start(bf16[1536,1024]{1,0:T(8,128)(2,1)S(1)} %get-tuple-element.8.hid_ref) | copy-start | bytes 9437188
  30.1 10.5 %collective-permute-start.1 = (f32[2,16,96,512]{3,2,1,0:T(8,128)}, f32[2,16,96,512]{3,2,1,0:T(8,128)}, u32[]{:S(2)}, u32[]{:S(2)}) collective-permute-start(f32[2,16,96,512]{3,2,1,0:T(8,128)} %shard_map.75), channel_id=1, source_target_pairs={{0,1},{1,0},{2,3},{3,2},{4,5},{5,4},{6,7},{7,6},{8,9},{9,8},{10,11... | collective-permute-start | bytes 18874376 | tf_op jit(solution)/shard_map/ppermute | solution.py:253
  36.9 12.8 %collective-permute-start = (f32[2,16,96,512]{3,2,1,0:T(8,128)}, f32[2,16,96,512]{3,2,1,0:T(8,128)}, u32[]{:S(2)}, u32[]{:S(2)}) collective-permute-start(f32[2,16,96,512]{3,2,1,0:T(8,128)} %shard_map.74), channel_id=1, source_target_pairs={{0,1},{1,0},{2,3},{3,2},{4,5},{5,4},{6,7},{7,6},{8,9},{9,8},{10,11... | collective-permute-start | bytes 18874376 | tf_op jit(solution)/shard_map/ppermute | solution.py:253
  64.1 5.7 %collective-permute-start.2 = (f32[4,16,96,128]{3,2,1,0:T(8,128)S(1)}, f32[4,16,96,128]{3,2,1,0:T(8,128)S(1)}, u32[]{:S(2)}, u32[]{:S(2)}) collective-permute-start(f32[4,16,96,128]{3,2,1,0:T(8,128)S(1)} %shard_map.79), channel_id=1, source_target_pairs={{0,1},{1,0},{2,3},{3,2},{4,5},{5,4},{6,7},{7,6},{8,9},{9,8},{10,11... | collective-permute-start | bytes 9437192 | tf_op jit(solution)/shard_map/ppermute | solution.py:253
  69.8 1.6 copy-start.3
  158.0 1.1 copy-start.2
Sparse Core Ops, SparseCore 0:
  57.4 100.5 reduce-scatter.3

commit v16 on v15

--- a/solution.py
+++ b/solution.py
@@ -144,9 +144,11 @@
     n = n_z * n_core
     t, hb = hidden.shape
 
-    def kernel(new_ref, old_ref, mask_ref, len_ref, hid_ref, out_ref, live_ref, ht_ref,
-               mine, staged, recv, copy_sem, send_sem, recv_sem):
+    def kernel(new_ref, old_ref, mask_ref, len_ref, hid_hbm, out_ref, live_ref, ht_ref,
+               hid_ref, mine, staged, recv, hid_sem, copy_sem, send_sem, recv_sem):
         me = lax.axis_index("z") * n_core + lax.axis_index("core")
+        fetch = pltpu.make_async_copy(hid_hbm, hid_ref, hid_sem)
+        fetch.start()
 
         def peer_of(p):
             return {"z": p // n_core, "core": p % n_core}
@@ -156,8 +158,9 @@
             pl.semaphore_signal(barrier, inc=1, device_id=peer_of(lax.rem(me + d, n)),
                                 device_id_type=pl.DeviceIdType.MESH)
         places = me * t + lax.broadcasted_iota(jnp.int32, (8, t), 1)
-        live = jnp.where(places < len_ref[0], mask_ref[...], 0).astype(jnp.float32)
-        gap = jnp.sum((new_ref[0:1, :] - old_ref[0:1, :]) * live[0:1, :])
+        mask8 = jnp.broadcast_to(mask_ref[...], (8, t))
+        live = jnp.where(places < len_ref[0], mask8, 0).astype(jnp.float32)
+        gap = jnp.sum((new_ref[...] - old_ref[...]) * live[0:1, :])
         count = jnp.sum(live[0:1, :])
         lanes = lax.broadcasted_iota(jnp.int32, (8, 128), 1)
         mine[...] = jnp.where(lanes == 0, gap, jnp.where(lanes == 1, count, 0.0))
@@ -166,6 +169,8 @@
         live_col = live.T[:, 0:1]
         live_ref[...] = live_col
         live_hid = live_col.astype(hid_ref.dtype)
+
+        fetch.wait()
 
         @pl.loop(0, hb // 128)
         def _(j):
@@ -202,12 +207,15 @@
         out_shape=(jax.ShapeDtypeStruct((8, 128), jnp.float32),
                    jax.ShapeDtypeStruct((t, 1), jnp.float32),
                    jax.ShapeDtypeStruct((hb, t), hidden.dtype)),
-        in_specs=[vmem, vmem, vmem, pl.BlockSpec(memory_space=pltpu.SMEM), vmem],
+        in_specs=[vmem, vmem, vmem, pl.BlockSpec(memory_space=pltpu.SMEM),
+                  pl.BlockSpec(memory_space=pl.ANY)],
         out_specs=(vmem, vmem, vmem),
         scratch_shapes=[
+            pltpu.VMEM((t, hb), hidden.dtype),
             pltpu.VMEM((8, 128), jnp.float32),
             pltpu.VMEM((8, 128), jnp.float32),
             pltpu.VMEM((n, 8, 128), jnp.float32),
+            pltpu.SemaphoreType.DMA,
             pltpu.SemaphoreType.DMA,
             pltpu.SemaphoreType.DMA((n,)),
             pltpu.SemaphoreType.DMA((n,)),
@@ -223,10 +231,8 @@
     n_core = lax.axis_size("core")
     width = old_logp.shape[1]
     ctx = lax.axis_index("z") * n_core + lax.axis_index("core")
-    rows8 = (8, width)
-    summed, live_col, hid_t = ctx_sum(
-        jnp.broadcast_to(new_logp, rows8), jnp.broadcast_to(old_logp, rows8),
-        jnp.broadcast_to(resp_mask, rows8), roll_len, hidden_acts, n_z, n_core)
+    summed, live_col, hid_t = ctx_sum(new_logp, old_logp, resp_mask, roll_len, hidden_acts,
+                                      n_z, n_core)
     gap_sum, count = summed[0, 0], summed[0, 1]
     adv = advantage[0, 0]
     length = jnp.maximum(count, 1.0)

time: 180 us -> 181 us (level)
    broadcast_in_dim x3 -> x0, local copies, waits for them, and re-layouts: 2.07 us -> none  [the longest x1 0.69 us: shards(): jnp.broadcast_to(new_logp, rows8)]
    unnamed x8 -> x14, local copies, waits for them, and re-layouts: 4.66 us -> 6.72 us
where the time goes in v16:
time: 181 us; the launch traced here: 180 us
  Pallas kernels  121 us (67%)
  waiting for transfers between devices  34.6 us (19%)
  between operations  16.1 us (9%)
  local copies, waits for them, and re-layouts  7.4 us (4%)
    pallas_call x3, Pallas kernels, z_reduce_scatter(): pl.pallas_call(kernel, out_shape=jax.ShapeDtypeStruct(rest_shape, jnp.flo...  67.9 us
    pallas_call x6, Pallas kernels, block_matmul(): pl.pallas_call(kernel, grid_spec=grid_spec, out_shape=out_shape, input_ou...  42.9 us
    unnamed x2, waiting for transfers between devices  24.5 us
    ppermute x3, waiting for transfers between devices, pre_reduced(): got.append(lax.ppermute(theirs, 'core', perm=swap))  10.1 us
    pallas_call x1, Pallas kernels, ctx_sum(): pl.pallas_call(kernel, out_shape=(jax.ShapeDtypeStruct((8, 128), jnp.floa...  9.88 us
    unnamed x14, local copies, waits for them, and re-layouts  6.72 us
  transfers between devices with their start and end apart: 4, of which 4 were waited for; matrix products, arithmetic and copies ran while one was open for 0% of the time, Pallas kernels for 46%

profile of v16, /device:TPU:0, one launch (start us, length us, event | category | flops | bytes accessed | tf_op | source)
XLA Modules:
  0.0 180.3 jit_solution(9027293216131795076)
XLA Ops:
  6.5 0.0 reduce-scatter.4.cloned.1.call-start
  7.2 0.0 copy-start.1
  7.2 1.9 %copy-done.1 = bf16[1024,1536]{1,0:T(8,128)(2,1)S(1)} copy-done((bf16[1024,1536]{1,0:T(8,128)(2,1)S(1)}, bf16[1024,1536]{1,0:T(8,128)(2,1)}, u32[]{:S(2)}) %copy-start.1) | copy-done | bytes 3145752
  9.1 0.0 copy-start.3
  9.1 0.7 copy-done.3
  9.8 0.0 copy-start.4
  9.8 0.7 copy-done.4
  10.5 0.0 copy-start.5
  10.5 0.7 copy-done.5
  11.1 9.9 %shard_map.73 = (f32[8,128]{1,0:T(8,128)S(1)}, f32[1024,1]{1,0:T(8,128)}, bf16[1536,1024]{1,0:T(8,128)(2,1)S(1)}) custom-call(f32[1,1024]{1,0:T(1,128)S(1)} %copy-done.3, f32[1,1024]{1,0:T(1,128)S(1)} %copy-done.4, s32[1,1024]{1,0:T(1,128)S(1)} %copy-done.5, s32[1]{0:T(128)S(6)} %copy.10.len_ref, bf16[1024,1536]{1,0:T(8,128)(2,1)S(1)} %copy-done.1), custom_call_target="tpu_custom_call" | custom-call | tf_op jit(solution)/shard_map/pallas_call | solution.py:205
  21.0 0.0 copy-start
  21.0 0.7 fusion
  23.7 6.7 %shard_map.75 = f32[2,16,96,512]{3,2,1,0:T(8,128)} custom-call(s32[1]{0:T(128)} %bitcast.8.col_ref, f32[1]{0:T(128)} %bitcast.5.w_ref, bf16[1024,5120]{1,0:T(8,128)(2,1)} %grad_ref.11, bf16[1536,1024]{1,0:T(8,128)(2,1)S(1)} %get-tuple-element.8.hid_ref), custom_call_target="tpu_custom_call" | custom-call | flops 3221225472 | bytes 12058624 | tf_op jit(solution)/shard_map/pallas_call | solution.py:79
  30.4 0.1 collective-permute-start.1
  30.5 6.6 %shard_map.74 = f32[2,16,96,512]{3,2,1,0:T(8,128)} custom-call(s32[1]{0:T(128)} %bitcast.6.col_ref, f32[1]{0:T(128)} %bitcast.5.w_ref, bf16[1024,5120]{1,0:T(8,128)(2,1)} %grad_ref.11, bf16[1536,1024]{1,0:T(8,128)(2,1)S(1)} %get-tuple-element.8.hid_ref), custom_call_target="tpu_custom_call" | custom-call | flops 3221225472 | bytes 12058624 | tf_op jit(solution)/shard_map/pallas_call | solution.py:79
  37.1 0.4 collective-permute-start
  37.5 3.4 %collective-permute-done.1.rest_0_ = f32[2,16,96,512]{3,2,1,0:T(8,128)} collective-permute-done((f32[2,16,96,512]{3,2,1,0:T(8,128)}, f32[2,16,96,512]{3,2,1,0:T(8,128)}, u32[]{:S(2)}, u32[]{:S(2)}) %collective-permute-start.1) | collective-permute-done | bytes 6291488 | tf_op jit(solution)/shard_map/ppermute | solution.py:259
  40.9 7.8 %shard_map.76.rest_1_ = f32[16,4,96,512]{3,2,1,0:T(8,128)} custom-call(s32[1]{0:T(128)} %bitcast.7.col_ref, f32[1]{0:T(128)} %bitcast.5.w_ref, bf16[1024,5120]{1,0:T(8,128)(2,1)} %grad_ref.11, bf16[1536,1024]{1,0:T(8,128)(2,1)S(1)} %get-tuple-element.8.hid_ref, f32[2,16,96,512]{3,2,1,0:T(8,128)} %collective-permute-done.1.rest_0_), custom_call_target="tpu_custom_call" | custom-call | flops 3221225472 | bytes 18350080 | tf_op jit(solution)/shard_map/pallas_call | solution.py:79
  48.6 1.2 collective-permute-done.rest_0_
  49.9 0.0 copy-done
  49.9 7.7 %shard_map.77 = f32[16,4,96,512]{3,2,1,0:T(8,128)} custom-call(s32[1]{0:T(128)} %bitcast.col_ref, f32[1]{0:T(128)} %bitcast.5.w_ref, bf16[1024,5120]{1,0:T(8,128)(2,1)} %grad_ref.11, bf16[1536,1024]{1,0:T(8,128)(2,1)S(1)} %get-tuple-element.8.hid_ref, f32[2,16,96,512]{3,2,1,0:T(8,128)} %collective-permute-done.rest_0_, ...), custom_call_target="tpu_custom_call", output_to_operand_aliasing={{}: (5, {})} | custom-call | flops 3221225472 | bytes 18350080 | tf_op jit(solution)/shard_map/pallas_call | solution.py:79
  57.6 0.0 reduce-scatter.4.cloned.1.call-update
  57.6 6.8 %shard_map.79 = f32[4,16,96,128]{3,2,1,0:T(8,128)S(1)} custom-call(s32[1]{0:T(128)} %bitcast.8.col_ref, f32[1]{0:T(128)} %bitcast.5.w_ref, bf16[1024,5120]{1,0:T(8,128)(2,1)} %grad_ref.11, bf16[1536,1024]{1,0:T(8,128)(2,1)} %copy-done), custom_call_target="tpu_custom_call" | custom-call | flops 1610612736 | bytes 11534336 | tf_op jit(solution)/shard_map/pallas_call | solution.py:79
  64.4 0.2 collective-permute-start.2
  64.6 5.5 %collective-permute-done.2.rest_0_ = f32[4,16,96,128]{3,2,1,0:T(8,128)S(1)} collective-permute-done((f32[4,16,96,128]{3,2,1,0:T(8,128)S(1)}, f32[4,16,96,128]{3,2,1,0:T(8,128)S(1)}, u32[]{:S(2)}, u32[]{:S(2)}) %collective-permute-start.2) | collective-permute-done | bytes 3145760 | tf_op jit(solution)/shard_map/ppermute | solution.py:259
  70.1 0.0 copy-start.6
  70.1 1.6 copy-done.6
  71.7 7.4 %shard_map.80.x_ref = f32[4,16,96,128]{3,2,1,0:T(8,128)S(1)} custom-call(s32[1]{0:T(128)} %bitcast.7.col_ref, f32[1]{0:T(128)} %bitcast.5.w_ref, bf16[1024,5120]{1,0:T(8,128)(2,1)} %grad_ref.11, bf16[1536,1024]{1,0:T(8,128)(2,1)} %copy-done, f32[4,16,96,128]{3,2,1,0:T(8,128)} %copy-done.6), custom_call_target="tpu_custom_call" | custom-call | flops 1610612736 | bytes 14680064 | tf_op jit(solution)/shard_map/pallas_call | solution.py:79
  79.2 38.3 %shard_map.81.x_ref = f32[16,96,128]{2,1,0:T(8,128)S(1)} custom-call(f32[4,16,96,128]{3,2,1,0:T(8,128)S(1)} %shard_map.80.x_ref), custom_call_target="tpu_custom_call" | custom-call | flops 786432 | bytes 9437184 | tf_op jit(solution)/shard_map/pallas_call | solution.py:128
  117.5 16.4 %shard_map.82 = f32[96,128]{1,0:T(8,128)S(1)} custom-call(f32[16,96,128]{2,1,0:T(8,128)S(1)} %shard_map.81.x_ref), custom_call_target="tpu_custom_call" | custom-call | flops 196608 | bytes 2359296 | tf_op jit(solution)/shard_map/pallas_call | solution.py:128
  134.0 24.5 %reduce-scatter.4.cloned.1.call-done = f32[1,4,96,512]{3,2,1,0:T(8,128)} async-done(((f32[16,4,96,512]{3,2,1,0:T(8,128)}), f32[1,4,96,512]{3,2,1,0:T(8,128)}) %reduce-scatter.4.cloned.1.call-update) | async-done | bytes 786448
  158.5 0.0 copy-start.2
  158.5 1.1 copy-done.2
  159.6 13.2 %shard_map.78 = f32[96,512]{1,0:T(8,128)S(1)} custom-call(f32[4,96,512]{2,1,0:T(8,128)S(1)} %bitcast.11), custom_call_target="tpu_custom_call" | custom-call | flops 196608 | bytes 2359296 | tf_op jit(solution)/shard_map/pallas_call | solution.py:128
  172.8 0.7 pad_maximum_fusion
Async XLA Ops:
  6.5 151.9 %reduce-scatter.4.cloned.1.call-start = ((), (), s32[]{:S(2)}) async-start(), calls=%async_computation.1 | async-start | bytes 13369344
  7.2 1.9 %copy-start.1 = (bf16[1024,1536]{1,0:T(8,128)(2,1)S(1)}, bf16[1024,1536]{1,0:T(8,128)(2,1)}, u32[]{:S(2)}) copy-start(bf16[1024,1536]{1,0:T(8,128)(2,1)} %hid_hbm.1) | copy-start | bytes 9437188
  9.1 0.7 copy-start.3
  9.8 0.7 copy-start.4
  10.5 0.7 copy-start.5
  21.0 28.9 %copy-start = (bf16[1536,1024]{1,0:T(8,128)(2,1)}, bf16[1536,1024]{1,0:T(8,128)(2,1)S(1)}, u32[]{:S(2)}) copy-start(bf16[1536,1024]{1,0:T(8,128)(2,1)S(1)} %get-tuple-element.8.hid_ref) | copy-start | bytes 9437188
  30.4 10.5 %collective-permute-start.1 = (f32[2,16,96,512]{3,2,1,0:T(8,128)}, f32[2,16,96,512]{3,2,1,0:T(8,128)}, u32[]{:S(2)}, u32[]{:S(2)}) collective-permute-start(f32[2,16,96,512]{3,2,1,0:T(8,128)} %shard_map.75), channel_id=1, source_target_pairs={{0,1},{1,0},{2,3},{3,2},{4,5},{5,4},{6,7},{7,6},{8,9},{9,8},{10,11... | collective-permute-start | bytes 18874376 | tf_op jit(solution)/shard_map/ppermute | solution.py:259
  37.1 12.8 %collective-permute-start = (f32[2,16,96,512]{3,2,1,0:T(8,128)}, f32[2,16,96,512]{3,2,1,0:T(8,128)}, u32[]{:S(2)}, u32[]{:S(2)}) collective-permute-start(f32[2,16,96,512]{3,2,1,0:T(8,128)} %shard_map.74), channel_id=1, source_target_pairs={{0,1},{1,0},{2,3},{3,2},{4,5},{5,4},{6,7},{7,6},{8,9},{9,8},{10,11... | collective-permute-start | bytes 18874376 | tf_op jit(solution)/shard_map/ppermute | solution.py:259
  64.4 5.7 %collective-permute-start.2 = (f32[4,16,96,128]{3,2,1,0:T(8,128)S(1)}, f32[4,16,96,128]{3,2,1,0:T(8,128)S(1)}, u32[]{:S(2)}, u32[]{:S(2)}) collective-permute-start(f32[4,16,96,128]{3,2,1,0:T(8,128)S(1)} %shard_map.79), channel_id=1, source_target_pairs={{0,1},{1,0},{2,3},{3,2},{4,5},{5,4},{6,7},{7,6},{8,9},{9,8},{10,11... | collective-permute-start | bytes 9437192 | tf_op jit(solution)/shard_map/ppermute | solution.py:259
  70.1 1.6 copy-start.6
  158.5 1.1 copy-start.2
Sparse Core Ops, SparseCore 0:
  57.7 100.7 reduce-scatter.3

commit v17 on v16

--- a/solution.py
+++ b/solution.py
@@ -171,12 +171,15 @@
         live_hid = live_col.astype(hid_ref.dtype)
 
         fetch.wait()
-
-        @pl.loop(0, hb // 128)
-        def _(j):
-            cols = pl.ds(pl.multiple_of(j * 128, 128), 128)
-            ht_ref[cols, :] = (hid_ref[:, cols] * live_hid).T
-
+        chunks = hb // 128
+
+        def transpose(first, last):
+            @pl.loop(first, last)
+            def _(j):
+                cols = pl.ds(pl.multiple_of(j * 128, 128), 128)
+                ht_ref[cols, :] = (hid_ref[:, cols] * live_hid).T
+
+        transpose(0, chunks // 2)
         local.wait()
         pl.semaphore_wait(barrier, n - 1)
         copies = []
@@ -188,6 +191,7 @@
             cp.start()
             copies.append(cp)
         recv[me] = staged[...]
+        transpose(chunks // 2, chunks)
         for d in range(1, n):
             src = lax.rem(me + n - d, n)
             pltpu.make_async_remote_copy(

time: 181 us -> 179 us (0.989)
  Pallas kernels: 121 us -> 119 us
where the time goes in v17:
time: 179 us
  Pallas kernels  119 us (66%)
  waiting for transfers between devices  34.7 us (19%)
  between operations  16.1 us (9%)
  local copies, waits for them, and re-layouts  7.4 us (4%)
    pallas_call x3, Pallas kernels, z_reduce_scatter(): pl.pallas_call(kernel, out_shape=jax.ShapeDtypeStruct(rest_shape, jnp.flo...  67.8 us
    pallas_call x6, Pallas kernels, block_matmul(): pl.pallas_call(kernel, grid_spec=grid_spec, out_shape=out_shape, input_ou...  42.9 us
    unnamed x2, waiting for transfers between devices  24.6 us
    ppermute x3, waiting for transfers between devices, pre_reduced(): got.append(lax.ppermute(theirs, 'core', perm=swap))  10.1 us
    pallas_call x1, Pallas kernels, ctx_sum(): pl.pallas_call(kernel, out_shape=(jax.ShapeDtypeStruct((8, 128), jnp.floa...  8.64 us
    unnamed x14, local copies, waits for them, and re-layouts  6.72 us
  transfers between devices with their start and end apart: 4, of which 4 were waited for; matrix products, arithmetic and copies ran while one was open for 0% of the time, Pallas kernels for 46%

profile of v17, /device:TPU:0, one launch (start us, length us, event | category | flops | bytes accessed | tf_op | source)
XLA Modules:
  0.0 179.0 jit_solution(1951674858404042325)
XLA Ops:
  6.5 0.0 reduce-scatter.4.cloned.1.call-start
  7.2 0.0 copy-start.1
  7.2 1.9 %copy-done.1 = bf16[1024,1536]{1,0:T(8,128)(2,1)S(1)} copy-done((bf16[1024,1536]{1,0:T(8,128)(2,1)S(1)}, bf16[1024,1536]{1,0:T(8,128)(2,1)}, u32[]{:S(2)}) %copy-start.1) | copy-done | bytes 3145752
  9.1 0.0 copy-start.3
  9.1 0.7 copy-done.3
  9.8 0.0 copy-start.4
  9.8 0.7 copy-done.4
  10.5 0.0 copy-start.5
  10.5 0.7 copy-done.5
  11.1 8.6 %shard_map.73 = (f32[8,128]{1,0:T(8,128)S(1)}, f32[1024,1]{1,0:T(8,128)}, bf16[1536,1024]{1,0:T(8,128)(2,1)S(1)}) custom-call(f32[1,1024]{1,0:T(1,128)S(1)} %copy-done.3, f32[1,1024]{1,0:T(1,128)S(1)} %copy-done.4, s32[1,1024]{1,0:T(1,128)S(1)} %copy-done.5, s32[1]{0:T(128)S(6)} %copy.10.len_ref, bf16[1024,1536]{1,0:T(8,128)(2,1)S(1)} %copy-done.1), custom_call_target="tpu_custom_call" | custom-call | tf_op jit(solution)/shard_map/pallas_call | solution.py:209
  19.8 0.0 copy-start
  19.8 0.7 fusion
  22.5 6.7 %shard_map.75 = f32[2,16,96,512]{3,2,1,0:T(8,128)} custom-call(s32[1]{0:T(128)} %bitcast.8.col_ref, f32[1]{0:T(128)} %bitcast.5.w_ref, bf16[1024,5120]{1,0:T(8,128)(2,1)} %grad_ref.11, bf16[1536,1024]{1,0:T(8,128)(2,1)S(1)} %get-tuple-element.8.hid_ref), custom_call_target="tpu_custom_call" | custom-call | flops 3221225472 | bytes 12058624 | tf_op jit(solution)/shard_map/pallas_call | solution.py:79
  29.1 0.1 collective-permute-start.1
  29.3 6.6 %shard_map.74 = f32[2,16,96,512]{3,2,1,0:T(8,128)} custom-call(s32[1]{0:T(128)} %bitcast.6.col_ref, f32[1]{0:T(128)} %bitcast.5.w_ref, bf16[1024,5120]{1,0:T(8,128)(2,1)} %grad_ref.11, bf16[1536,1024]{1,0:T(8,128)(2,1)S(1)} %get-tuple-element.8.hid_ref), custom_call_target="tpu_custom_call" | custom-call | flops 3221225472 | bytes 12058624 | tf_op jit(solution)/shard_map/pallas_call | solution.py:79
  35.9 0.4 collective-permute-start
  36.3 3.4 %collective-permute-done.1.rest_0_ = f32[2,16,96,512]{3,2,1,0:T(8,128)} collective-permute-done((f32[2,16,96,512]{3,2,1,0:T(8,128)}, f32[2,16,96,512]{3,2,1,0:T(8,128)}, u32[]{:S(2)}, u32[]{:S(2)}) %collective-permute-start.1) | collective-permute-done | bytes 6291488 | tf_op jit(solution)/shard_map/ppermute | solution.py:263
  39.6 7.8 %shard_map.76.rest_1_ = f32[16,4,96,512]{3,2,1,0:T(8,128)} custom-call(s32[1]{0:T(128)} %bitcast.7.col_ref, f32[1]{0:T(128)} %bitcast.5.w_ref, bf16[1024,5120]{1,0:T(8,128)(2,1)} %grad_ref.11, bf16[1536,1024]{1,0:T(8,128)(2,1)S(1)} %get-tuple-element.8.hid_ref, f32[2,16,96,512]{3,2,1,0:T(8,128)} %collective-permute-done.1.rest_0_), custom_call_target="tpu_custom_call" | custom-call | flops 3221225472 | bytes 18350080 | tf_op jit(solution)/shard_map/pallas_call | solution.py:79
  47.4 1.2 collective-permute-done.rest_0_
  48.6 0.0 copy-done
  48.6 7.7 %shard_map.77 = f32[16,4,96,512]{3,2,1,0:T(8,128)} custom-call(s32[1]{0:T(128)} %bitcast.col_ref, f32[1]{0:T(128)} %bitcast.5.w_ref, bf16[1024,5120]{1,0:T(8,128)(2,1)} %grad_ref.11, bf16[1536,1024]{1,0:T(8,128)(2,1)S(1)} %get-tuple-element.8.hid_ref, f32[2,16,96,512]{3,2,1,0:T(8,128)} %collective-permute-done.rest_0_, ...), custom_call_target="tpu_custom_call", output_to_operand_aliasing={{}: (5, {})} | custom-call | flops 3221225472 | bytes 18350080 | tf_op jit(solution)/shard_map/pallas_call | solution.py:79
  56.3 0.0 reduce-scatter.4.cloned.1.call-update
  56.3 6.8 %shard_map.79 = f32[4,16,96,128]{3,2,1,0:T(8,128)S(1)} custom-call(s32[1]{0:T(128)} %bitcast.8.col_ref, f32[1]{0:T(128)} %bitcast.5.w_ref, bf16[1024,5120]{1,0:T(8,128)(2,1)} %grad_ref.11, bf16[1536,1024]{1,0:T(8,128)(2,1)} %copy-done), custom_call_target="tpu_custom_call" | custom-call | flops 1610612736 | bytes 11534336 | tf_op jit(solution)/shard_map/pallas_call | solution.py:79
  63.1 0.2 collective-permute-start.2
  63.3 5.5 %collective-permute-done.2.rest_0_ = f32[4,16,96,128]{3,2,1,0:T(8,128)S(1)} collective-permute-done((f32[4,16,96,128]{3,2,1,0:T(8,128)S(1)}, f32[4,16,96,128]{3,2,1,0:T(8,128)S(1)}, u32[]{:S(2)}, u32[]{:S(2)}) %collective-permute-start.2) | collective-permute-done | bytes 3145760 | tf_op jit(solution)/shard_map/ppermute | solution.py:263
  68.9 0.0 copy-start.6
  68.9 1.6 copy-done.6
  70.5 7.4 %shard_map.80.x_ref = f32[4,16,96,128]{3,2,1,0:T(8,128)S(1)} custom-call(s32[1]{0:T(128)} %bitcast.7.col_ref, f32[1]{0:T(128)} %bitcast.5.w_ref, bf16[1024,5120]{1,0:T(8,128)(2,1)} %grad_ref.11, bf16[1536,1024]{1,0:T(8,128)(2,1)} %copy-done, f32[4,16,96,128]{3,2,1,0:T(8,128)} %copy-done.6), custom_call_target="tpu_custom_call" | custom-call | flops 1610612736 | bytes 14680064 | tf_op jit(solution)/shard_map/pallas_call | solution.py:79
  77.9 38.4 %shard_map.81.x_ref = f32[16,96,128]{2,1,0:T(8,128)S(1)} custom-call(f32[4,16,96,128]{3,2,1,0:T(8,128)S(1)} %shard_map.80.x_ref), custom_call_target="tpu_custom_call" | custom-call | flops 786432 | bytes 9437184 | tf_op jit(solution)/shard_map/pallas_call | solution.py:128
  116.3 16.3 %shard_map.82 = f32[96,128]{1,0:T(8,128)S(1)} custom-call(f32[16,96,128]{2,1,0:T(8,128)S(1)} %shard_map.81.x_ref), custom_call_target="tpu_custom_call" | custom-call | flops 196608 | bytes 2359296 | tf_op jit(solution)/shard_map/pallas_call | solution.py:128
  132.6 24.6 %reduce-scatter.4.cloned.1.call-done = f32[1,4,96,512]{3,2,1,0:T(8,128)} async-done(((f32[16,4,96,512]{3,2,1,0:T(8,128)}), f32[1,4,96,512]{3,2,1,0:T(8,128)}) %reduce-scatter.4.cloned.1.call-update) | async-done | bytes 786448
  157.2 0.0 copy-start.2
  157.2 1.1 copy-done.2
  158.3 13.1 %shard_map.78 = f32[96,512]{1,0:T(8,128)S(1)} custom-call(f32[4,96,512]{2,1,0:T(8,128)S(1)} %bitcast.11), custom_call_target="tpu_custom_call" | custom-call | flops 196608 | bytes 2359296 | tf_op jit(solution)/shard_map/pallas_call | solution.py:128
  171.5 0.7 pad_maximum_fusion
Async XLA Ops:
  6.5 150.7 %reduce-scatter.4.cloned.1.call-start = ((), (), s32[]{:S(2)}) async-start(), calls=%async_computation.1 | async-start | bytes 13369344
  7.2 1.9 %copy-start.1 = (bf16[1024,1536]{1,0:T(8,128)(2,1)S(1)}, bf16[1024,1536]{1,0:T(8,128)(2,1)}, u32[]{:S(2)}) copy-start(bf16[1024,1536]{1,0:T(8,128)(2,1)} %hid_hbm.1) | copy-start | bytes 9437188
  9.1 0.7 copy-start.3
  9.8 0.7 copy-start.4
  10.5 0.7 copy-start.5
  19.8 28.9 %copy-start = (bf16[1536,1024]{1,0:T(8,128)(2,1)}, bf16[1536,1024]{1,0:T(8,128)(2,1)S(1)}, u32[]{:S(2)}) copy-start(bf16[1536,1024]{1,0:T(8,128)(2,1)S(1)} %get-tuple-element.8.hid_ref) | copy-start | bytes 9437188
  29.1 10.5 %collective-permute-start.1 = (f32[2,16,96,512]{3,2,1,0:T(8,128)}, f32[2,16,96,512]{3,2,1,0:T(8,128)}, u32[]{:S(2)}, u32[]{:S(2)}) collective-permute-start(f32[2,16,96,512]{3,2,1,0:T(8,128)} %shard_map.75), channel_id=1, source_target_pairs={{0,1},{1,0},{2,3},{3,2},{4,5},{5,4},{6,7},{7,6},{8,9},{9,8},{10,11... | collective-permute-start | bytes 18874376 | tf_op jit(solution)/shard_map/ppermute | solution.py:263
  35.9 12.8 %collective-permute-start = (f32[2,16,96,512]{3,2,1,0:T(8,128)}, f32[2,16,96,512]{3,2,1,0:T(8,128)}, u32[]{:S(2)}, u32[]{:S(2)}) collective-permute-start(f32[2,16,96,512]{3,2,1,0:T(8,128)} %shard_map.74), channel_id=1, source_target_pairs={{0,1},{1,0},{2,3},{3,2},{4,5},{5,4},{6,7},{7,6},{8,9},{9,8},{10,11... | collective-permute-start | bytes 18874376 | tf_op jit(solution)/shard_map/ppermute | solution.py:263
  63.1 5.7 %collective-permute-start.2 = (f32[4,16,96,128]{3,2,1,0:T(8,128)S(1)}, f32[4,16,96,128]{3,2,1,0:T(8,128)S(1)}, u32[]{:S(2)}, u32[]{:S(2)}) collective-permute-start(f32[4,16,96,128]{3,2,1,0:T(8,128)S(1)} %shard_map.79), channel_id=1, source_target_pairs={{0,1},{1,0},{2,3},{3,2},{4,5},{5,4},{6,7},{7,6},{8,9},{9,8},{10,11... | collective-permute-start | bytes 9437192 | tf_op jit(solution)/shard_map/ppermute | solution.py:263
  68.9 1.6 copy-start.6
  157.2 1.1 copy-start.2
Sparse Core Ops, SparseCore 0:
  56.5 100.6 reduce-scatter.3

commit v18 on v17

--- a/solution.py
+++ b/solution.py
@@ -144,9 +144,14 @@
     n = n_z * n_core
     t, hb = hidden.shape
 
-    def kernel(new_ref, old_ref, mask_ref, len_ref, hid_hbm, out_ref, live_ref, ht_ref,
-               hid_ref, mine, staged, recv, hid_sem, copy_sem, send_sem, recv_sem):
+    def kernel(new_hbm, old_hbm, mask_hbm, len_ref, hid_hbm, out_ref, live_ref, ht_ref,
+               hid_ref, new_ref, old_ref, mask_ref, mine, staged, recv, hid_sem, row_sem,
+               copy_sem, send_sem, recv_sem):
         me = lax.axis_index("z") * n_core + lax.axis_index("core")
+        rows = [pltpu.make_async_copy(a, b, row_sem.at[i]) for i, (a, b) in enumerate(
+            ((new_hbm, new_ref), (old_hbm, old_ref), (mask_hbm, mask_ref)))]
+        for cp in rows:
+            cp.start()
         fetch = pltpu.make_async_copy(hid_hbm, hid_ref, hid_sem)
         fetch.start()
 
@@ -157,6 +162,8 @@
         for d in range(1, n):
             pl.semaphore_signal(barrier, inc=1, device_id=peer_of(lax.rem(me + d, n)),
                                 device_id_type=pl.DeviceIdType.MESH)
+        for cp in rows:
+            cp.wait()
         places = me * t + lax.broadcasted_iota(jnp.int32, (8, t), 1)
         mask8 = jnp.broadcast_to(mask_ref[...], (8, t))
         live = jnp.where(places < len_ref[0], mask8, 0).astype(jnp.float32)
@@ -211,21 +218,25 @@
         out_shape=(jax.ShapeDtypeStruct((8, 128), jnp.float32),
                    jax.ShapeDtypeStruct((t, 1), jnp.float32),
                    jax.ShapeDtypeStruct((hb, t), hidden.dtype)),
-        in_specs=[vmem, vmem, vmem, pl.BlockSpec(memory_space=pltpu.SMEM),
-                  pl.BlockSpec(memory_space=pl.ANY)],
+        in_specs=[pl.BlockSpec(memory_space=pl.ANY)] * 3 + [
+            pl.BlockSpec(memory_space=pltpu.SMEM), pl.BlockSpec(memory_space=pl.ANY)],
         out_specs=(vmem, vmem, vmem),
         scratch_shapes=[
             pltpu.VMEM((t, hb), hidden.dtype),
+            pltpu.VMEM(new_lp.shape, new_lp.dtype),
+            pltpu.VMEM(old_lp.shape, old_lp.dtype),
+            pltpu.VMEM(mask.shape, mask.dtype),
             pltpu.VMEM((8, 128), jnp.float32),
             pltpu.VMEM((8, 128), jnp.float32),
             pltpu.VMEM((n, 8, 128), jnp.float32),
             pltpu.SemaphoreType.DMA,
+            pltpu.SemaphoreType.DMA((3,)),
             pltpu.SemaphoreType.DMA,
             pltpu.SemaphoreType.DMA((n,)),
             pltpu.SemaphoreType.DMA((n,)),
         ],
         compiler_params=pltpu.CompilerParams(
-            collective_id=1, has_side_effects=True, vmem_limit_bytes=32 * 1024 * 1024),
+            collective_id=1, has_side_effects=True, vmem_limit_bytes=64 * 1024 * 1024),
     )(new_lp, old_lp, mask, roll_len, hidden)
 
 

time: 179 us -> 180 us (level)
  Pallas kernels: 119 us -> 122 us
    pallas_call x1, Pallas kernels: 8.64 us -> 11 us  [ctx_sum(): pl.pallas_call(kernel, out_shape=(jax.ShapeDtypeStruct((8, 128), jnp.floa...]
    unnamed x14 -> x8, local copies, waits for them, and re-layouts: 6.72 us -> 4.65 us
where the time goes in v18:
time: 180 us
  Pallas kernels  122 us (68%)
  waiting for transfers between devices  34.8 us (19%)
  between operations  16.1 us (9%)
  local copies, waits for them, and re-layouts  5.98 us (3%)
    pallas_call x3, Pallas kernels, z_reduce_scatter(): pl.pallas_call(kernel, out_shape=jax.ShapeDtypeStruct(rest_shape, jnp.flo...  67.7 us
    pallas_call x6, Pallas kernels, block_matmul(): pl.pallas_call(kernel, grid_spec=grid_spec, out_shape=out_shape, input_ou...  43 us
    unnamed x2, waiting for transfers between devices  24.6 us
    pallas_call x1, Pallas kernels, ctx_sum(): pl.pallas_call(kernel, out_shape=(jax.ShapeDtypeStruct((8, 128), jnp.floa...  11 us
    ppermute x3, waiting for transfers between devices, pre_reduced(): got.append(lax.ppermute(theirs, 'core', perm=swap))  10.2 us
    unnamed x8, local copies, waits for them, and re-layouts  4.65 us
  transfers between devices with their start and end apart: 4, of which 4 were waited for; matrix products, arithmetic and copies ran while one was open for 0% of the time, Pallas kernels for 46%

profile of v18, /device:TPU:0, one launch (start us, length us, event | category | flops | bytes accessed | tf_op | source)
XLA Modules:
  0.0 180.0 jit_solution(11187952821173731578)
XLA Ops:
  6.5 0.0 reduce-scatter.4.cloned.1.call-start
  7.2 11.0 %shard_map.73 = (f32[8,128]{1,0:T(8,128)}, f32[1024,1]{1,0:T(8,128)}, bf16[1536,1024]{1,0:T(8,128)(2,1)}) custom-call(f32[1,1024]{1,0:T(1,128)} %new_hbm.1, f32[1,1024]{1,0:T(1,128)} %old_hbm.1, s32[1,1024]{1,0:T(1,128)} %mask_hbm.1, s32[1]{0:T(128)S(6)} %copy.10.len_ref, bf16[1024,1536]{1,0:T(8,128)(2,1)} %hid_hbm.1), custom_call_target="tpu_custom_call" | custom-call | tf_op jit(solution)/shard_map/pallas_call | solution.py:216
  18.2 1.3 fusion
  21.5 0.0 copy-start
  21.5 1.9 %copy-done = bf16[1536,1024]{1,0:T(8,128)(2,1)S(1)} copy-done((bf16[1536,1024]{1,0:T(8,128)(2,1)S(1)}, bf16[1536,1024]{1,0:T(8,128)(2,1)}, u32[]{:S(2)}) %copy-start) | copy-done | bytes 3145752
  23.4 0.0 copy-start.1
  23.4 6.8 %shard_map.75 = f32[2,16,96,512]{3,2,1,0:T(8,128)} custom-call(s32[1]{0:T(128)} %bitcast.8.col_ref, f32[1]{0:T(128)} %bitcast.5.w_ref, bf16[1024,5120]{1,0:T(8,128)(2,1)} %grad_ref.11, bf16[1536,1024]{1,0:T(8,128)(2,1)S(1)} %copy-done), custom_call_target="tpu_custom_call" | custom-call | flops 3221225472 | bytes 12058624 | tf_op jit(solution)/shard_map/pallas_call | solution.py:79
  30.2 0.1 collective-permute-start.1
  30.3 0.0 copy-done.1
  30.3 6.6 %shard_map.74 = f32[2,16,96,512]{3,2,1,0:T(8,128)} custom-call(s32[1]{0:T(128)} %bitcast.6.col_ref, f32[1]{0:T(128)} %bitcast.5.w_ref, bf16[1024,5120]{1,0:T(8,128)(2,1)} %grad_ref.11, bf16[1536,1024]{1,0:T(8,128)(2,1)S(1)} %copy-done.1), custom_call_target="tpu_custom_call" | custom-call | flops 3221225472 | bytes 12058624 | tf_op jit(solution)/shard_map/pallas_call | solution.py:79
  37.0 0.4 collective-permute-start
  37.4 3.4 %collective-permute-done.1.rest_0_ = f32[2,16,96,512]{3,2,1,0:T(8,128)} collective-permute-done((f32[2,16,96,512]{3,2,1,0:T(8,128)}, f32[2,16,96,512]{3,2,1,0:T(8,128)}, u32[]{:S(2)}, u32[]{:S(2)}) %collective-permute-start.1) | collective-permute-done | bytes 6291488 | tf_op jit(solution)/shard_map/ppermute | solution.py:274
  40.7 7.7 %shard_map.76.rest_1_ = f32[16,4,96,512]{3,2,1,0:T(8,128)} custom-call(s32[1]{0:T(128)} %bitcast.7.col_ref, f32[1]{0:T(128)} %bitcast.5.w_ref, bf16[1024,5120]{1,0:T(8,128)(2,1)} %grad_ref.11, bf16[1536,1024]{1,0:T(8,128)(2,1)S(1)} %copy-done.1, f32[2,16,96,512]{3,2,1,0:T(8,128)} %collective-permute-done.1.rest_0_), custom_call_target="tpu_custom_call" | custom-call | flops 3221225472 | bytes 18350080 | tf_op jit(solution)/shard_map/pallas_call | solution.py:79
  48.4 1.3 collective-permute-done.rest_0_
  49.7 7.6 %shard_map.77 = f32[16,4,96,512]{3,2,1,0:T(8,128)} custom-call(s32[1]{0:T(128)} %bitcast.col_ref, f32[1]{0:T(128)} %bitcast.5.w_ref, bf16[1024,5120]{1,0:T(8,128)(2,1)} %grad_ref.11, bf16[1536,1024]{1,0:T(8,128)(2,1)S(1)} %copy-done.1, f32[2,16,96,512]{3,2,1,0:T(8,128)} %collective-permute-done.rest_0_, ...), custom_call_target="tpu_custom_call", output_to_operand_aliasing={{}: (5, {})} | custom-call | flops 3221225472 | bytes 18350080 | tf_op jit(solution)/shard_map/pallas_call | solution.py:79
  57.3 0.0 reduce-scatter.4.cloned.1.call-update
  57.4 6.8 %shard_map.79 = f32[4,16,96,128]{3,2,1,0:T(8,128)S(1)} custom-call(s32[1]{0:T(128)} %bitcast.8.col_ref, f32[1]{0:T(128)} %bitcast.5.w_ref, bf16[1024,5120]{1,0:T(8,128)(2,1)} %grad_ref.11, bf16[1536,1024]{1,0:T(8,128)(2,1)} %get-tuple-element.8.hid_ref), custom_call_target="tpu_custom_call" | custom-call | flops 1610612736 | bytes 11534336 | tf_op jit(solution)/shard_map/pallas_call | solution.py:79
  64.1 0.2 collective-permute-start.2
  64.4 5.5 %collective-permute-done.2.rest_0_ = f32[4,16,96,128]{3,2,1,0:T(8,128)S(1)} collective-permute-done((f32[4,16,96,128]{3,2,1,0:T(8,128)S(1)}, f32[4,16,96,128]{3,2,1,0:T(8,128)S(1)}, u32[]{:S(2)}, u32[]{:S(2)}) %collective-permute-start.2) | collective-permute-done | bytes 3145760 | tf_op jit(solution)/shard_map/ppermute | solution.py:274
  69.9 0.0 copy-start.3
  69.9 1.6 copy-done.3
  71.5 7.4 %shard_map.80.x_ref = f32[4,16,96,128]{3,2,1,0:T(8,128)S(1)} custom-call(s32[1]{0:T(128)} %bitcast.7.col_ref, f32[1]{0:T(128)} %bitcast.5.w_ref, bf16[1024,5120]{1,0:T(8,128)(2,1)} %grad_ref.11, bf16[1536,1024]{1,0:T(8,128)(2,1)} %get-tuple-element.8.hid_ref, f32[4,16,96,128]{3,2,1,0:T(8,128)} %copy-done.3), custom_call_target="tpu_custom_call" | custom-call | flops 1610612736 | bytes 14680064 | tf_op jit(solution)/shard_map/pallas_call | solution.py:79
  79.0 38.3 %shard_map.81.x_ref = f32[16,96,128]{2,1,0:T(8,128)S(1)} custom-call(f32[4,16,96,128]{3,2,1,0:T(8,128)S(1)} %shard_map.80.x_ref), custom_call_target="tpu_custom_call" | custom-call | flops 786432 | bytes 9437184 | tf_op jit(solution)/shard_map/pallas_call | solution.py:128
  117.3 16.2 %shard_map.82 = f32[96,128]{1,0:T(8,128)S(1)} custom-call(f32[16,96,128]{2,1,0:T(8,128)S(1)} %shard_map.81.x_ref), custom_call_target="tpu_custom_call" | custom-call | flops 196608 | bytes 2359296 | tf_op jit(solution)/shard_map/pallas_call | solution.py:128
  133.5 24.6 %reduce-scatter.4.cloned.1.call-done = f32[1,4,96,512]{3,2,1,0:T(8,128)} async-done(((f32[16,4,96,512]{3,2,1,0:T(8,128)}), f32[1,4,96,512]{3,2,1,0:T(8,128)}) %reduce-scatter.4.cloned.1.call-update) | async-done | bytes 786448
  158.1 0.0 copy-start.2
  158.1 1.1 copy-done.2
  159.2 13.2 %shard_map.78 = f32[96,512]{1,0:T(8,128)S(1)} custom-call(f32[4,96,512]{2,1,0:T(8,128)S(1)} %bitcast.11), custom_call_target="tpu_custom_call" | custom-call | flops 196608 | bytes 2359296 | tf_op jit(solution)/shard_map/pallas_call | solution.py:128
  172.4 0.7 pad_maximum_fusion
Async XLA Ops:
  6.5 151.6 %reduce-scatter.4.cloned.1.call-start = ((), (), s32[]{:S(2)}) async-start(), calls=%async_computation.1 | async-start | bytes 13369344
  21.5 1.9 %copy-start = (bf16[1536,1024]{1,0:T(8,128)(2,1)S(1)}, bf16[1536,1024]{1,0:T(8,128)(2,1)}, u32[]{:S(2)}) copy-start(bf16[1536,1024]{1,0:T(8,128)(2,1)} %get-tuple-element.8.hid_ref) | copy-start | bytes 9437188
  23.4 6.9 %copy-start.1 = (bf16[1536,1024]{1,0:T(8,128)(2,1)S(1)}, bf16[1536,1024]{1,0:T(8,128)(2,1)}, u32[]{:S(2)}) copy-start(bf16[1536,1024]{1,0:T(8,128)(2,1)} %get-tuple-element.8.hid_ref) | copy-start | bytes 9437188
  30.2 10.5 %collective-permute-start.1 = (f32[2,16,96,512]{3,2,1,0:T(8,128)}, f32[2,16,96,512]{3,2,1,0:T(8,128)}, u32[]{:S(2)}, u32[]{:S(2)}) collective-permute-start(f32[2,16,96,512]{3,2,1,0:T(8,128)} %shard_map.75), channel_id=1, source_target_pairs={{0,1},{1,0},{2,3},{3,2},{4,5},{5,4},{6,7},{7,6},{8,9},{9,8},{10,11... | collective-permute-start | bytes 18874376 | tf_op jit(solution)/shard_map/ppermute | solution.py:274
  37.0 12.7 %collective-permute-start = (f32[2,16,96,512]{3,2,1,0:T(8,128)}, f32[2,16,96,512]{3,2,1,0:T(8,128)}, u32[]{:S(2)}, u32[]{:S(2)}) collective-permute-start(f32[2,16,96,512]{3,2,1,0:T(8,128)} %shard_map.74), channel_id=1, source_target_pairs={{0,1},{1,0},{2,3},{3,2},{4,5},{5,4},{6,7},{7,6},{8,9},{9,8},{10,11... | collective-permute-start | bytes 18874376 | tf_op jit(solution)/shard_map/ppermute | solution.py:274
  64.1 5.7 %collective-permute-start.2 = (f32[4,16,96,128]{3,2,1,0:T(8,128)S(1)}, f32[4,16,96,128]{3,2,1,0:T(8,128)S(1)}, u32[]{:S(2)}, u32[]{:S(2)}) collective-permute-start(f32[4,16,96,128]{3,2,1,0:T(8,128)S(1)} %shard_map.79), channel_id=1, source_target_pairs={{0,1},{1,0},{2,3},{3,2},{4,5},{5,4},{6,7},{7,6},{8,9},{9,8},{10,11... | collective-permute-start | bytes 9437192 | tf_op jit(solution)/shard_map/ppermute | solution.py:274
  69.9 1.6 copy-start.3
  158.1 1.1 copy-start.2
Sparse Core Ops, SparseCore 0:
  57.5 100.5 reduce-scatter.3

commit v19 on v17

--- a/solution.py
+++ b/solution.py
@@ -89,14 +89,17 @@
     )(*args)
 
 
-def z_reduce_scatter(x, axis, n, cid):
+def z_reduce_scatter(x, axis, n, cid, in_place=False):
     rest_shape = x.shape[1:]
     size = 1
     for s in x.shape:
         size *= s
 
-    def kernel(x_ref, out_ref, recv, send_sem, recv_sem):
+    def kernel(x_ref, out_ref, recv, own, own_sem, send_sem, recv_sem):
         me = lax.axis_index(axis)
+        if in_place:
+            fetch = pltpu.make_async_copy(x_ref.at[me], own, own_sem)
+            fetch.start()
         barrier = pltpu.get_barrier_semaphore()
         for d in range(1, n):
             peer = lax.rem(me + d, n)
@@ -112,7 +115,11 @@
                 device_id={axis: peer}, device_id_type=pl.DeviceIdType.MESH)
             cp.start()
             copies.append(cp)
-        total = x_ref[me]
+        if in_place:
+            fetch.wait()
+            total = own[...]
+        else:
+            total = x_ref[me]
         for d in range(1, n):
             src = lax.rem(me + n - d, n)
             incoming = pltpu.make_async_remote_copy(
@@ -128,15 +135,18 @@
     return pl.pallas_call(
         kernel,
         out_shape=jax.ShapeDtypeStruct(rest_shape, jnp.float32),
-        in_specs=[pl.BlockSpec(memory_space=pltpu.VMEM)],
+        in_specs=[pl.BlockSpec(memory_space=pl.ANY if in_place else pltpu.VMEM)],
         out_specs=pl.BlockSpec(memory_space=pltpu.VMEM),
         scratch_shapes=[
             pltpu.VMEM(x.shape, jnp.float32),
+            pltpu.VMEM(rest_shape, jnp.float32),
+            pltpu.SemaphoreType.DMA,
             pltpu.SemaphoreType.DMA((n,)),
             pltpu.SemaphoreType.DMA((n,)),
         ],
         compiler_params=pltpu.CompilerParams(
-            collective_id=cid, has_side_effects=True, vmem_limit_bytes=40 * 1024 * 1024),
+            collective_id=cid, has_side_effects=True,
+            vmem_limit_bytes=(64 if in_place else 40) * 1024 * 1024),
         cost_estimate=pl.CostEstimate(flops=size, transcendentals=0, bytes_accessed=3 * size * 4),
     )(x)
 
@@ -274,7 +284,7 @@
     z_first = pre_reduced(keep, col, True, n_z)
     late = z_reduce_scatter(z_first, "z", n_z, 0)
     late = z_reduce_scatter(late, "dp", n_dp, 2)
-    early = z_reduce_scatter(rows, "z", n_z, 3)
+    early = z_reduce_scatter(rows, "z", n_z, 3, in_place=True)
     return jnp.concatenate([early, late], axis=1)
 
 

time: 179 us -> 180 us (level)
  no operation moved by 1% of the time
where the time goes in v19:
time: 180 us
  Pallas kernels  120 us (67%)
  waiting for transfers between devices  34.1 us (19%)
  between operations  16.1 us (9%)
  local copies, waits for them, and re-layouts  6.88 us (4%)
    pallas_call x3, Pallas kernels, z_reduce_scatter(): pl.pallas_call(kernel, out_shape=jax.ShapeDtypeStruct(rest_shape, jnp.flo...  68.7 us
    pallas_call x6, Pallas kernels, block_matmul(): pl.pallas_call(kernel, grid_spec=grid_spec, out_shape=out_shape, input_ou...  42.9 us
    unnamed x2, waiting for transfers between devices  24 us
    ppermute x3, waiting for transfers between devices, pre_reduced(): got.append(lax.ppermute(theirs, 'core', perm=swap))  10.1 us
    pallas_call x1, Pallas kernels, ctx_sum(): pl.pallas_call(kernel, out_shape=(jax.ShapeDtypeStruct((8, 128), jnp.floa...  8.64 us
    unnamed x14, local copies, waits for them, and re-layouts  6.2 us
  transfers between devices with their start and end apart: 4, of which 4 were waited for; matrix products, arithmetic and copies ran while one was open for 0% of the time, Pallas kernels for 46%

profile of v19, /device:TPU:0, one launch (start us, length us, event | category | flops | bytes accessed | tf_op | source)
XLA Modules:
  0.0 179.7 jit_solution(4777568890937765187)
XLA Ops:
  6.5 0.0 reduce-scatter.4.cloned.1.call-start
  7.2 0.0 copy-start.1
  7.2 1.9 %copy-done.1 = bf16[1024,1536]{1,0:T(8,128)(2,1)S(1)} copy-done((bf16[1024,1536]{1,0:T(8,128)(2,1)S(1)}, bf16[1024,1536]{1,0:T(8,128)(2,1)}, u32[]{:S(2)}) %copy-start.1) | copy-done | bytes 3145752
  9.1 0.0 copy-start.3
  9.1 0.7 copy-done.3
  9.8 0.0 copy-start.4
  9.8 0.7 copy-done.4
  10.5 0.0 copy-start.5
  10.5 0.7 copy-done.5
  11.1 8.6 %shard_map.73 = (f32[8,128]{1,0:T(8,128)S(1)}, f32[1024,1]{1,0:T(8,128)}, bf16[1536,1024]{1,0:T(8,128)(2,1)S(1)}) custom-call(f32[1,1024]{1,0:T(1,128)S(1)} %copy-done.3, f32[1,1024]{1,0:T(1,128)S(1)} %copy-done.4, s32[1,1024]{1,0:T(1,128)S(1)} %copy-done.5, s32[1]{0:T(128)S(6)} %copy.10.len_ref, bf16[1024,1536]{1,0:T(8,128)(2,1)S(1)} %copy-done.1), custom_call_target="tpu_custom_call" | custom-call | tf_op jit(solution)/shard_map/pallas_call | solution.py:219
  19.8 0.0 copy-start
  19.8 0.7 fusion
  22.5 6.7 %shard_map.75 = f32[2,16,96,512]{3,2,1,0:T(8,128)} custom-call(s32[1]{0:T(128)} %bitcast.8.col_ref, f32[1]{0:T(128)} %bitcast.5.w_ref, bf16[1024,5120]{1,0:T(8,128)(2,1)} %grad_ref.11, bf16[1536,1024]{1,0:T(8,128)(2,1)S(1)} %get-tuple-element.8.hid_ref), custom_call_target="tpu_custom_call" | custom-call | flops 3221225472 | bytes 12058624 | tf_op jit(solution)/shard_map/pallas_call | solution.py:79
  29.1 0.1 collective-permute-start.1
  29.3 6.6 %shard_map.74 = f32[2,16,96,512]{3,2,1,0:T(8,128)} custom-call(s32[1]{0:T(128)} %bitcast.6.col_ref, f32[1]{0:T(128)} %bitcast.5.w_ref, bf16[1024,5120]{1,0:T(8,128)(2,1)} %grad_ref.11, bf16[1536,1024]{1,0:T(8,128)(2,1)S(1)} %get-tuple-element.8.hid_ref), custom_call_target="tpu_custom_call" | custom-call | flops 3221225472 | bytes 12058624 | tf_op jit(solution)/shard_map/pallas_call | solution.py:79
  35.9 0.4 collective-permute-start
  36.3 3.4 %collective-permute-done.1.rest_0_ = f32[2,16,96,512]{3,2,1,0:T(8,128)} collective-permute-done((f32[2,16,96,512]{3,2,1,0:T(8,128)}, f32[2,16,96,512]{3,2,1,0:T(8,128)}, u32[]{:S(2)}, u32[]{:S(2)}) %collective-permute-start.1) | collective-permute-done | bytes 6291488 | tf_op jit(solution)/shard_map/ppermute | solution.py:273
  39.6 7.8 %shard_map.76.rest_1_ = f32[16,4,96,512]{3,2,1,0:T(8,128)} custom-call(s32[1]{0:T(128)} %bitcast.7.col_ref, f32[1]{0:T(128)} %bitcast.5.w_ref, bf16[1024,5120]{1,0:T(8,128)(2,1)} %grad_ref.11, bf16[1536,1024]{1,0:T(8,128)(2,1)S(1)} %get-tuple-element.8.hid_ref, f32[2,16,96,512]{3,2,1,0:T(8,128)} %collective-permute-done.1.rest_0_), custom_call_target="tpu_custom_call" | custom-call | flops 3221225472 | bytes 18350080 | tf_op jit(solution)/shard_map/pallas_call | solution.py:79
  47.4 1.2 collective-permute-done.rest_0_
  48.6 0.0 copy-done
  48.6 7.7 %shard_map.77 = f32[16,4,96,512]{3,2,1,0:T(8,128)} custom-call(s32[1]{0:T(128)} %bitcast.col_ref, f32[1]{0:T(128)} %bitcast.5.w_ref, bf16[1024,5120]{1,0:T(8,128)(2,1)} %grad_ref.11, bf16[1536,1024]{1,0:T(8,128)(2,1)S(1)} %get-tuple-element.8.hid_ref, f32[2,16,96,512]{3,2,1,0:T(8,128)} %collective-permute-done.rest_0_, ...), custom_call_target="tpu_custom_call", output_to_operand_aliasing={{}: (5, {})} | custom-call | flops 3221225472 | bytes 18350080 | tf_op jit(solution)/shard_map/pallas_call | solution.py:79
  56.3 0.0 reduce-scatter.4.cloned.1.call-update
  56.3 6.8 %shard_map.79 = f32[4,16,96,128]{3,2,1,0:T(8,128)S(1)} custom-call(s32[1]{0:T(128)} %bitcast.8.col_ref, f32[1]{0:T(128)} %bitcast.5.w_ref, bf16[1024,5120]{1,0:T(8,128)(2,1)} %grad_ref.11, bf16[1536,1024]{1,0:T(8,128)(2,1)} %copy-done), custom_call_target="tpu_custom_call" | custom-call | flops 1610612736 | bytes 11534336 | tf_op jit(solution)/shard_map/pallas_call | solution.py:79
  63.1 0.2 collective-permute-start.2
  63.3 5.5 %collective-permute-done.2.rest_0_ = f32[4,16,96,128]{3,2,1,0:T(8,128)S(1)} collective-permute-done((f32[4,16,96,128]{3,2,1,0:T(8,128)S(1)}, f32[4,16,96,128]{3,2,1,0:T(8,128)S(1)}, u32[]{:S(2)}, u32[]{:S(2)}) %collective-permute-start.2) | collective-permute-done | bytes 3145760 | tf_op jit(solution)/shard_map/ppermute | solution.py:273
  68.9 0.0 copy-start.6
  68.9 1.6 copy-done.6
  70.5 7.4 %shard_map.80.x_ref = f32[4,16,96,128]{3,2,1,0:T(8,128)S(1)} custom-call(s32[1]{0:T(128)} %bitcast.7.col_ref, f32[1]{0:T(128)} %bitcast.5.w_ref, bf16[1024,5120]{1,0:T(8,128)(2,1)} %grad_ref.11, bf16[1536,1024]{1,0:T(8,128)(2,1)} %copy-done, f32[4,16,96,128]{3,2,1,0:T(8,128)} %copy-done.6), custom_call_target="tpu_custom_call" | custom-call | flops 1610612736 | bytes 14680064 | tf_op jit(solution)/shard_map/pallas_call | solution.py:79
  77.9 38.4 %shard_map.81.x_ref = f32[16,96,128]{2,1,0:T(8,128)S(1)} custom-call(f32[4,16,96,128]{3,2,1,0:T(8,128)S(1)} %shard_map.80.x_ref), custom_call_target="tpu_custom_call" | custom-call | flops 786432 | bytes 9437184 | tf_op jit(solution)/shard_map/pallas_call | solution.py:135
  116.3 16.3 %shard_map.82 = f32[96,128]{1,0:T(8,128)S(1)} custom-call(f32[16,96,128]{2,1,0:T(8,128)S(1)} %shard_map.81.x_ref), custom_call_target="tpu_custom_call" | custom-call | flops 196608 | bytes 2359296 | tf_op jit(solution)/shard_map/pallas_call | solution.py:135
  132.6 0.0 copy-start.2
  132.6 0.6 copy-done.2
  133.2 24.0 %reduce-scatter.4.cloned.1.call-done = f32[1,4,96,512]{3,2,1,0:T(8,128)} async-done(((f32[16,4,96,512]{3,2,1,0:T(8,128)}), f32[1,4,96,512]{3,2,1,0:T(8,128)}) %reduce-scatter.4.cloned.1.call-update) | async-done | bytes 786448
  157.2 14.0 %shard_map.78 = f32[96,512]{1,0:T(8,128)} custom-call(f32[4,96,512]{2,1,0:T(8,128)} %bitcast.11), custom_call_target="tpu_custom_call" | custom-call | flops 196608 | bytes 2359296 | tf_op jit(solution)/shard_map/pallas_call | solution.py:135
  171.2 1.7 pad_maximum_fusion
Async XLA Ops:
  6.5 150.7 %reduce-scatter.4.cloned.1.call-start = ((), (), s32[]{:S(2)}) async-start(), calls=%async_computation.1 | async-start | bytes 13369344
  7.2 1.9 %copy-start.1 = (bf16[1024,1536]{1,0:T(8,128)(2,1)S(1)}, bf16[1024,1536]{1,0:T(8,128)(2,1)}, u32[]{:S(2)}) copy-start(bf16[1024,1536]{1,0:T(8,128)(2,1)} %hid_hbm.1) | copy-start | bytes 9437188
  9.1 0.7 copy-start.3
  9.8 0.7 copy-start.4
  10.5 0.7 copy-start.5
  19.8 28.9 %copy-start = (bf16[1536,1024]{1,0:T(8,128)(2,1)}, bf16[1536,1024]{1,0:T(8,128)(2,1)S(1)}, u32[]{:S(2)}) copy-start(bf16[1536,1024]{1,0:T(8,128)(2,1)S(1)} %get-tuple-element.8.hid_ref) | copy-start | bytes 9437188
  29.1 10.5 %collective-permute-start.1 = (f32[2,16,96,512]{3,2,1,0:T(8,128)}, f32[2,16,96,512]{3,2,1,0:T(8,128)}, u32[]{:S(2)}, u32[]{:S(2)}) collective-permute-start(f32[2,16,96,512]{3,2,1,0:T(8,128)} %shard_map.75), channel_id=1, source_target_pairs={{0,1},{1,0},{2,3},{3,2},{4,5},{5,4},{6,7},{7,6},{8,9},{9,8},{10,11... | collective-permute-start | bytes 18874376 | tf_op jit(solution)/shard_map/ppermute | solution.py:273
  35.9 12.8 %collective-permute-start = (f32[2,16,96,512]{3,2,1,0:T(8,128)}, f32[2,16,96,512]{3,2,1,0:T(8,128)}, u32[]{:S(2)}, u32[]{:S(2)}) collective-permute-start(f32[2,16,96,512]{3,2,1,0:T(8,128)} %shard_map.74), channel_id=1, source_target_pairs={{0,1},{1,0},{2,3},{3,2},{4,5},{5,4},{6,7},{7,6},{8,9},{9,8},{10,11... | collective-permute-start | bytes 18874376 | tf_op jit(solution)/shard_map/ppermute | solution.py:273
  63.1 5.7 %collective-permute-start.2 = (f32[4,16,96,128]{3,2,1,0:T(8,128)S(1)}, f32[4,16,96,128]{3,2,1,0:T(8,128)S(1)}, u32[]{:S(2)}, u32[]{:S(2)}) collective-permute-start(f32[4,16,96,128]{3,2,1,0:T(8,128)S(1)} %shard_map.79), channel_id=1, source_target_pairs={{0,1},{1,0},{2,3},{3,2},{4,5},{5,4},{6,7},{7,6},{8,9},{9,8},{10,11... | collective-permute-start | bytes 9437192 | tf_op jit(solution)/shard_map/ppermute | solution.py:273
  68.9 1.6 copy-start.6
  132.6 0.6 copy-start.2
Sparse Core Ops, SparseCore 0:
  56.5 100.6 reduce-scatter.3

commit v20 on v19

--- a/solution.py
+++ b/solution.py
@@ -154,9 +154,14 @@
     n = n_z * n_core
     t, hb = hidden.shape
 
-    def kernel(new_ref, old_ref, mask_ref, len_ref, hid_hbm, out_ref, live_ref, ht_ref,
-               hid_ref, mine, staged, recv, hid_sem, copy_sem, send_sem, recv_sem):
+    def kernel(new_hbm, old_hbm, mask_hbm, len_ref, hid_hbm, out_ref, live_ref, ht_ref,
+               hid_ref, new_ref, old_ref, mask_ref, mine, staged, recv, hid_sem, row_sem,
+               copy_sem, send_sem, recv_sem):
         me = lax.axis_index("z") * n_core + lax.axis_index("core")
+        rows = [pltpu.make_async_copy(a, b, row_sem.at[i]) for i, (a, b) in enumerate(
+            ((new_hbm, new_ref), (old_hbm, old_ref), (mask_hbm, mask_ref)))]
+        for cp in rows:
+            cp.start()
         fetch = pltpu.make_async_copy(hid_hbm, hid_ref, hid_sem)
         fetch.start()
 
@@ -167,6 +172,8 @@
         for d in range(1, n):
             pl.semaphore_signal(barrier, inc=1, device_id=peer_of(lax.rem(me + d, n)),
                                 device_id_type=pl.DeviceIdType.MESH)
+        for cp in rows:
+            cp.wait()
         places = me * t + lax.broadcasted_iota(jnp.int32, (8, t), 1)
         mask8 = jnp.broadcast_to(mask_ref[...], (8, t))
         live = jnp.where(places < len_ref[0], mask8, 0).astype(jnp.float32)
@@ -221,21 +228,25 @@
         out_shape=(jax.ShapeDtypeStruct((8, 128), jnp.float32),
                    jax.ShapeDtypeStruct((t, 1), jnp.float32),
                    jax.ShapeDtypeStruct((hb, t), hidden.dtype)),
-        in_specs=[vmem, vmem, vmem, pl.BlockSpec(memory_space=pltpu.SMEM),
-                  pl.BlockSpec(memory_space=pl.ANY)],
+        in_specs=[pl.BlockSpec(memory_space=pl.ANY)] * 3 + [
+            pl.BlockSpec(memory_space=pltpu.SMEM), pl.BlockSpec(memory_space=pl.ANY)],
         out_specs=(vmem, vmem, vmem),
         scratch_shapes=[
             pltpu.VMEM((t, hb), hidden.dtype),
+            pltpu.VMEM(new_lp.shape, new_lp.dtype),
+            pltpu.VMEM(old_lp.shape, old_lp.dtype),
+            pltpu.VMEM(mask.shape, mask.dtype),
             pltpu.VMEM((8, 128), jnp.float32),
             pltpu.VMEM((8, 128), jnp.float32),
             pltpu.VMEM((n, 8, 128), jnp.float32),
             pltpu.SemaphoreType.DMA,
+            pltpu.SemaphoreType.DMA((3,)),
             pltpu.SemaphoreType.DMA,
             pltpu.SemaphoreType.DMA((n,)),
             pltpu.SemaphoreType.DMA((n,)),
         ],
         compiler_params=pltpu.CompilerParams(
-            collective_id=1, has_side_effects=True, vmem_limit_bytes=32 * 1024 * 1024),
+            collective_id=1, has_side_effects=True, vmem_limit_bytes=64 * 1024 * 1024),
     )(new_lp, old_lp, mask, roll_len, hidden)
 
 

time: 180 us -> 181 us (level)
  Pallas kernels: 120 us -> 123 us
    pallas_call x1, Pallas kernels: 8.64 us -> 11 us  [ctx_sum(): pl.pallas_call(kernel, out_shape=(jax.ShapeDtypeStruct((8, 128), jnp.floa...]
    unnamed x14 -> x8, local copies, waits for them, and re-layouts: 6.2 us -> 4.12 us
where the time goes in v20:
time: 181 us
  Pallas kernels  123 us (68%)
  waiting for transfers between devices  34.2 us (19%)
  between operations  16.1 us (9%)
  local copies, waits for them, and re-layouts  5.45 us (3%)
    pallas_call x3, Pallas kernels, z_reduce_scatter(): pl.pallas_call(kernel, out_shape=jax.ShapeDtypeStruct(rest_shape, jnp.flo...  68.6 us
    pallas_call x6, Pallas kernels, block_matmul(): pl.pallas_call(kernel, grid_spec=grid_spec, out_shape=out_shape, input_ou...  43 us
    unnamed x2, waiting for transfers between devices  24 us
    pallas_call x1, Pallas kernels, ctx_sum(): pl.pallas_call(kernel, out_shape=(jax.ShapeDtypeStruct((8, 128), jnp.floa...  11 us
    ppermute x3, waiting for transfers between devices, pre_reduced(): got.append(lax.ppermute(theirs, 'core', perm=swap))  10.2 us
    unnamed x8, local copies, waits for them, and re-layouts  4.12 us
  transfers between devices with their start and end apart: 4, of which 4 were waited for; matrix products, arithmetic and copies ran while one was open for 0% of the time, Pallas kernels for 46%

profile of v20, /device:TPU:0, one launch (start us, length us, event | category | flops | bytes accessed | tf_op | source)
XLA Modules:
  0.0 180.7 jit_solution(9019156640179990741)
XLA Ops:
  6.5 0.0 reduce-scatter.4.cloned.1.call-start
  7.2 11.0 %shard_map.73 = (f32[8,128]{1,0:T(8,128)}, f32[1024,1]{1,0:T(8,128)}, bf16[1536,1024]{1,0:T(8,128)(2,1)}) custom-call(f32[1,1024]{1,0:T(1,128)} %new_hbm.1, f32[1,1024]{1,0:T(1,128)} %old_hbm.1, s32[1,1024]{1,0:T(1,128)} %mask_hbm.1, s32[1]{0:T(128)S(6)} %copy.10.len_ref, bf16[1024,1536]{1,0:T(8,128)(2,1)} %hid_hbm.1), custom_call_target="tpu_custom_call" | custom-call | tf_op jit(solution)/shard_map/pallas_call | solution.py:226
  18.2 1.3 fusion
  21.5 0.0 copy-start
  21.5 1.9 %copy-done = bf16[1536,1024]{1,0:T(8,128)(2,1)S(1)} copy-done((bf16[1536,1024]{1,0:T(8,128)(2,1)S(1)}, bf16[1536,1024]{1,0:T(8,128)(2,1)}, u32[]{:S(2)}) %copy-start) | copy-done | bytes 3145752
  23.4 0.0 copy-start.1
  23.4 6.8 %shard_map.75 = f32[2,16,96,512]{3,2,1,0:T(8,128)} custom-call(s32[1]{0:T(128)} %bitcast.8.col_ref, f32[1]{0:T(128)} %bitcast.5.w_ref, bf16[1024,5120]{1,0:T(8,128)(2,1)} %grad_ref.11, bf16[1536,1024]{1,0:T(8,128)(2,1)S(1)} %copy-done), custom_call_target="tpu_custom_call" | custom-call | flops 3221225472 | bytes 12058624 | tf_op jit(solution)/shard_map/pallas_call | solution.py:79
  30.2 0.1 collective-permute-start.1
  30.3 0.0 copy-done.1
  30.3 6.6 %shard_map.74 = f32[2,16,96,512]{3,2,1,0:T(8,128)} custom-call(s32[1]{0:T(128)} %bitcast.6.col_ref, f32[1]{0:T(128)} %bitcast.5.w_ref, bf16[1024,5120]{1,0:T(8,128)(2,1)} %grad_ref.11, bf16[1536,1024]{1,0:T(8,128)(2,1)S(1)} %copy-done.1), custom_call_target="tpu_custom_call" | custom-call | flops 3221225472 | bytes 12058624 | tf_op jit(solution)/shard_map/pallas_call | solution.py:79
  37.0 0.4 collective-permute-start
  37.4 3.4 %collective-permute-done.1.rest_0_ = f32[2,16,96,512]{3,2,1,0:T(8,128)} collective-permute-done((f32[2,16,96,512]{3,2,1,0:T(8,128)}, f32[2,16,96,512]{3,2,1,0:T(8,128)}, u32[]{:S(2)}, u32[]{:S(2)}) %collective-permute-start.1) | collective-permute-done | bytes 6291488 | tf_op jit(solution)/shard_map/ppermute | solution.py:284
  40.7 7.7 %shard_map.76.rest_1_ = f32[16,4,96,512]{3,2,1,0:T(8,128)} custom-call(s32[1]{0:T(128)} %bitcast.7.col_ref, f32[1]{0:T(128)} %bitcast.5.w_ref, bf16[1024,5120]{1,0:T(8,128)(2,1)} %grad_ref.11, bf16[1536,1024]{1,0:T(8,128)(2,1)S(1)} %copy-done.1, f32[2,16,96,512]{3,2,1,0:T(8,128)} %collective-permute-done.1.rest_0_), custom_call_target="tpu_custom_call" | custom-call | flops 3221225472 | bytes 18350080 | tf_op jit(solution)/shard_map/pallas_call | solution.py:79
  48.4 1.3 collective-permute-done.rest_0_
  49.7 7.6 %shard_map.77 = f32[16,4,96,512]{3,2,1,0:T(8,128)} custom-call(s32[1]{0:T(128)} %bitcast.col_ref, f32[1]{0:T(128)} %bitcast.5.w_ref, bf16[1024,5120]{1,0:T(8,128)(2,1)} %grad_ref.11, bf16[1536,1024]{1,0:T(8,128)(2,1)S(1)} %copy-done.1, f32[2,16,96,512]{3,2,1,0:T(8,128)} %collective-permute-done.rest_0_, ...), custom_call_target="tpu_custom_call", output_to_operand_aliasing={{}: (5, {})} | custom-call | flops 3221225472 | bytes 18350080 | tf_op jit(solution)/shard_map/pallas_call | solution.py:79
  57.3 0.0 reduce-scatter.4.cloned.1.call-update
  57.4 6.8 %shard_map.79 = f32[4,16,96,128]{3,2,1,0:T(8,128)S(1)} custom-call(s32[1]{0:T(128)} %bitcast.8.col_ref, f32[1]{0:T(128)} %bitcast.5.w_ref, bf16[1024,5120]{1,0:T(8,128)(2,1)} %grad_ref.11, bf16[1536,1024]{1,0:T(8,128)(2,1)} %get-tuple-element.8.hid_ref), custom_call_target="tpu_custom_call" | custom-call | flops 1610612736 | bytes 11534336 | tf_op jit(solution)/shard_map/pallas_call | solution.py:79
  64.1 0.2 collective-permute-start.2
  64.4 5.5 %collective-permute-done.2.rest_0_ = f32[4,16,96,128]{3,2,1,0:T(8,128)S(1)} collective-permute-done((f32[4,16,96,128]{3,2,1,0:T(8,128)S(1)}, f32[4,16,96,128]{3,2,1,0:T(8,128)S(1)}, u32[]{:S(2)}, u32[]{:S(2)}) %collective-permute-start.2) | collective-permute-done | bytes 3145760 | tf_op jit(solution)/shard_map/ppermute | solution.py:284
  69.9 0.0 copy-start.3
  69.9 1.6 copy-done.3
  71.5 7.4 %shard_map.80.x_ref = f32[4,16,96,128]{3,2,1,0:T(8,128)S(1)} custom-call(s32[1]{0:T(128)} %bitcast.7.col_ref, f32[1]{0:T(128)} %bitcast.5.w_ref, bf16[1024,5120]{1,0:T(8,128)(2,1)} %grad_ref.11, bf16[1536,1024]{1,0:T(8,128)(2,1)} %get-tuple-element.8.hid_ref, f32[4,16,96,128]{3,2,1,0:T(8,128)} %copy-done.3), custom_call_target="tpu_custom_call" | custom-call | flops 1610612736 | bytes 14680064 | tf_op jit(solution)/shard_map/pallas_call | solution.py:79
  79.0 38.3 %shard_map.81.x_ref = f32[16,96,128]{2,1,0:T(8,128)S(1)} custom-call(f32[4,16,96,128]{3,2,1,0:T(8,128)S(1)} %shard_map.80.x_ref), custom_call_target="tpu_custom_call" | custom-call | flops 786432 | bytes 9437184 | tf_op jit(solution)/shard_map/pallas_call | solution.py:135
  117.3 16.2 %shard_map.82 = f32[96,128]{1,0:T(8,128)S(1)} custom-call(f32[16,96,128]{2,1,0:T(8,128)S(1)} %shard_map.81.x_ref), custom_call_target="tpu_custom_call" | custom-call | flops 196608 | bytes 2359296 | tf_op jit(solution)/shard_map/pallas_call | solution.py:135
  133.5 0.0 copy-start.2
  133.5 0.6 copy-done.2
  134.1 24.0 %reduce-scatter.4.cloned.1.call-done = f32[1,4,96,512]{3,2,1,0:T(8,128)} async-done(((f32[16,4,96,512]{3,2,1,0:T(8,128)}), f32[1,4,96,512]{3,2,1,0:T(8,128)}) %reduce-scatter.4.cloned.1.call-update) | async-done | bytes 786448
  158.1 14.1 %shard_map.78 = f32[96,512]{1,0:T(8,128)} custom-call(f32[4,96,512]{2,1,0:T(8,128)} %bitcast.11), custom_call_target="tpu_custom_call" | custom-call | flops 196608 | bytes 2359296 | tf_op jit(solution)/shard_map/pallas_call | solution.py:135
  172.2 1.7 pad_maximum_fusion
Async XLA Ops:
  6.5 151.6 %reduce-scatter.4.cloned.1.call-start = ((), (), s32[]{:S(2)}) async-start(), calls=%async_computation.1 | async-start | bytes 13369344
  21.5 1.9 %copy-start = (bf16[1536,1024]{1,0:T(8,128)(2,1)S(1)}, bf16[1536,1024]{1,0:T(8,128)(2,1)}, u32[]{:S(2)}) copy-start(bf16[1536,1024]{1,0:T(8,128)(2,1)} %get-tuple-element.8.hid_ref) | copy-start | bytes 9437188
  23.4 6.9 %copy-start.1 = (bf16[1536,1024]{1,0:T(8,128)(2,1)S(1)}, bf16[1536,1024]{1,0:T(8,128)(2,1)}, u32[]{:S(2)}) copy-start(bf16[1536,1024]{1,0:T(8,128)(2,1)} %get-tuple-element.8.hid_ref) | copy-start | bytes 9437188
  30.2 10.5 %collective-permute-start.1 = (f32[2,16,96,512]{3,2,1,0:T(8,128)}, f32[2,16,96,512]{3,2,1,0:T(8,128)}, u32[]{:S(2)}, u32[]{:S(2)}) collective-permute-start(f32[2,16,96,512]{3,2,1,0:T(8,128)} %shard_map.75), channel_id=1, source_target_pairs={{0,1},{1,0},{2,3},{3,2},{4,5},{5,4},{6,7},{7,6},{8,9},{9,8},{10,11... | collective-permute-start | bytes 18874376 | tf_op jit(solution)/shard_map/ppermute | solution.py:284
  37.0 12.7 %collective-permute-start = (f32[2,16,96,512]{3,2,1,0:T(8,128)}, f32[2,16,96,512]{3,2,1,0:T(8,128)}, u32[]{:S(2)}, u32[]{:S(2)}) collective-permute-start(f32[2,16,96,512]{3,2,1,0:T(8,128)} %shard_map.74), channel_id=1, source_target_pairs={{0,1},{1,0},{2,3},{3,2},{4,5},{5,4},{6,7},{7,6},{8,9},{9,8},{10,11... | collective-permute-start | bytes 18874376 | tf_op jit(solution)/shard_map/ppermute | solution.py:284
  64.1 5.7 %collective-permute-start.2 = (f32[4,16,96,128]{3,2,1,0:T(8,128)S(1)}, f32[4,16,96,128]{3,2,1,0:T(8,128)S(1)}, u32[]{:S(2)}, u32[]{:S(2)}) collective-permute-start(f32[4,16,96,128]{3,2,1,0:T(8,128)S(1)} %shard_map.79), channel_id=1, source_target_pairs={{0,1},{1,0},{2,3},{3,2},{4,5},{5,4},{6,7},{7,6},{8,9},{9,8},{10,11... | collective-permute-start | bytes 9437192 | tf_op jit(solution)/shard_map/ppermute | solution.py:284
  69.9 1.6 copy-start.3
  133.5 0.6 copy-start.2
Sparse Core Ops, SparseCore 0:
  57.5 100.5 reduce-scatter.3
